TPU v7x, 128 devices: a whole 4x4x4 slice. The times are simulated.
128 devices in a mesh: seq: 32 (over y_hi, x, z), batch: 4 (over y_lo, core).
Axes of the slice: x: 4, y: 4 (y_hi: 2, y_lo: 2; y = y_hi * 2 + y_lo), z: 4, core: 2. Of those that a mesh axis runs over, the one named last changes fastest.
Arguments:
- tokens: bfloat16 [4, 8192, 256], P('batch', 'seq'), may hold values from -6 to 6
- out_grad: bfloat16 [4, 8192, 256], P('batch', 'seq'), may hold values from -6 to 6
- in_weight: bfloat16 [256, 768], replicated, may hold values from -0.375 to 0.375
- out_weight: bfloat16 [256, 256], replicated, may hold values from -0.375 to 0.375
- skip_bias: float32 [256], replicated, may hold values from -4 to 4
- embed_weight: float32 [5, 64], replicated, may hold values from -4 to 4
- embed_bias: float32 [64], replicated, may hold values from -4 to 4
- hidden_weight: float32 [64, 64], replicated, may hold values from -0.75 to 0.75
- hidden_bias: float32 [64], replicated, may hold values from -4 to 4
- filter_weight: float32 [64, 256], replicated, may hold values from -0.75 to 0.75
- sine_freq: float32 [2, 64], replicated, may hold values from 0.5 to 3
- decay_rate: float32 [256], replicated, may hold values from 0.00037475585 to 0.0018737793
Outputs:
- grad_tokens: bfloat16 [4, 8192, 256], P('batch', 'seq')
- grad_in_weight: float32 [256, 768], replicated
- grad_out_weight: float32 [256, 256], replicated
- grad_skip_bias: float32 [256], replicated
- grad_embed_weight: float32 [5, 64], replicated
- grad_embed_bias: float32 [64], replicated
- grad_hidden_weight: float32 [64, 64], replicated
- grad_hidden_bias: float32 [64], replicated
- grad_filter_weight: float32 [64, 256], replicated
- grad_sine_freq: float32 [2, 64], replicated
All inputs are finite; a program needn't handle non-finite values.
Results may differ from a plain program's by a relative error of at most 0.013.
Values may be sent and summed in bfloat16 or wider, within the bound.
No kernel may reach another device: no remote copies, remote signals or barrier semaphores. Data moves between devices by JAX's collectives and lax.ppermute only.
A program may use at most 64 MiB of HBM per device.

v0:
```python
import math

import jax
import jax.numpy as jnp
from jax import lax
from jax.sharding import PartitionSpec as P

highest = lax.Precision.HIGHEST


def side_by_side(arrays, axis, split_dim, concat_dim, along):
    both = jnp.concatenate(arrays, axis=along)
    whole, at, done = (
        lax.all_to_all(both, axis, split_axis=split_dim, concat_axis=concat_dim, tiled=True),
        0,
        [],
    )
    for a in arrays:
        done.append(lax.slice_in_dim(whole, at, at + a.shape[along], axis=along))
        at += a.shape[along]
    return tuple(done)


def in_one(arrays, axis):
    flat, at, done = (jnp.concatenate([a.reshape(-1) for a in arrays]), 0, [])
    so_far = lax.psum(flat, axis)
    for a in arrays:
        done.append(so_far[at : at + a.size].reshape(a.shape))
        at += a.size
    return tuple(done)


def angle_table(row_count, col_count, period):
    index_product = (
        jnp.arange(row_count, dtype=jnp.int32)[:, None]
        * jnp.arange(col_count, dtype=jnp.int32)[None, :]
        % period
    )
    angles = index_product.astype(jnp.float32) * (2.0 * math.pi / period)
    return (jnp.cos(angles), jnp.sin(angles))


def make_tables(length):
    total = 2 * length
    first_len = 2
    while first_len * first_len < total and total % (2 * first_len) == 0:
        first_len = first_len * 2
    second_len = total // first_len
    outer_cos, outer_sin = angle_table(first_len, first_len, first_len)
    inner_cos, inner_sin = angle_table(second_len, second_len, second_len)
    twist_cos, twist_sin = angle_table(first_len, second_len, total)
    return (outer_cos, outer_sin, inner_cos, inner_sin, twist_cos, twist_sin)


def right_multiply(stack_part, table):
    return jnp.einsum("...km,mj->...kj", stack_part, table, precision=highest)


def spectrum(signal, tables):
    outer_cos, outer_sin, inner_cos, inner_sin, twist_cos, twist_sin = tables
    half_len = outer_cos.shape[0] // 2
    second_len = inner_cos.shape[0]
    blocks = signal.reshape(signal.shape[:-1] + (half_len, second_len))
    real_section = jnp.einsum("kn,...nm->...km", outer_cos[:, :half_len], blocks, precision=highest)
    imag_section = -jnp.einsum(
        "kn,...nm->...km", outer_sin[:, :half_len], blocks, precision=highest
    )
    real_twist = real_section * twist_cos + imag_section * twist_sin
    imag_twist = imag_section * twist_cos - real_section * twist_sin
    real_out = right_multiply(real_twist, inner_cos) + right_multiply(imag_twist, inner_sin)
    imag_out = right_multiply(imag_twist, inner_cos) - right_multiply(real_twist, inner_sin)
    return (real_out, imag_out)


def inverse(spectra, tables):
    real_in, imag_in = spectra
    outer_cos, outer_sin, inner_cos, inner_sin, twist_cos, twist_sin = tables
    first_len = outer_cos.shape[0]
    half_len = first_len // 2
    second_len = inner_cos.shape[0]
    real_section = right_multiply(real_in, inner_cos) - right_multiply(imag_in, inner_sin)
    imag_section = right_multiply(imag_in, inner_cos) + right_multiply(real_in, inner_sin)
    real_twist = real_section * twist_cos - imag_section * twist_sin
    imag_twist = real_section * twist_sin + imag_section * twist_cos
    signal = jnp.einsum("nk,...km->...nm", outer_cos[:half_len], real_twist, precision=highest)
    signal = signal - jnp.einsum(
        "nk,...km->...nm", outer_sin[:half_len], imag_twist, precision=highest
    )
    signal = signal / float(first_len * second_len)
    return signal.reshape(signal.shape[:-2] + (half_len * second_len,))


def multiply(left_pair, right_pair, conjugate):
    left_real, left_imag = left_pair
    right_real, right_imag = right_pair
    if conjugate:
        return (
            left_real * right_real + left_imag * right_imag,
            left_imag * right_real - left_real * right_imag,
        )
    return (
        left_real * right_real - left_imag * right_imag,
        left_real * right_imag + left_imag * right_real,
    )


def embedding(positions, length, band_count):
    scaled = positions / length
    rows_list = [scaled]
    for band_index in range(1, band_count + 1):
        angle = 2.0 * math.pi * band_index * scaled
        rows_list.append(jnp.cos(angle))
        rows_list.append(jnp.sin(angle))
    return jnp.stack(rows_list, axis=0)


def modulation(decay_part, positions, length):
    return 4.0 * jnp.exp(-decay_part[:, None] * positions[None, :]) / math.sqrt(length)


def contract_first(left_side, right_side):
    return lax.dot_general(left_side, right_side, (((0,), (0,)), ((), ())), precision=highest)


def contract_last(left_side, right_side):
    return lax.dot_general(left_side, right_side, (((1,), (1,)), ((), ())), precision=highest)


def mlp_forward(embed_rows, embed_weight, embed_bias, hidden_weight, hidden_bias, sine_freq):
    pre_one = contract_first(embed_weight, embed_rows) + embed_bias[:, None]
    act_one = jnp.sin(sine_freq[0][:, None] * pre_one)
    pre_two = contract_first(hidden_weight, act_one) + hidden_bias[:, None]
    act_two = jnp.sin(sine_freq[1][:, None] * pre_two)
    return (pre_one, act_one, pre_two, act_two)


def filter_values(activations, weight_part, modul):
    return contract_first(weight_part, activations[3]) * modul


def mlp_backward(
    embed_rows, activations, hidden_weight, sine_freq, weight_part, modul, grad_filter
):
    pre_one, act_one, pre_two, act_two = activations
    grad_kernel = grad_filter * modul
    grad_weight_part = contract_last(act_two, grad_kernel)
    grad_act_two = jnp.dot(weight_part, grad_kernel, precision=highest)
    cos_two = jnp.cos(sine_freq[1][:, None] * pre_two)
    grad_pre_two = grad_act_two * sine_freq[1][:, None] * cos_two
    grad_freq_two = jnp.sum(grad_act_two * pre_two * cos_two, axis=1)
    grad_hidden_bias = jnp.sum(grad_pre_two, axis=1)
    grad_hidden_weight = contract_last(act_one, grad_pre_two)
    grad_act_one = jnp.dot(hidden_weight, grad_pre_two, precision=highest)
    cos_one = jnp.cos(sine_freq[0][:, None] * pre_one)
    grad_pre_one = grad_act_one * sine_freq[0][:, None] * cos_one
    grad_freq_one = jnp.sum(grad_act_one * pre_one * cos_one, axis=1)
    grad_embed_bias = jnp.sum(grad_pre_one, axis=1)
    grad_embed_weight = contract_last(embed_rows, grad_pre_one)
    return (
        grad_embed_weight,
        grad_embed_bias,
        grad_hidden_weight,
        grad_hidden_bias,
        grad_weight_part,
        jnp.stack([grad_freq_one, grad_freq_two], axis=0),
    )


def spread_out(parts, seq_count, batch_count):
    chan_dev = parts.shape[1]
    pos_dev = parts.shape[2]
    shaped = parts.reshape(seq_count, batch_count, chan_dev, pos_dev)
    return jnp.transpose(shaped, (1, 2, 0, 3)).reshape(batch_count, chan_dev, seq_count * pos_dev)


def gather_back(signals, seq_count, batch_count):
    chan_dev = signals.shape[1]
    pos_dev = signals.shape[2] // seq_count
    shaped = signals.reshape(batch_count, chan_dev, seq_count, pos_dev)
    return jnp.transpose(shaped, (2, 0, 1, 3)).reshape(seq_count * batch_count, chan_dev, pos_dev)


def shards(
    tokens,
    out_grad,
    in_weight,
    out_weight,
    skip_bias,
    embed_weight,
    embed_bias,
    hidden_weight,
    hidden_bias,
    filter_weight,
    sine_freq,
    decay_rate,
):
    tokens_local = tokens[0]
    grad_local = out_grad[0]
    pos_dev = tokens_local.shape[0]
    model_width = tokens_local.shape[1]
    seq_count = lax.axis_size("seq")
    batch_count = lax.axis_size("batch")
    length = pos_dev * seq_count
    seq_index = lax.axis_index("seq")
    batch_index = lax.axis_index("batch")
    projected = jnp.dot(tokens_local, in_weight, preferred_element_type=jnp.float32)
    gate_out = projected[:, :model_width].astype(jnp.bfloat16)
    gate_in = projected[:, model_width : 2 * model_width].astype(jnp.bfloat16)
    values_in = projected[:, 2 * model_width :].astype(jnp.bfloat16)
    mixed = (values_in.astype(jnp.float32) * gate_in.astype(jnp.float32)).astype(jnp.bfloat16)
    grad_gated = lax.dot_general(
        grad_local, out_weight, (((1,), (1,)), ((), ())), preferred_element_type=jnp.float32
    ).astype(jnp.bfloat16)
    grad_conv = (grad_gated.astype(jnp.float32) * gate_out.astype(jnp.float32)).astype(jnp.bfloat16)
    bias_part = jnp.sum(grad_conv.astype(jnp.float32) * mixed.astype(jnp.float32), axis=0)
    mixed_parts, grad_parts = side_by_side(
        (mixed.T[None], grad_conv.T[None]), ("seq", "batch"), 1, 0, 2
    )
    mixed_chan = spread_out(mixed_parts, seq_count, batch_count)
    grad_chan = spread_out(grad_parts, seq_count, batch_count)
    chan_dev = model_width // (seq_count * batch_count)
    chan_start = (seq_index * batch_count + batch_index) * chan_dev
    all_positions = jnp.arange(length, dtype=jnp.float32)
    band_count = (embed_weight.shape[0] - 1) // 2
    embed_all = embedding(all_positions, length, band_count)
    weight_part = lax.dynamic_slice_in_dim(filter_weight, chan_start, chan_dev, 1)
    decay_part = lax.dynamic_slice_in_dim(decay_rate, chan_start, chan_dev, 0)
    bias_chan = lax.dynamic_slice_in_dim(skip_bias, chan_start, chan_dev, 0)[:, None]
    modul_all = modulation(decay_part, all_positions, length)
    activations = mlp_forward(
        embed_all, embed_weight, embed_bias, hidden_weight, hidden_bias, sine_freq
    )
    filter_chan = filter_values(activations, weight_part, modul_all)
    tables = make_tables(length)
    mixed_float = mixed_chan.astype(jnp.float32)
    grad_float = grad_chan.astype(jnp.float32)
    mixed_spec = spectrum(mixed_float, tables)
    grad_spec = spectrum(grad_float, tables)
    filter_spec = spectrum(filter_chan, tables)
    conv_chan = (
        inverse(multiply(mixed_spec, filter_spec, False), tables) + bias_chan * mixed_float
    ).astype(jnp.bfloat16)
    grad_mixed_chan = (
        inverse(multiply(grad_spec, filter_spec, True), tables) + bias_chan * grad_float
    ).astype(jnp.bfloat16)
    grad_filter_seq = inverse(multiply(grad_spec, mixed_spec, True), tables)
    grad_filter_local = jnp.sum(grad_filter_seq, axis=0)
    conv_parts, grad_mixed_parts = side_by_side(
        (
            gather_back(conv_chan, seq_count, batch_count),
            gather_back(grad_mixed_chan, seq_count, batch_count),
        ),
        ("seq", "batch"),
        0,
        1,
        2,
    )
    conv_rows = conv_parts[0]
    grad_mixed_rows = grad_mixed_parts[0]
    conv_float = conv_rows.T.astype(jnp.float32)
    grad_mixed_float = grad_mixed_rows.T.astype(jnp.float32)
    gated = (gate_out.astype(jnp.float32) * conv_float).astype(jnp.bfloat16)
    grad_out_weight = lax.dot_general(
        gated, grad_local, (((0,), (0,)), ((), ())), preferred_element_type=jnp.float32
    )
    grad_gate_out = (grad_gated.astype(jnp.float32) * conv_float).astype(jnp.bfloat16)
    grad_gate_in = (grad_mixed_float * values_in.astype(jnp.float32)).astype(jnp.bfloat16)
    grad_values = (grad_mixed_float * gate_in.astype(jnp.float32)).astype(jnp.bfloat16)
    grad_proj = jnp.concatenate([grad_gate_out, grad_gate_in, grad_values], axis=1)
    grad_tokens = lax.dot_general(
        grad_proj, in_weight, (((1,), (1,)), ((), ())), preferred_element_type=jnp.float32
    ).astype(jnp.bfloat16)
    grad_in_weight = lax.dot_general(
        tokens_local, grad_proj, (((0,), (0,)), ((), ())), preferred_element_type=jnp.float32
    )
    filter_grads = mlp_backward(
        embed_all, activations, hidden_weight, sine_freq, weight_part, modul_all, grad_filter_local
    )
    zero_grad = jnp.zeros((hidden_weight.shape[0], model_width), jnp.float32)
    grad_filter_weight = lax.dynamic_update_slice_in_dim(zero_grad, filter_grads[4], chan_start, 1)
    totals = in_one(
        (
            grad_in_weight,
            grad_out_weight,
            bias_part,
            filter_grads[0],
            filter_grads[1],
            filter_grads[2],
            filter_grads[3],
            grad_filter_weight,
            filter_grads[5],
        ),
        ("seq", "batch"),
    )
    grad_scale = 1.0 / math.sqrt(batch_count * length)
    filter_scale = grad_scale / 4.0
    return (
        grad_tokens[None],
        totals[0] * grad_scale,
        totals[1] * grad_scale,
        totals[2] * grad_scale,
        totals[3] * filter_scale,
        totals[4] * filter_scale,
        totals[5] * filter_scale,
        totals[6] * filter_scale,
        totals[7] * filter_scale,
        totals[8] * filter_scale,
    )


def solution(mesh):
    placed = (
        P("batch", "seq", None),
        P("batch", "seq", None),
        P(),
        P(),
        P(),
        P(),
        P(),
        P(),
        P(),
        P(),
        P(),
        P(),
    )
    return jax.shard_map(
        shards,
        mesh=mesh,
        in_specs=placed,
        out_specs=(P("batch", "seq", None), P(), P(), P(), P(), P(), P(), P(), P(), P()),
        check_vma=False,
    )
```

profile of v0, /device:TPU:1, one launch (start us, length us, event | category | flops | bytes accessed | tf_op | source)
XLA Modules:
  0.0 340.7 jit_solution(12501284637838919645)
XLA Ops:
  7.2 1.0 copy-done
  8.2 1.2 convolution_convert_fusion
  9.4 1.3 fusion.10
  12.4 2.2 reduce.6
  14.6 0.8 reshape.295
  15.4 12.0 %all-to-all-start = ((bf16[128,2,512]{2,1,0:T(2,128)(2,1)}), bf16[128,2,512]{2,1,0:T(2,128)(2,1)}, u32[]{:S(2)}, u32[]{:S(2)}) async-start(bf16[128,2,512]{2,1,0:T(2,128)(2,1)} %reshape.295), calls=%async_computation | async-start | bytes 524288 | tf_op jit(solution)/shard_map/all_to_all | solution.py:14
  28.3 1.0 fusion.129
  29.3 1.0 fusion.127
  31.3 1.8 convolution_add_fusion.1
  33.2 4.9 %all-to-all-done = bf16[128,2,512]{2,1,0:T(2,128)(2,1)} async-done(((bf16[128,2,512]{2,1,0:T(2,128)(2,1)}), bf16[128,2,512]{2,1,0:T(2,128)(2,1)}, u32[]{:S(2)}, u32[]{:S(2)}) %all-to-all-start) | async-done | bytes 262176 | tf_op jit(solution)/shard_map/all_to_all | solution.py:14
  38.0 2.4 reshape.296
  40.4 2.2 bitcast_reduce_fusion
  42.6 1.1 all_to_all.9
  45.5 2.0 fusion.69
  47.5 2.0 fusion.68
  50.2 1.0 reshape.249
  52.1 1.2 fusion.70
  53.3 1.2 fusion.71
  54.5 1.2 convolution_subtract_fusion.4
  55.7 1.2 convolution_add_fusion.6
  56.9 1.6 convolution_add_fusion.4
  58.5 1.2 multiply_add_fusion
  59.8 0.9 fusion.94
  60.6 0.9 fusion.96
  61.5 0.9 convolution_add_fusion.2
  62.4 0.9 convolution_subtract_fusion
  63.3 0.8 fusion.22
  64.1 0.8 fusion.11
  64.9 1.8 fusion.159
  66.8 17.0 %fusion.270 = (f32[64]{0:T(128)}, f32[64,8192]{1,0:T(8,128)S(1)}, f32[64]{0:T(128)}, f32[64,8192]{1,0:T(8,128)S(1)}) fusion(f32[64,8192]{1,0:T(8,128)S(1)} %fusion.159, f32[64]{0:T(128)S(1)} %get-tuple-element.28, f32[64]{0:T(128)S(1)} %copy-done.32, f32[64,64]{1,0:T(8,128)S(1)} %copy-done.22, f32[8192,64]{0,1:T(8,128)S(1)} %convolution_add_fusion.1, ...), kind=kOutput, calls=%fused_computation.335 | convolution fusion | flops 407371648 | bytes 8406272 | tf_op jit(solution)/shard_map/dot_general | solution.py:122
  83.8 7.9 %fusion.14 = f32[1,2,64,128]{3,1,2,0:T(2,128)S(1)} fusion(f32[64,8192]{1,0:T(8,128)S(1)} %get-tuple-element.33, f32[64]{0:T(128)S(1)} %get-tuple-element.28, f32[2]{0:T(128)S(1)} %dynamic-slice_negate_fusion, f32[64,256]{1,0:T(8,128)S(1)} %copy-done.25, s32[]{:T(128)S(6)} %select_n.151), kind=kOutput, calls=%fused_computation.51 | convolution fusion | flops 13156352 | bytes 2196484 | tf_op jit(solution)/shard_map/dot_general | solution.py:122
  94.7 0.9 fusion.104
  95.7 1.1 fusion.106
  96.8 1.7 fusion.98
  98.5 1.8 fusion.100
  100.3 10.5 %multiply_reduce_fusion.1 = (f32[64]{0:T(128)}, f32[64]{0:T(128)}, f32[8192,64]{0,1:T(8,128)}) fusion(f32[8192,64]{0,1:T(8,128)S(1)} %convolution_add_fusion.1, f32[64]{0:T(128)S(1)} %get-tuple-element.29, f32[64,8192]{1,0:T(8,128)S(1)} %get-tuple-element.13, f32[64,64]{1,0:T(8,128)S(1)} %copy-done.22), kind=kOutput, calls=%fused_computation.5 | convolution fusion | flops 406323072 | bytes 6308608 | tf_op jit(solution)/shard_map/dot_general | solution.py:153
  110.8 9.3 %fusion.1 = f32[64,64]{1,0:T(8,128)} fusion(f32[64,8192]{1,0:T(8,128)S(1)} %get-tuple-element.13, f32[8192,64]{0,1:T(8,128)S(1)} %convolution_add_fusion.1, f32[64]{0:T(128)S(1)} %get-tuple-element.29), kind=kOutput, calls=%fused_computation.12 | convolution fusion | flops 403177472 | bytes 4210944 | tf_op jit(solution)/shard_map/dot_general | solution.py:126
  120.1 0.9 convolution_add_fusion.5
  121.1 0.9 convolution_subtract_fusion.3
  122.0 0.8 fusion.36
  122.8 1.5 fusion.9
  124.2 1.7 reshape.246
  126.0 2.4 convolution_add_fusion.3
  128.4 0.9 convolution_subtract_fusion.1
  129.4 0.8 fusion.29
  130.2 0.8 fusion.7
  130.9 0.8 reshape.250
  131.7 1.2 fusion.59
  133.2 0.9 pad_maximum_fusion.2
  134.1 4.9 %all-to-all-start.1 = ((bf16[128,2,512]{2,1,0:T(2,128)(2,1)}), bf16[128,2,512]{2,1,0:T(2,128)(2,1)S(1)}, u32[]{:S(2)}, u32[]{:S(2)}) async-start(bf16[128,2,512]{2,1,0:T(2,128)(2,1)} %pad_maximum_fusion.2), calls=%async_computation.1 | async-start | bytes 524288 | tf_op jit(solution)/shard_map/all_to_all | solution.py:14
  139.1 10.1 %fusion.120 = f32[5,64]{1,0:T(8,128)S(1)} fusion(f32[5,8192]{1,0:T(8,128)S(1)} %copy-done.11, f32[8192,64]{0,1:T(8,128)} %get-tuple-element.34, f32[8192,64]{0,1:T(8,128)S(1)} %convolution_add_fusion.1, f32[64]{0:T(128)S(1)} %get-tuple-element.29), kind=kOutput, calls=%fused_computation.196 | convolution fusion | flops 33030144 | bytes 4359680 | tf_op jit(solution)/shard_map/dot_general | solution.py:126
  149.4 10.2 %fusion.2 = f32[64,2]{1,0:T(8,128)S(1)} fusion(f32[64,8192]{1,0:T(8,128)} %copy-done.1, f32[64]{0:T(128)S(1)} %get-tuple-element.28, f32[1,2,64,128]{3,2,1,0:T(8,128)S(1)} %bitcast.252, f32[2]{0:T(128)S(1)} %dynamic-slice_negate_fusion), kind=kOutput, calls=%fused_computation.13 | convolution fusion | flops 13156352 | bytes 2163464 | tf_op jit(solution)/shard_map/dot_general | solution.py:126
  162.1 9.8 %concatenate.15 = f32[283456]{0:T(1024)} concatenate(f32[196608]{0:T(1024)S(1)} %reshape.252, f32[65536]{0:T(1024)S(1)} %bitcast.250, f32[256]{0:T(256)S(1)} %get-tuple-element.19, f32[320]{0:T(512)S(1)} %reshape.254, f32[64]{0:T(128)S(1)} %copy-done.28, f32[4096]{0:T(1024)S(1)} %reshape.255, f32[64]{0:T(128)S(1)} %copy-done.27, f32[16384]{0:T(1024)S(1)} %bitcast.257, ...), dimensions={0} | concatenate | bytes 2267648 | tf_op jit(solution)/shard_map/concatenate | solution.py:25
  171.9 1.0 fusion.12
  172.9 148.3 %all-reduce.2.cloned.1.call-done = f32[283456]{0:T(1024)} async-done(((f32[283456]{0:T(1024)}), f32[283456]{0:T(1024)}) %all-reduce.2.cloned.1.call-update) | async-done | bytes 1133840 | tf_op jit(solution)/shard_map/psum | solution.py:26
  321.2 1.2 slice_multiply_fusion
  322.4 1.0 mul.1107
  323.4 1.0 slice_multiply_fusion.1
  324.4 0.8 mul.1110
  326.5 0.7 slice_multiply_fusion.3
  327.9 1.0 slice_multiply_fusion.2
  329.5 0.7 slice_multiply_fusion.6
  330.9 1.2 slice_multiply_fusion.5
  332.2 1.3 slice_multiply_fusion.7
  (127 shorter events, 16.0 us)
Async XLA Ops:
  7.2 1.0 copy-start
  9.4 1.3 copy-start.6
  10.7 0.7 copy-start.8
  10.7 19.6 %copy-start.31 = (f32[2,64]{1,0:T(2,128)S(1)}, f32[2,64]{1,0:T(2,128)}, u32[]{:S(2)}) copy-start(f32[2,64]{1,0:T(2,128)} %param.22) | copy-start | bytes 1540
  10.7 19.6 %copy-start.35 = (f32[256]{0:T(256)S(1)}, f32[256]{0:T(256)}, u32[]{:S(2)}) copy-start(f32[256]{0:T(256)} %param.23) | copy-start | bytes 3076
  10.7 19.7 %copy-start.36 = (f32[256]{0:T(256)S(1)}, f32[256]{0:T(256)}, u32[]{:S(2)}) copy-start(f32[256]{0:T(256)} %param.16) | copy-start | bytes 3076
  11.4 19.9 %copy-start.26 = (f32[5,64]{1,0:T(8,128)S(1)}, f32[5,64]{1,0:T(8,128)}, u32[]{:S(2)}) copy-start(f32[5,64]{1,0:T(8,128)} %param.17) | copy-start | bytes 3844
  11.4 19.9 %copy-start.34 = (f32[64]{0:T(128)S(1)}, f32[64]{0:T(128)}, u32[]{:S(2)}) copy-start(f32[64]{0:T(128)} %param.18) | copy-start | bytes 772
  15.4 22.6 %all-to-all-start = ((bf16[128,2,512]{2,1,0:T(2,128)(2,1)}), bf16[128,2,512]{2,1,0:T(2,128)(2,1)}, u32[]{:S(2)}, u32[]{:S(2)}) async-start(bf16[128,2,512]{2,1,0:T(2,128)(2,1)} %reshape.295), calls=%async_computation | async-start | bytes 524288 | tf_op jit(solution)/shard_map/all_to_all | solution.py:14
  31.3 12.4 %copy-start.10 = (f32[5,8192]{1,0:T(8,128)}, f32[5,8192]{1,0:T(8,128)S(1)}, u32[]{:S(2)}) copy-start(f32[5,8192]{1,0:T(8,128)S(1)} %stack.8) | copy-start | bytes 491524
  43.9 0.7 copy-start.15
  43.9 5.6 %copy-start.17 = (bf16[128,2,256]{2,1,0:T(2,128)(2,1)}, bf16[128,2,256]{2,1,0:T(2,128)(2,1)S(1)}, u32[]{:S(2)}) copy-start(bf16[128,2,256]{2,1,0:T(2,128)(2,1)S(1)} %get-tuple-element.27) | copy-start | bytes 393220
  45.5 2.0 copy-start.4
  51.6 2.9 copy-start.5
  51.6 2.9 copy-start.13
  53.3 2.4 copy-start.12
  59.7 38.8 %copy-start.2 = (f32[4,2,128,128]{3,2,1,0:T(8,128)}, f32[4,2,128,128]{3,2,1,0:T(8,128)S(1)}, u32[]{:S(2)}) copy-start(f32[4,2,128,128]{3,2,1,0:T(8,128)S(1)} %get-tuple-element.32) | copy-start | bytes 1572868
  62.4 2.5 copy-start.25
  64.1 2.7 copy-start.22
  64.1 2.7 copy-start.32
  64.9 1.9 copy-start.19
  83.8 10.4 %copy-start.1 = (f32[64,8192]{1,0:T(8,128)}, f32[64,8192]{1,0:T(8,128)S(1)}, u32[]{:S(2)}) copy-start(f32[64,8192]{1,0:T(8,128)S(1)} %get-tuple-element.33) | copy-start | bytes 6291460
  126.0 2.4 copy-start.3
  126.0 2.4 copy-start.14
  129.4 2.3 copy-start.16
  129.4 2.3 copy-start.18
  130.2 1.6 copy-start.33
  130.2 8.9 %copy-start.11 = (f32[5,8192]{1,0:T(8,128)S(1)}, f32[5,8192]{1,0:T(8,128)}, u32[]{:S(2)}) copy-start(f32[5,8192]{1,0:T(8,128)} %copy-done.10) | copy-start | bytes 491524
  134.1 26.3 %all-to-all-start.1 = ((bf16[128,2,512]{2,1,0:T(2,128)(2,1)}), bf16[128,2,512]{2,1,0:T(2,128)(2,1)S(1)}, u32[]{:S(2)}, u32[]{:S(2)}) async-start(bf16[128,2,512]{2,1,0:T(2,128)(2,1)} %pad_maximum_fusion.2), calls=%async_computation.1 | async-start | bytes 524288 | tf_op jit(solution)/shard_map/all_to_all | solution.py:14
  139.0 182.1 %all-reduce.2.cloned.1.call-start = ((), (), s32[]{:S(2)}) async-start(), calls=%async_computation.2 | async-start | bytes 2269184 | tf_op jit(solution)/shard_map/psum | solution.py:26
  139.1 10.2 %copy-start.23 = (f32[64,64]{1,0:T(8,128)S(1)}, f32[64,64]{1,0:T(8,128)}, u32[]{:S(2)}) copy-start(f32[64,64]{1,0:T(8,128)} %fusion.1) | copy-start | bytes 49156
  139.1 10.3 %copy-start.20 = (f32[2,128,64]{1,2,0:T(8,128)S(1)}, f32[2,128,64]{1,2,0:T(8,128)}, u32[]{:S(2)}) copy-start(f32[2,128,64]{1,2,0:T(8,128)} %copy-done.19) | copy-start | bytes 196612
  149.2 11.1 %copy-start.29 = (f32[64]{0:T(128)S(1)}, f32[64]{0:T(128)}, u32[]{:S(2)}) copy-start(f32[64]{0:T(128)} %get-tuple-element.14) | copy-start | bytes 772
  149.2 11.1 %copy-start.30 = (f32[64]{0:T(128)S(1)}, f32[64]{0:T(128)}, u32[]{:S(2)}) copy-start(f32[64]{0:T(128)} %get-tuple-element.10) | copy-start | bytes 772
  149.2 11.4 %copy-start.9 = (f32[256,256]{1,0:T(8,128)S(1)}, f32[256,256]{1,0:T(8,128)}, u32[]{:S(2)}) copy-start(f32[256,256]{1,0:T(8,128)} %copy-done.8) | copy-start | bytes 786436
  149.4 11.3 %copy-start.7 = (bf16[256,768]{1,0:T(8,128)(2,1)S(1)}, bf16[256,768]{1,0:T(8,128)(2,1)}, u32[]{:S(2)}) copy-start(bf16[256,768]{1,0:T(8,128)(2,1)} %copy-done.6) | copy-start | bytes 1179652
  149.4 11.3 %copy-start.21 = (bf16[1,256,256]{2,1,0:T(8,128)(2,1)S(1)}, bf16[1,256,256]{2,1,0:T(8,128)(2,1)}, u32[]{:S(2)}) copy-start(bf16[1,256,256]{2,1,0:T(8,128)(2,1)} %param.13) | copy-start | bytes 393220
  159.6 1.5 copy-start.24
  161.4 0.7 copy-start.27
  161.4 0.7 copy-start.28
Sparse Core Ops, SparseCore 0:
  172.1 149.0 all-reduce.1
where the time goes:
time: 347 us; the launch traced here: 341 us
  waiting for transfers between devices  153 us (44%)
  matrix products  109 us (31%)
  local copies, waits for them, and re-layouts  31.3 us (9%)
  starting transfers between devices  16.9 us (5%)
  between operations  15.4 us (4%)
  other arithmetic  15.3 us (4%)
    psum x1, waiting for transfers between devices, in_one(): so_far = lax.psum(flat, axis)  148 us
    dot_general x3, matrix products, contract_last(): lax.dot_general(left_side, right_side, (((1,), (1,)), ((), ())), precisio...  29.5 us
    dot_general x24, matrix products, right_multiply(): return jnp.einsum('...km,mj->...kj', stack_part, table, precision=highest)  28.2 us
    dot_general x3, matrix products, contract_first(): lax.dot_general(left_side, right_side, (((0,), (0,)), ((), ())), precisio...  26.7 us
    all_to_all x2, starting transfers between devices, side_by_side(): lax.all_to_all(both, axis, split_axis=split_dim, concat_axis=concat_dim,...  16.9 us
    dot_general x1, matrix products, mlp_backward(): grad_act_one = jnp.dot(hidden_weight, grad_pre_two, precision=highest)  10.5 us
    concatenate x1, local copies, waits for them, and re-layouts, in_one(): flat, at, done = (jnp.concatenate([a.reshape(-1) for a in arrays]), 0, [])  9.82 us
  transfers between devices with their start and end apart: 3, of which 2 were waited for; matrix products, arithmetic and copies ran while one was open for 8% of the time, Pallas kernels for 0%

commit v1 on v0

v1 whole, which is shorter than its diff:
```python
import math

import jax
import jax.numpy as jnp
from jax import lax
from jax.experimental import pallas as pl
from jax.experimental.pallas import tpu as pltpu
from jax.sharding import PartitionSpec as P

F32 = jnp.float32
BF16 = jnp.bfloat16
HIGHEST = lax.Precision.HIGHEST
AXES = ("seq", "batch")
LENGTH = 8192
BANDS = 2
NN = (((1,), (0,)), ((), ()))
NT = (((1,), (1,)), ((), ()))


def mm(a, b, dims=NN):
    return lax.dot_general(a, b, dims, preferred_element_type=F32)


def mm_full(a, b, dims=NN):
    return lax.dot_general(a, b, dims, precision=HIGHEST, preferred_element_type=F32)


def iota(shape, dim):
    return lax.broadcasted_iota(jnp.int32, shape, dim)


def one_hot(cond):
    return jnp.where(cond, 1.0, 0.0).astype(BF16)


def own_index():
    return lax.axis_index("seq") * lax.axis_size("batch") + lax.axis_index("batch")


def modulation(decay, first, shape):
    pos = (first + iota(shape, 0)).astype(F32)
    return 4.0 * jnp.exp(-decay * pos) / math.sqrt(LENGTH)


def forward_kernel(
    tok, og, wi, wo, ew, eb, hw, hb, fw, sf, dr,
    slab, go_o, gi_o, v_o, gg_o, bias_o, emb_o, pre1_o, act1_o, pre2_o, act2_o, scr,
):
    first = own_index() * 64
    proj = mm(tok[...], wi[...])
    go = proj[:, :256].astype(BF16)
    gi = proj[:, 256:512].astype(BF16)
    v = proj[:, 512:].astype(BF16)
    gg = mm(og[...], wo[...], NT).astype(BF16)
    go_o[...] = go
    gi_o[...] = gi
    v_o[...] = v
    gg_o[...] = gg
    mixed = (v.astype(F32) * gi.astype(F32)).astype(BF16).astype(F32)
    gc = (gg.astype(F32) * go.astype(F32)).astype(BF16).astype(F32)
    bias_o[...] = jnp.sum(gc * mixed, axis=0, keepdims=True)
    mixed_t = mixed.T
    gc_t = gc.T
    scaled = (first + iota((64, 64), 0)).astype(F32) / LENGTH
    rows = [scaled]
    for band in range(1, BANDS + 1):
        angle = 2.0 * math.pi * band * scaled
        rows.append(jnp.cos(angle))
        rows.append(jnp.sin(angle))
    pre1 = eb[...]
    for k in range(5):
        pre1 = pre1 + rows[k] * ew[k : k + 1, :]
        emb_o[k] = rows[k]
    act1 = jnp.sin(sf[0:1, :] * pre1)
    pre2 = mm_full(act1, hw[...]) + hb[...]
    act2 = jnp.sin(sf[1:2, :] * pre2)
    pre1_o[...] = pre1
    act1_o[...] = act1
    pre2_o[...] = pre2
    act2_o[...] = act2
    filt = mm_full(act2, fw[...]) * modulation(dr[...], first, (64, 256))
    place = one_hot(iota((64, 256), 1) == iota((64, 256), 0) + 64 * lax.axis_index("batch"))
    filt_t = mm(filt.T.astype(BF16), place)
    for at, whole in ((0, mixed_t), (4, gc_t), (8, filt_t)):
        for ch in range(2):
            for half in range(2):
                scr[:, at + 2 * ch + half, :] = whole[
                    128 * ch : 128 * ch + 128, 128 * half : 128 * half + 128
                ]
    slab[...] = scr[...].astype(BF16)


def conv_kernel(recv, skip, out, scr, osc, spad, spad_odd, fscr, acc, gpad, gs, gsc):
    scr[...] = recv[...].astype(F32)
    own = own_index()
    rev256 = one_hot(iota((256, 256), 0) + iota((256, 256), 1) == 255)
    rev128 = one_hot(iota((128, 128), 0) + iota((128, 128), 1) == 127)

    def order(row, col):
        blk, sig = row // 8, row % 8
        return (row >= 0) & (
            jnp.where(sig < 4, blk * 4 + sig, 128 + (31 - blk) * 4 + sig - 4) == col
        )

    row, col = iota((256, 256), 0), iota((256, 256), 1)
    perm = one_hot(order(row, col))
    perm_odd = one_hot(order(row - 8, col))
    back = one_hot(order(col, row))
    gather_f = one_hot(iota((256, 128), 1) // 4 == iota((256, 128), 0) // 8)
    spread_g = one_hot(iota((128, 64), 0) // 2 == iota((128, 64), 1))
    lane, sub = iota((128, 128), 1), iota((128, 128), 0)
    upper = lane >= sub
    keep = lane <= sub
    spad[0:256, :] = jnp.zeros((256, 256), BF16)
    spad_odd[0:256, :] = jnp.zeros((256, 256), BF16)
    for ch in range(2):
        xs = [scr[:, 2 * ch + h, :] for h in range(2)]
        gs_in = [scr[:, 4 + 2 * ch + h, :] for h in range(2)]
        fs = [scr[:, 8 + 2 * ch + h, :] for h in range(2)]
        x2 = jnp.concatenate(xs, axis=1).astype(BF16)
        g2 = jnp.concatenate(gs_in, axis=1).astype(BF16)
        g_rev = mm(g2, rev256).astype(BF16)
        both = jnp.concatenate([x2, g_rev], axis=0)
        spad[256:512, :] = mm(perm, both).astype(BF16)
        spad_odd[256:512, :] = mm(perm_odd, both).astype(BF16)
        fscr[...] = mm(gather_f, jnp.concatenate(fs, axis=1).astype(BF16))
        acc[...] = jnp.zeros((256, 256), F32)

        def conv_step(m, carry):
            w_last, u_last = carry
            us = [u_last]
            for n in range(4):
                at = pl.multiple_of(16 * m + 8 * (n // 2), 8)
                line = fscr[pl.ds(at, 8), 128 * (n % 2) : 128 * (n % 2) + 128]
                w = pltpu.roll(
                    jnp.concatenate([line] * 16, axis=0), 0, 1, stride=1, stride_axis=0
                )
                us.append(jnp.where(upper, w, w_last).astype(BF16))
                w_last = w
            toep = jnp.concatenate(
                [
                    jnp.concatenate([us[1], us[2]], axis=1),
                    jnp.concatenate([us[0], us[1]], axis=1),
                    jnp.concatenate([us[3], us[4]], axis=1),
                    jnp.concatenate([us[2], us[3]], axis=1),
                ],
                axis=0,
            )
            at = pl.multiple_of(256 - 16 * m, 16)
            left = jnp.concatenate(
                [spad[pl.ds(at, 256), :], spad_odd[pl.ds(at, 256), :]], axis=1
            )
            acc[...] += mm(left, toep)
            return (w_last, us[4])

        lax.fori_loop(
            0, 16, conv_step, (jnp.zeros((128, 128), F32), jnp.zeros((128, 128), BF16))
        )
        skip_now = skip[own + 128 * ch]
        done = (acc[...] + skip_now * spad[256:512, :].astype(F32)).astype(BF16)
        apart = mm(back, done)
        conv2 = apart[0:128, :]
        gm2 = mm(apart[128:256, :].astype(BF16), rev256)
        for h in range(2):
            osc[:, 2 * ch + h, :] = conv2[:, 128 * h : 128 * h + 128]
            osc[:, 4 + 2 * ch + h, :] = gm2[:, 128 * h : 128 * h + 128]

        x_rev = jnp.concatenate(
            [mm(rev128, x.astype(BF16), NT).astype(BF16) for x in xs], axis=1
        )
        for h in range(2):
            gpad[0:128, :] = gs_in[h]
            gpad[128:288, :] = jnp.zeros((160, 128), F32)
            for s in range(4):
                gs[4 * h + s] = gpad[4 * s : 4 * s + 256, :].astype(BF16)

        def corr_step(q, d_last):
            for s in range(4):
                at = pl.multiple_of(16 * q, 16)
                at_next = pl.multiple_of(16 * q + 16 * (s // 3), 16)
                g0 = gs[s, pl.ds(at, 128), :]
                g1 = gs[4 + s, pl.ds(at, 128), :]
                g0_next = gs[(s + 1) % 4, pl.ds(at_next, 128), :]
                right = jnp.concatenate(
                    [
                        jnp.concatenate([g0, g1], axis=1),
                        jnp.concatenate([g1, g0_next], axis=1),
                    ],
                    axis=0,
                )
                c = mm(x_rev, right)
                for odd in range(2):
                    d = pltpu.roll(
                        c[:, 128 * odd : 128 * odd + 128], 1, 1, stride=1, stride_axis=0
                    )
                    part = jnp.where(keep, d_last, d).reshape(16, 8, 128).sum(axis=0)
                    gsc[pl.ds(pl.multiple_of(64 * q + 8 * (2 * s + odd), 8), 8), :] = part
                    d_last = d
            return d_last

        d_end = lax.fori_loop(0, 8, corr_step, jnp.zeros((128, 128), F32))
        gsc[512:520, :] = jnp.where(keep, d_end, 0.0).reshape(16, 8, 128).sum(axis=0)
        gf = gsc[8:520, :].reshape(64, 8, 128).sum(axis=1)
        hi = gf.astype(BF16)
        lo = (gf - hi.astype(F32)).astype(BF16)
        osc[:, 8 + ch, :] = mm(spread_g, hi)
        osc[:, 10 + ch, :] = mm(spread_g, lo)
    out[...] = osc[...].astype(BF16)


def backward_kernel(
    recv, go, gi, v, gg, tok, og, wi, emb, pre1, act1, pre2, act2, bias, hw, fw, sf, dr,
    gtok, slab, scr, tmp, sm, ssc,
):
    own = own_index()
    first = own * 64
    scr[...] = recv[...].astype(F32)

    def whole(at):
        return jnp.concatenate(
            [
                jnp.concatenate([scr[:, at + 2 * ch, :], scr[:, at + 2 * ch + 1, :]], axis=1)
                for ch in range(2)
            ],
            axis=0,
        )

    conv = whole(0).T
    gm = whole(4).T
    gated_t = (go[...].astype(F32) * conv).T.astype(BF16)
    grad_ow = mm(gated_t, og[...])
    gp = jnp.concatenate(
        [
            (gg[...].astype(F32) * conv).astype(BF16),
            (gm * v[...].astype(F32)).astype(BF16),
            (gm * gi[...].astype(F32)).astype(BF16),
        ],
        axis=1,
    )
    gtok[...] = mm(gp, wi[...], NT).astype(BF16)
    grad_iw = mm(tok[...].astype(F32).T.astype(BF16), gp)
    for rt in range(16):
        for cb in range(8):
            src = grad_iw if cb < 6 else grad_ow
            at = 128 * (cb if cb < 6 else cb - 6)
            slab[rt * 8 + cb, 0:16, :] = src[16 * rt : 16 * rt + 16, at : at + 128].astype(BF16)

    gf_pair = jnp.concatenate(
        [scr[:, 8 + ch, :] + scr[:, 10 + ch, :] for ch in range(2)], axis=0
    )
    tmp[...] = gf_pair.T
    gf = tmp[pl.ds(pl.multiple_of((own % 2) * 64, 64), 64), :]
    gk = gf * modulation(dr[...], first, (64, 256))
    grad_fw = mm_full(act2[...].T, gk)
    ga2 = mm_full(gk, fw[...], NT)
    cos2 = jnp.cos(sf[1:2, :] * pre2[...])
    gp2 = ga2 * sf[1:2, :] * cos2
    grad_f2 = jnp.sum(ga2 * pre2[...] * cos2, axis=0, keepdims=True)
    grad_hb = jnp.sum(gp2, axis=0, keepdims=True)
    grad_hw = mm_full(act1[...].T, gp2)
    ga1 = mm_full(gp2, hw[...], NT)
    cos1 = jnp.cos(sf[0:1, :] * pre1[...])
    gp1 = ga1 * sf[0:1, :] * cos1
    grad_f1 = jnp.sum(ga1 * pre1[...] * cos1, axis=0, keepdims=True)
    grad_eb = jnp.sum(gp1, axis=0, keepdims=True)
    sm[...] = jnp.zeros((128, 128), F32)
    sm[0:64, 0:64] = grad_hw
    for k in range(5):
        sm[64 + k : 65 + k, 0:64] = jnp.sum(emb[k] * gp1, axis=0, keepdims=True)
    sm[69:70, 0:64] = grad_eb
    sm[70:71, 0:64] = grad_hb
    sm[71:72, 0:64] = grad_f1
    sm[72:73, 0:64] = grad_f2
    sm[73:74, :] = bias[:, 0:128]
    sm[74:75, :] = bias[:, 128:256]
    small = (jnp.concatenate([grad_fw[:, 0:128], grad_fw[:, 128:256]], axis=0), sm[...])
    for k in range(2):
        hi = small[k].astype(BF16).astype(F32)
        ssc[:, 2 * k, :] = hi
        ssc[:, 2 * k + 1, :] = small[k] - hi
        ssc[:, 4 + 2 * k, :] = jnp.zeros((128, 128), F32)
        ssc[:, 5 + 2 * k, :] = jnp.zeros((128, 128), F32)
    slab[:, 16:24, :] = ssc[...].astype(BF16)


def sum_kernel(recv, out):
    total = jnp.sum(recv[...].astype(F32), axis=0)
    main = total[0:16, :]
    small = total[16:24, :]
    rows = []
    for k in range(2):
        now = small[2 * k : 2 * k + 1, :] + small[2 * k + 1 : 2 * k + 2, :]
        hi = now.astype(BF16).astype(F32)
        rows += [hi, now - hi]
    rows.append(jnp.zeros((4, 128), F32))
    done = jnp.concatenate([main] + rows, axis=0).astype(BF16)
    out[...] = jnp.broadcast_to(done[None], out.shape)


def unpack_kernel(recv, giw, gow, gsb, gew, geb, ghw, ghb, gfw, gsf, scr):
    scale = 1.0 / math.sqrt(4 * LENGTH)
    fscale = scale / 4.0
    for rt in range(16):
        for cb in range(8):
            tile = recv[rt * 8 + cb, 0:16, :].astype(F32) * scale
            if cb < 6:
                giw[16 * rt : 16 * rt + 16, 128 * cb : 128 * cb + 128] = tile
            else:
                gow[16 * rt : 16 * rt + 16, 128 * (cb - 6) : 128 * (cb - 6) + 128] = tile
    scr[...] = recv[:, 16:24, :].astype(F32)
    first = (scr[:, 0, :] + scr[:, 1, :]) * fscale
    gfw[:, 0:128] = first[0:64, :]
    gfw[:, 128:256] = first[64:128, :]
    second = scr[:, 2, :] + scr[:, 3, :]
    ghw[...] = second[0:64, 0:64] * fscale
    gew[...] = second[64:69, 0:64] * fscale
    geb[...] = second[69:70, 0:64] * fscale
    ghb[...] = second[70:71, 0:64] * fscale
    gsf[...] = second[71:73, 0:64] * fscale
    gsb[:, 0:128] = second[73:74, :] * scale
    gsb[:, 128:256] = second[74:75, :] * scale


def call(kernel, name, out_shape, scratch=(), smem_at=()):
    def run(*args):
        return pl.pallas_call(
            kernel,
            out_shape=out_shape,
            in_specs=[
                pl.BlockSpec(memory_space=pltpu.SMEM if k in smem_at else pltpu.VMEM)
                for k in range(len(args))
            ],
            scratch_shapes=list(scratch),
            compiler_params=pltpu.CompilerParams(vmem_limit_bytes=48 * 1024 * 1024),
            name=name,
        )(*args)

    return run


def exchange(x):
    return lax.all_to_all(x, AXES, split_axis=0, concat_axis=0, tiled=True)


def sds(*shape, dtype=F32):
    return jax.ShapeDtypeStruct(shape, dtype)


def shards(
    tokens, out_grad, in_weight, out_weight, skip_bias, embed_weight, embed_bias,
    hidden_weight, hidden_bias, filter_weight, sine_freq, decay_rate,
):
    tok = tokens[0]
    og = out_grad[0]
    decay = decay_rate[None, :]
    square = sds(256, 256, dtype=BF16)
    hidden = sds(64, 64)
    (slab, go, gi, v, gg, bias, emb, pre1, act1, pre2, act2) = call(
        forward_kernel,
        "forward",
        (sds(128, 16, 128, dtype=BF16), square, square, square, square, sds(1, 256),
         sds(5, 64, 64), hidden, hidden, hidden, hidden),
        [pltpu.VMEM((128, 16, 128), F32)],
    )(tok, og, in_weight, out_weight, embed_weight, embed_bias[None, :], hidden_weight,
      hidden_bias[None, :], filter_weight, sine_freq, decay)
    recv = exchange(slab)
    sent = call(
        conv_kernel,
        "conv",
        sds(128, 16, 128, dtype=BF16),
        [
            pltpu.VMEM((128, 16, 128), F32),
            pltpu.VMEM((128, 16, 128), F32),
            pltpu.VMEM((512, 256), BF16),
            pltpu.VMEM((512, 256), BF16),
            pltpu.VMEM((256, 256), F32),
            pltpu.VMEM((256, 256), F32),
            pltpu.VMEM((288, 128), F32),
            pltpu.VMEM((8, 256, 128), BF16),
            pltpu.VMEM((520, 128), F32),
        ],
        (1,),
    )(recv, skip_bias)
    recv = exchange(sent)
    gtok, slab = call(
        backward_kernel,
        "backward",
        (square, sds(128, 24, 128, dtype=BF16)),
        [
            pltpu.VMEM((128, 16, 128), F32),
            pltpu.VMEM((128, 256), F32),
            pltpu.VMEM((128, 128), F32),
            pltpu.VMEM((128, 8, 128), F32),
        ],
    )(recv, go, gi, v, gg, tok, og, in_weight, emb, pre1, act1, pre2, act2, bias, hidden_weight,
      filter_weight, sine_freq, decay)
    recv = exchange(slab)
    total = call(sum_kernel, "total", sds(128, 24, 128, dtype=BF16))(recv)
    recv = exchange(total)
    giw, gow, gsb, gew, geb, ghw, ghb, gfw, gsf = call(
        unpack_kernel,
        "unpack",
        (sds(256, 768), sds(256, 256), sds(1, 256), sds(5, 64), sds(1, 64), sds(64, 64),
         sds(1, 64), sds(64, 256), sds(2, 64)),
        [pltpu.VMEM((128, 8, 128), F32)],
    )(recv)
    return (gtok[None], giw, gow, gsb[0], gew, geb[0], ghw, ghb[0], gfw, gsf)


def solution(mesh):
    return jax.shard_map(
        shards,
        mesh=mesh,
        in_specs=(P("batch", "seq", None),) * 2 + (P(),) * 10,
        out_specs=(P("batch", "seq", None),) + (P(),) * 9,
        check_vma=False,
    )
```

time: 347 us -> 116 us (0.33); the launches traced: 341 us -> 116 us
  waiting for transfers between devices: 153 us -> 0 us
  matrix products: 109 us -> 0 us
  blocking collectives: 0 us -> 83.9 us
  local copies, waits for them, and re-layouts: 31.3 us -> 6.03 us
  Pallas kernels: 0 us -> 24.8 us
  starting transfers between devices: 16.9 us -> 0 us
  other arithmetic: 15.3 us -> 0 us
  between operations: 15.4 us -> 0.78 us
    psum x1 -> x0, waiting for transfers between devices: 148 us -> none  [in_one(): so_far = lax.psum(flat, axis)]
    dot_general x49 -> x0, matrix products: 109 us -> none  [the longest x3 29.5 us: contract_last(): lax.dot_general(left_side, right_side, (((1,), (1,)), ((), ())), precisio...]
    all_to_all x0 -> x4, blocking collectives: none -> 83.9 us  [exchange(): return lax.all_to_all(x, AXES, split_axis=0, concat_axis=0, tiled=True)]
    pallas_call x0 -> x5, Pallas kernels: none -> 24.8 us  [run(): pl.pallas_call(kernel, out_shape=out_shape, in_specs=[pl.BlockSpec(memory...]
    all_to_all x2 -> x0, starting transfers between devices: 16.9 us -> none  [side_by_side(): lax.all_to_all(both, axis, split_axis=split_dim, concat_axis=concat_dim,...]
    concatenate x2 -> x0, local copies, waits for them, and re-layouts: 10.3 us -> none  [the longest x1 9.82 us: in_one(): flat, at, done = (jnp.concatenate([a.reshape(-1) for a in arrays]), 0, [])]
    mul x8 -> x0, other arithmetic: 7.82 us -> none  [the longest x1 1.27 us: shards(): totals[6] * filter_scale]
    all_to_all x2 -> x0, waiting for transfers between devices: 4.89 us -> none  [side_by_side(): lax.all_to_all(both, axis, split_axis=split_dim, concat_axis=concat_dim,...]
  transfers between devices with their start and end apart: 3 -> 0, of which waited for: 2 -> 0; matrix products, arithmetic and copies ran while one was open for 8% -> 0% of each run, Pallas kernels for 0% -> 0%
where the time goes in v1:
time: 116 us
  blocking collectives  83.9 us (72%)
  Pallas kernels  24.8 us (21%)
  local copies, waits for them, and re-layouts  6.03 us (5%)
    all_to_all x4, blocking collectives, exchange(): return lax.all_to_all(x, AXES, split_axis=0, concat_axis=0, tiled=True)  83.9 us
    pallas_call x5, Pallas kernels, run(): pl.pallas_call(kernel, out_shape=out_shape, in_specs=[pl.BlockSpec(memory...  24.8 us
    unnamed x34, local copies, waits for them, and re-layouts  6.03 us

profile of v1, /device:TPU:1, one launch (start us, length us, event | category | flops | bytes accessed | tf_op | source)
XLA Modules:
  0.0 115.6 jit_solution(2879995653209584502)
XLA Ops:
  0.6 0.0 copy-start.11
  0.7 0.0 copy-start.13
  0.7 0.0 copy-start.16
  0.7 0.0 copy-start.12
  0.7 0.0 copy-start.15
  0.7 0.6 copy-done.11
  1.3 0.0 copy-done.13
  1.3 0.0 copy-done.16
  1.3 0.0 copy-done.12
  1.4 0.0 copy-done.15
  1.4 0.0 copy-start
  1.4 1.0 copy-done
  2.4 0.0 copy-start.2
  2.4 0.9 copy-done.2
  3.3 0.0 copy-start.4
  3.3 0.9 copy-done.4
  4.2 0.0 copy-start.6
  4.2 0.8 copy-done.6
  5.0 0.0 copy-start.8
  5.0 0.8 copy-done.8
  5.8 0.0 copy-start.10
  5.8 0.9 copy-done.10
  6.7 1.6 %forward.1 = (bf16[128,16,128]{2,1,0:T(8,128)(2,1)S(1)}, bf16[256,256]{1,0:T(8,128)(2,1)S(1)}, bf16[256,256]{1,0:T(8,128)(2,1)S(1)}, bf16[256,256]{1,0:T(8,128)(...) custom-call(bf16[256,256]{1,0:T(8,128)(2,1)S(1)} %bitcast.9, ...), custom_call_target="tpu_custom_call" | custom-call | tf_op jit(solution)/shard_map/forward/pallas_call | solution.py:326
  8.2 0.0 copy-start.14
  8.3 24.9 %all_to_all.20.recv = bf16[128,16,128]{2,1,0:T(8,128)(2,1)S(1)} all-to-all(bf16[128,16,128]{2,1,0:T(8,128)(2,1)S(1)} %get-tuple-element.32), channel_id=1, replica_groups=mesh['seq'=32,'batch'=4] {'seq','batch'}, dimensions={0} | all-to-all | bytes 1048576 | tf_op jit(solution)/shard_map/all_to_all | solution.py:342
  33.1 0.0 copy-done.14
  33.1 20.1 %conv.1 = bf16[128,16,128]{2,1,0:T(8,128)(2,1)S(1)} custom-call(bf16[128,16,128]{2,1,0:T(8,128)(2,1)S(1)} %all_to_all.20.recv, f32[256]{0:T(256)S(1)} %copy-done.14), custom_call_target="tpu_custom_call" | custom-call | tf_op jit(solution)/shard_map/conv/pallas_call | solution.py:326
  53.3 0.0 copy-start.1
  53.3 0.0 copy-start.3
  53.3 0.0 copy-start.5
  53.3 0.0 copy-start.7
  53.3 0.0 copy-start.9
  53.3 18.0 %all_to_all.21.recv = bf16[128,16,128]{2,1,0:T(8,128)(2,1)S(1)} all-to-all(bf16[128,16,128]{2,1,0:T(8,128)(2,1)S(1)} %conv.1), channel_id=1, replica_groups=mesh['seq'=32,'batch'=4] {'seq','batch'}, dimensions={0} | all-to-all | bytes 1048576 | tf_op jit(solution)/shard_map/all_to_all | solution.py:342
  71.3 0.0 copy-done.1
  71.3 0.0 copy-done.3
  71.3 0.0 copy-done.5
  71.3 0.0 copy-done.7
  71.3 0.0 copy-done.9
  71.3 1.8 %backward.1 = (bf16[256,256]{1,0:T(8,128)(2,1)}, bf16[128,24,128]{2,1,0:T(8,128)(2,1)S(1)}) custom-call(bf16[128,16,128]{2,1,0:T(8,128)(2,1)S(1)} %all_to_all.21.recv, bf16[256,256]{1,0:T(8,128)(2,1)S(1)} %get-tuple-element.33.go, bf16[256,256]{1,0:T(8,128)(2,1)S(1)} %get-tuple-element.34.gi, bf16[256,256]{1,0:T(8,128)(2,1)S(1)} %get-tuple-element.35.v, ...), custom_call_target="tpu_custom_call" | custom-call | tf_op jit(solution)/shard_map/backward/pallas_call | solution.py:326
  73.1 20.4 %all_to_all.22.recv = bf16[128,24,128]{2,1,0:T(8,128)(2,1)S(1)} all-to-all(bf16[128,24,128]{2,1,0:T(8,128)(2,1)S(1)} %get-tuple-element.44), channel_id=1, replica_groups=mesh['seq'=32,'batch'=4] {'seq','batch'}, dimensions={0} | all-to-all | bytes 1572864 | tf_op jit(solution)/shard_map/all_to_all | solution.py:342
  93.5 0.2 total.1
  93.7 20.7 %all_to_all.23.recv = bf16[128,24,128]{2,1,0:T(8,128)(2,1)S(1)} all-to-all(bf16[128,24,128]{2,1,0:T(8,128)(2,1)S(1)} %total.1), channel_id=1, replica_groups=mesh['seq'=32,'batch'=4] {'seq','batch'}, dimensions={0} | all-to-all | bytes 1572864 | tf_op jit(solution)/shard_map/all_to_all | solution.py:342
  114.4 1.1 unpack.1
Async XLA Ops:
  0.6 0.7 copy-start.11
  0.7 0.7 copy-start.13
  0.7 0.7 copy-start.16
  0.7 0.7 copy-start.12
  0.7 0.7 copy-start.15
  1.4 1.0 copy-start
  2.4 0.9 copy-start.2
  3.3 0.9 copy-start.4
  4.2 0.8 copy-start.6
  5.0 0.8 copy-start.8
  5.8 0.9 copy-start.10
  8.2 24.9 %copy-start.14 = (f32[256]{0:T(256)S(1)}, f32[256]{0:T(256)}, u32[]{:S(2)}) copy-start(f32[256]{0:T(256)} %skip.1) | copy-start | bytes 3076
  53.3 18.0 %copy-start.1 = (bf16[256,768]{1,0:T(8,128)(2,1)S(1)}, bf16[256,768]{1,0:T(8,128)(2,1)}, u32[]{:S(2)}) copy-start(bf16[256,768]{1,0:T(8,128)(2,1)} %wi.3) | copy-start | bytes 1179652
  53.3 18.0 %copy-start.3 = (bf16[1,256,256]{2,1,0:T(8,128)(2,1)S(1)}, bf16[1,256,256]{2,1,0:T(8,128)(2,1)}, u32[]{:S(2)}) copy-start(bf16[1,256,256]{2,1,0:T(8,128)(2,1)} %param.12) | copy-start | bytes 393220
  53.3 18.0 %copy-start.5 = (bf16[1,256,256]{2,1,0:T(8,128)(2,1)S(1)}, bf16[1,256,256]{2,1,0:T(8,128)(2,1)}, u32[]{:S(2)}) copy-start(bf16[1,256,256]{2,1,0:T(8,128)(2,1)} %param.13) | copy-start | bytes 393220
  53.3 18.0 %copy-start.7 = (f32[64,256]{1,0:T(8,128)S(1)}, f32[64,256]{1,0:T(8,128)}, u32[]{:S(2)}) copy-start(f32[64,256]{1,0:T(8,128)} %fw.3) | copy-start | bytes 196612
  53.3 18.0 %copy-start.9 = (f32[64,64]{1,0:T(8,128)S(1)}, f32[64,64]{1,0:T(8,128)}, u32[]{:S(2)}) copy-start(f32[64,64]{1,0:T(8,128)} %hw.3) | copy-start | bytes 49156

commit v2 on v1

v2 whole, which is shorter than its diff:
```python
import math

import jax
import jax.numpy as jnp
from jax import lax
from jax.experimental import pallas as pl
from jax.experimental.pallas import tpu as pltpu
from jax.sharding import PartitionSpec as P

F32 = jnp.float32
BF16 = jnp.bfloat16
HIGHEST = lax.Precision.HIGHEST
AXES = ("seq", "batch")
LENGTH = 8192
BANDS = 2
NN = (((1,), (0,)), ((), ()))
NT = (((1,), (1,)), ((), ()))


def mm(a, b, dims=NN):
    return lax.dot_general(a, b, dims, preferred_element_type=F32)


def mm_full(a, b, dims=NN):
    return lax.dot_general(a, b, dims, precision=HIGHEST, preferred_element_type=F32)


def iota(shape, dim):
    return lax.broadcasted_iota(jnp.int32, shape, dim)


def one_hot(cond):
    return jnp.where(cond, 1.0, 0.0).astype(BF16)


def own_index():
    return lax.axis_index("seq") * lax.axis_size("batch") + lax.axis_index("batch")


def modulation(decay, first, shape):
    pos = (first + iota(shape, 0)).astype(F32)
    return 4.0 * jnp.exp(-decay * pos) / math.sqrt(LENGTH)


def forward_kernel(
    tok_h, og_h, wi_h, wo_h, ew_h, eb_h, hw_h, hb_h, fw_h, sf_h, dr_h,
    slab, go_o, gi_o, v_o, gg_o, bias_o, emb_o, pre1_o, act1_o, pre2_o, act2_o,
    tok, og, wi, wo, ew, eb, hw, hb, fw, sf, dr, scr, sems,
):
    pairs = (
        (tok_h, tok), (wi_h, wi), (og_h, og), (wo_h, wo), (sf_h, sf), (ew_h, ew), (eb_h, eb),
        (hw_h, hw), (hb_h, hb), (fw_h, fw), (dr_h, dr),
    )
    copies = [pltpu.make_async_copy(a, b, sems.at[k]) for k, (a, b) in enumerate(pairs)]
    for c in copies:
        c.start()
    first = own_index() * 64
    scaled = (first + iota((64, 64), 0)).astype(F32) / LENGTH
    rows = [scaled]
    for band in range(1, BANDS + 1):
        angle = 2.0 * math.pi * band * scaled
        rows.append(jnp.cos(angle))
        rows.append(jnp.sin(angle))
    for c in copies:
        c.wait()
    proj = mm(tok[...], wi[...])
    go = proj[:, :256].astype(BF16)
    gi = proj[:, 256:512].astype(BF16)
    v = proj[:, 512:].astype(BF16)
    gg = mm(og[...], wo[...], NT).astype(BF16)
    go_o[...] = go
    gi_o[...] = gi
    v_o[...] = v
    gg_o[...] = gg
    mixed = (v.astype(F32) * gi.astype(F32)).astype(BF16).astype(F32)
    gc = (gg.astype(F32) * go.astype(F32)).astype(BF16).astype(F32)
    bias_o[...] = jnp.sum(gc * mixed, axis=0, keepdims=True)
    mixed_t = mixed.T
    gc_t = gc.T
    pre1 = eb[...]
    for k in range(5):
        pre1 = pre1 + rows[k] * ew[k : k + 1, :]
        emb_o[k] = rows[k]
    act1 = jnp.sin(sf[0:1, :] * pre1)
    pre2 = mm_full(act1, hw[...]) + hb[...]
    act2 = jnp.sin(sf[1:2, :] * pre2)
    pre1_o[...] = pre1
    act1_o[...] = act1
    pre2_o[...] = pre2
    act2_o[...] = act2
    filt = mm_full(act2, fw[...]) * modulation(dr[...], first, (64, 256))
    side = 64 * (lax.axis_index("batch") % 2)
    place = one_hot(iota((64, 128), 1) == iota((64, 128), 0) + side)
    filt_t = mm(filt.T.astype(BF16), place)
    for ch in range(2):
        scr[pl.ds(8 + ch, 128, stride=10), :] = filt_t[128 * ch : 128 * ch + 128, :]
        for at, whole in ((0, mixed_t), (4, gc_t)):
            for half in range(2):
                scr[pl.ds(at + 2 * ch + half, 128, stride=10), :] = whole[
                    128 * ch : 128 * ch + 128, 128 * half : 128 * half + 128
                ]
    slab[...] = scr[...].astype(BF16)


def row_rolls(x):
    row = iota(x.shape, 0)
    for bit in range(3):
        x = jnp.where((row >> bit) & 1 == 1, pltpu.roll(x, 1 << bit, 1), x)
    return x


def conv_kernel(recv, skip, out, scr, osc, fscr, ubuf, gpad, gs, gsc):
    scr[...] = recv[...].astype(F32)
    own = own_index()
    row, col = iota((256, 256), 0), iota((256, 256), 1)
    rev256 = one_hot(row + col == 255)
    rev128 = one_hot(iota((128, 128), 0) + iota((128, 128), 1) == 127)

    def source(r):
        blk, sig = r >> 3, r & 7
        return jnp.where(sig < 4, blk * 4 + sig, 128 + (31 - blk) * 4 + sig - 4)

    perm = one_hot(source(row) == col)
    back = one_hot(source(col) == row)
    gather = [
        one_hot(iota((256, 128), 1) >> 1 == 2 * (iota((256, 128), 0) >> 3) + h) for h in range(2)
    ]
    spread_g = one_hot(iota((128, 64), 0) >> 1 == iota((128, 64), 1))
    lane, sub = iota((8, 128), 1), iota((8, 128), 0)
    ready = lane >= sub

    def line(r):
        return scr[pl.ds(r, 128, stride=10), :]

    for ch in range(2):
        f_in = line(8 + ch).astype(BF16)
        fscr[ch, 0:8, :] = jnp.zeros((8, 256), F32)
        for h in range(2):
            fscr[ch, 8:264, 128 * h : 128 * h + 128] = row_rolls(mm(gather[h], f_in))
        ubuf[ch, 0:128, :] = jnp.zeros((128, 128), BF16)

    def toeplitz_step(n, carry):
        for ch in range(2):
            at = pl.multiple_of(8 * n, 8)
            before = fscr[ch, pl.ds(at, 8), 128:256]
            now = fscr[ch, pl.ds(pl.multiple_of(at + 8, 8), 8), :]
            for odd in range(2):
                last = before if odd == 0 else now[:, 0:128]
                this = now[:, 128 * odd : 128 * odd + 128]
                fresh = jnp.where(ready, this, last)
                tiles = [fresh]
                for g in range(1, 16):
                    picked = jnp.where(lane < 128 - 8 * g, fresh, last)
                    tiles.append(pltpu.roll(picked, 8 * g, 1))
                to = pl.multiple_of(256 * n + 128 * (odd + 1), 128)
                ubuf[ch, pl.ds(to, 128), :] = jnp.concatenate(tiles, axis=0).astype(BF16)
        return carry

    lax.fori_loop(0, 32, toeplitz_step, 0)

    for ch in range(2):
        xs = [line(2 * ch + h) for h in range(2)]
        gs_in = [line(4 + 2 * ch + h) for h in range(2)]
        x2 = jnp.concatenate(xs, axis=1).astype(BF16)
        g2 = jnp.concatenate(gs_in, axis=1).astype(BF16)
        g_rev = mm(g2, rev256).astype(BF16)
        mixed_up = mm(perm, jnp.concatenate([x2, g_rev], axis=0))
        shifted = (
            mixed_up.astype(BF16),
            jnp.concatenate([jnp.zeros((8, 256), F32), mixed_up[0:248, :]], axis=0).astype(BF16),
        )
        total = None
        for q in range(4):
            low = 64 * q
            left, right = [], []
            for k in range(8 * q, 8 * q + 8):
                down = 16 * (k // 2)
                piece = shifted[k % 2]
                if down <= low:
                    left.append(piece[low - down : 256 - down, :])
                else:
                    left.append(
                        jnp.concatenate(
                            [jnp.zeros((down - low, 256), BF16), piece[0 : 256 - down, :]], axis=0
                        )
                    )
                u = [ubuf[ch, 128 * n : 128 * n + 128, :] for n in range(2 * k, 2 * k + 3)]
                right.append(jnp.concatenate([u[1], u[2]], axis=1))
                right.append(jnp.concatenate([u[0], u[1]], axis=1))
            part = mm(jnp.concatenate(left, axis=1), jnp.concatenate(right, axis=0))
            if total is None:
                total = part
            else:
                total = jnp.concatenate([total[0:low, :], total[low:, :] + part], axis=0)
        mine = iota((1, 256), 1) == own + 128 * ch
        skip_now = jnp.sum(jnp.where(mine, skip[...], 0.0), axis=1, keepdims=True)
        done = (total + skip_now * mixed_up).astype(BF16)
        apart = mm(back, done)
        conv2 = apart[0:128, :]
        gm2 = mm(apart[128:256, :].astype(BF16), rev256)
        for h in range(2):
            osc[pl.ds(2 * ch + h, 128, stride=10), :] = conv2[:, 128 * h : 128 * h + 128]
            osc[pl.ds(4 + 2 * ch + h, 128, stride=10), :] = gm2[:, 128 * h : 128 * h + 128]

        x_rev = jnp.concatenate(
            [mm(rev128, x.astype(BF16), NT).astype(BF16) for x in xs], axis=1
        )
        for h in range(2):
            gpad[0:128, :] = gs_in[h]
            gpad[128:288, :] = jnp.zeros((160, 128), F32)
            for s in range(4):
                gs[4 * h + s] = gpad[4 * s : 4 * s + 256, :].astype(BF16)

        def corr_step(q, c_last):
            for s in range(4):
                at = pl.multiple_of(16 * q, 16)
                at_next = pl.multiple_of(16 * q + 16 * (s // 3), 16)
                g0 = gs[s, pl.ds(at, 128), :]
                g1 = gs[4 + s, pl.ds(at, 128), :]
                g0_next = gs[(s + 1) % 4, pl.ds(at_next, 128), :]
                right = jnp.concatenate(
                    [
                        jnp.concatenate([g0, g1], axis=1),
                        jnp.concatenate([g1, g0_next], axis=1),
                    ],
                    axis=0,
                )
                both = mm(x_rev, right)
                for odd in range(2):
                    c = both[:, 128 * odd : 128 * odd + 128]
                    part = diagonals(c_last, c)
                    gsc[pl.ds(pl.multiple_of(64 * q + 8 * (2 * s + odd), 8), 8), :] = part
                    c_last = c
            return c_last

        def diagonals(c_last, c):
            part = None
            for g in range(16):
                old = c_last[8 * g : 8 * g + 8, :]
                if c is None:
                    new = jnp.zeros((8, 128), F32)
                else:
                    new = c[8 * g : 8 * g + 8, :]
                now = pltpu.roll(jnp.where(lane + sub >= 127 - 8 * g, old, new), 8 * g + 1, 1)
                part = now if part is None else part + now
            return part

        c_end = lax.fori_loop(0, 8, corr_step, jnp.zeros((128, 128), F32))
        gsc[512:520, :] = diagonals(c_end, None)
        gf = row_rolls(gsc[8:520, :]).reshape(64, 8, 128).sum(axis=1)
        osc[pl.ds(8 + ch, 128, stride=10), :] = mm(spread_g, gf.astype(BF16))
    out[...] = osc[...].astype(BF16)


def backward_kernel(
    recv, go, gi, v, gg, tok, og, wi, emb, pre1, act1, pre2, act2, bias, hw, fw, sf, dr,
    gtok, slab, scr, tmp, sm, ssc,
):
    own = own_index()
    first = own * 64
    scr[...] = recv[...].astype(F32)

    def line(r):
        return scr[pl.ds(r, 128, stride=10), :]

    def whole(at):
        return jnp.concatenate(
            [
                jnp.concatenate([line(at + 2 * ch), line(at + 2 * ch + 1)], axis=1)
                for ch in range(2)
            ],
            axis=0,
        )

    conv = whole(0).T
    gm = whole(4).T
    gated_t = (go[...].astype(F32) * conv).T.astype(BF16)
    grad_ow = mm(gated_t, og[...])
    gp = jnp.concatenate(
        [
            (gg[...].astype(F32) * conv).astype(BF16),
            (gm * v[...].astype(F32)).astype(BF16),
            (gm * gi[...].astype(F32)).astype(BF16),
        ],
        axis=1,
    )
    gtok[...] = mm(gp, wi[...], NT).astype(BF16)
    grad_iw = mm(tok[...].astype(F32).T.astype(BF16), gp)
    for rb in range(2):
        for cb in range(8):
            src = grad_iw if cb < 6 else grad_ow
            at = 128 * (cb if cb < 6 else cb - 6)
            ssc[pl.ds(8 * rb + cb, 128, stride=18), :] = src[
                128 * rb : 128 * rb + 128, at : at + 128
            ]

    tmp[...] = jnp.concatenate([line(8), line(9)], axis=0).T
    gf = tmp[pl.ds(pl.multiple_of((own % 2) * 64, 64), 64), :]
    gk = gf * modulation(dr[...], first, (64, 256))
    grad_fw = mm_full(act2[...].T, gk)
    ga2 = mm_full(gk, fw[...], NT)
    cos2 = jnp.cos(sf[1:2, :] * pre2[...])
    gp2 = ga2 * sf[1:2, :] * cos2
    grad_f2 = jnp.sum(ga2 * pre2[...] * cos2, axis=0, keepdims=True)
    grad_hb = jnp.sum(gp2, axis=0, keepdims=True)
    grad_hw = mm_full(act1[...].T, gp2)
    ga1 = mm_full(gp2, hw[...], NT)
    cos1 = jnp.cos(sf[0:1, :] * pre1[...])
    gp1 = ga1 * sf[0:1, :] * cos1
    grad_f1 = jnp.sum(ga1 * pre1[...] * cos1, axis=0, keepdims=True)
    grad_eb = jnp.sum(gp1, axis=0, keepdims=True)
    sm[...] = jnp.zeros((128, 128), F32)
    sm[0:64, 0:64] = grad_hw
    for k in range(5):
        sm[64 + k : 65 + k, 0:64] = jnp.sum(emb[k] * gp1, axis=0, keepdims=True)
    sm[69:70, 0:64] = grad_eb
    sm[70:71, 0:64] = grad_hb
    sm[71:72, 0:64] = grad_f1
    sm[72:73, 0:64] = grad_f2
    sm[73:74, :] = bias[:, 0:128]
    sm[74:75, :] = bias[:, 128:256]
    ssc[pl.ds(16, 64, stride=18), :] = grad_fw[:, 0:128]
    ssc[pl.ds(16 + 64 * 18, 64, stride=18), :] = grad_fw[:, 128:256]
    ssc[pl.ds(17, 128, stride=18), :] = sm[...]
    slab[...] = ssc[...].astype(BF16)


def mod18(x):
    return x - 18 * jnp.floor((x.astype(F32) + 0.5) / 18.0).astype(jnp.int32)


def sum_kernel(recv, out):
    pick = one_hot(mod18(iota((32, 2304), 1)) == iota((32, 2304), 0))
    total = mm(pick, recv[...]).astype(BF16)
    again = one_hot(mod18(iota((144, 32), 0)) == iota((144, 32), 1))
    block = mm(again, total).astype(BF16)
    for k in range(16):
        out[144 * k : 144 * k + 144, :] = block


def unpack_kernel(recv, giw, gow, gsb, gew, geb, ghw, ghb, gfw, gsf, scr):
    scale = 1.0 / math.sqrt(4 * LENGTH)
    fscale = scale / 4.0
    scr[...] = recv[...].astype(F32)
    for rb in range(2):
        for cb in range(8):
            tile = scr[pl.ds(8 * rb + cb, 128, stride=18), :] * scale
            if cb < 6:
                giw[128 * rb : 128 * rb + 128, 128 * cb : 128 * cb + 128] = tile
            else:
                gow[128 * rb : 128 * rb + 128, 128 * (cb - 6) : 128 * (cb - 6) + 128] = tile
    first = scr[pl.ds(16, 128, stride=18), :] * fscale
    gfw[:, 0:128] = first[0:64, :]
    gfw[:, 128:256] = first[64:128, :]
    second = scr[pl.ds(17, 128, stride=18), :]
    ghw[...] = second[0:64, 0:64] * fscale
    gew[...] = second[64:69, 0:64] * fscale
    geb[...] = second[69:70, 0:64] * fscale
    ghb[...] = second[70:71, 0:64] * fscale
    gsf[...] = second[71:73, 0:64] * fscale
    gsb[:, 0:128] = second[73:74, :] * scale
    gsb[:, 128:256] = second[74:75, :] * scale


def call(kernel, name, out_shape, scratch=(), from_hbm=False):
    def run(*args):
        return pl.pallas_call(
            kernel,
            out_shape=out_shape,
            in_specs=[
                pl.BlockSpec(memory_space=pltpu.HBM if from_hbm else pltpu.VMEM)
                for _ in args
            ],
            scratch_shapes=list(scratch),
            compiler_params=pltpu.CompilerParams(vmem_limit_bytes=48 * 1024 * 1024),
            name=name,
        )(*args)

    return run


def exchange(x, rows):
    y = x.reshape(128, rows // 2, 2, 128)
    y = lax.all_to_all(y, AXES, split_axis=0, concat_axis=0, tiled=True)
    return y.reshape(128 * rows, 128)


def sds(*shape, dtype=F32):
    return jax.ShapeDtypeStruct(shape, dtype)


def shards(
    tokens, out_grad, in_weight, out_weight, skip_bias, embed_weight, embed_bias,
    hidden_weight, hidden_bias, filter_weight, sine_freq, decay_rate,
):
    tok = tokens[0]
    og = out_grad[0]
    decay = decay_rate[None, :]
    square = sds(256, 256, dtype=BF16)
    hidden = sds(64, 64)
    inputs = (tok, og, in_weight, out_weight, embed_weight, embed_bias[None, :], hidden_weight,
              hidden_bias[None, :], filter_weight, sine_freq, decay)
    (slab, go, gi, v, gg, bias, emb, pre1, act1, pre2, act2) = call(
        forward_kernel,
        "forward",
        (sds(1280, 128, dtype=BF16), square, square, square, square, sds(1, 256),
         sds(5, 64, 64), hidden, hidden, hidden, hidden),
        [pltpu.VMEM(x.shape, x.dtype) for x in inputs]
        + [pltpu.VMEM((1280, 128), F32), pltpu.SemaphoreType.DMA((len(inputs),))],
        from_hbm=True,
    )(*inputs)
    recv = exchange(slab, 10)
    sent = call(
        conv_kernel,
        "conv",
        sds(1280, 128, dtype=BF16),
        [
            pltpu.VMEM((1280, 128), F32),
            pltpu.VMEM((1280, 128), F32),
            pltpu.VMEM((2, 264, 256), F32),
            pltpu.VMEM((2, 65 * 128, 128), BF16),
            pltpu.VMEM((288, 128), F32),
            pltpu.VMEM((8, 256, 128), BF16),
            pltpu.VMEM((520, 128), F32),
        ],
    )(recv, skip_bias[None, :])
    recv = exchange(sent, 10)
    gtok, slab = call(
        backward_kernel,
        "backward",
        (square, sds(2304, 128, dtype=BF16)),
        [
            pltpu.VMEM((1280, 128), F32),
            pltpu.VMEM((128, 256), F32),
            pltpu.VMEM((128, 128), F32),
            pltpu.VMEM((2304, 128), F32),
        ],
    )(recv, go, gi, v, gg, tok, og, in_weight, emb, pre1, act1, pre2, act2, bias, hidden_weight,
      filter_weight, sine_freq, decay)
    recv = exchange(slab, 18)
    total = call(sum_kernel, "total", sds(2304, 128, dtype=BF16))(recv)
    recv = exchange(total, 18)
    giw, gow, gsb, gew, geb, ghw, ghb, gfw, gsf = call(
        unpack_kernel,
        "unpack",
        (sds(256, 768), sds(256, 256), sds(1, 256), sds(5, 64), sds(1, 64), sds(64, 64),
         sds(1, 64), sds(64, 256), sds(2, 64)),
        [pltpu.VMEM((2304, 128), F32)],
    )(recv)
    return (gtok[None], giw, gow, gsb[0], gew, geb[0], ghw, ghb[0], gfw, gsf)


def solution(mesh):
    return jax.shard_map(
        shards,
        mesh=mesh,
        in_specs=(P("batch", "seq", None),) * 2 + (P(),) * 10,
        out_specs=(P("batch", "seq", None),) + (P(),) * 9,
        check_vma=False,
    )
```

time: 116 us -> 103 us (0.89)
  blocking collectives: 83.9 us -> 76 us
  Pallas kernels: 24.8 us -> 19.4 us
    all_to_all x4, blocking collectives: 83.9 us -> 76 us  [exchange(): y = lax.all_to_all(y, AXES, split_axis=0, concat_axis=0, tiled=True)]
    pallas_call x5, Pallas kernels: 24.8 us -> 19.4 us  [run(): pl.pallas_call(kernel, out_shape=out_shape, in_specs=[pl.BlockSpec(memory...]
where the time goes in v2:
time: 103 us
  blocking collectives  76 us (74%)
  Pallas kernels  19.4 us (19%)
  local copies, waits for them, and re-layouts  6.7 us (7%)
    all_to_all x4, blocking collectives, exchange(): y = lax.all_to_all(y, AXES, split_axis=0, concat_axis=0, tiled=True)  76 us
    pallas_call x5, Pallas kernels, run(): pl.pallas_call(kernel, out_shape=out_shape, in_specs=[pl.BlockSpec(memory...  19.4 us
    unnamed x34, local copies, waits for them, and re-layouts  6.7 us

profile of v2, /device:TPU:1, one launch (start us, length us, event | category | flops | bytes accessed | tf_op | source)
XLA Modules:
  0.0 102.8 jit_solution(16890539410430989984)
XLA Ops:
  0.6 0.0 copy-start.11
  0.7 0.0 copy-start.13
  0.7 0.0 copy-start.16
  0.7 0.0 copy-start.12
  0.7 0.0 copy-start.15
  0.7 0.6 copy-done.11
  1.3 0.0 copy-done.13
  1.3 0.0 copy-done.16
  1.3 0.0 copy-done.12
  1.4 0.0 copy-done.15
  1.4 0.0 copy-start
  1.4 1.0 copy-done
  2.4 0.0 copy-start.2
  2.4 0.9 copy-done.2
  3.3 0.0 copy-start.4
  3.3 0.9 copy-done.4
  4.2 0.0 copy-start.6
  4.2 0.8 copy-done.6
  5.0 0.0 copy-start.8
  5.0 0.8 copy-done.8
  5.8 0.0 copy-start.10
  5.8 0.9 copy-done.10
  6.7 2.3 %forward.1 = (bf16[1280,128]{1,0:T(8,128)(2,1)S(1)}, bf16[256,256]{1,0:T(8,128)(2,1)S(1)}, bf16[256,256]{1,0:T(8,128)(2,1)S(1)}, bf16[256,256]{1,0:T(8,128)(2,1)...) custom-call(bf16[256,256]{1,0:T(8,128)(2,1)S(1)} %bitcast.25, ...), custom_call_target="tpu_custom_call" | custom-call | tf_op jit(solution)/shard_map/forward/pallas_call | solution.py:367
  9.0 22.9 %all_to_all.20 = bf16[128,5,2,128]{3,2,1,0:T(2,128)(2,1)S(1)} all-to-all(bf16[128,5,2,128]{3,2,1,0:T(2,128)(2,1)S(1)} %bitcast.29), channel_id=1, replica_groups=mesh['seq'=32,'batch'=4] {'seq','batch'}, dimensions={0} | all-to-all | bytes 655360 | tf_op jit(solution)/shard_map/all_to_all | solution.py:384
  31.9 0.0 copy-start.14
  31.9 0.7 copy-done.14
  32.6 0.0 copy-start.7
  32.6 0.0 copy-start.9
  32.6 14.3 %conv.1 = bf16[1280,128]{1,0:T(8,128)(2,1)S(1)} custom-call(bf16[1280,128]{1,0:T(8,128)(2,1)S(1)} %bitcast.21, f32[1,256]{1,0:T(1,128)S(1)} %bitcast.32), custom_call_target="tpu_custom_call" | custom-call | tf_op jit(solution)/shard_map/conv/pallas_call | solution.py:367
  46.8 0.0 copy-start.1
  46.9 0.0 copy-start.3
  46.9 0.0 copy-start.5
  46.9 15.9 %all_to_all.21 = bf16[128,5,2,128]{3,2,1,0:T(2,128)(2,1)S(1)} all-to-all(bf16[128,5,2,128]{3,2,1,0:T(2,128)(2,1)S(1)} %bitcast.22), channel_id=1, replica_groups=mesh['seq'=32,'batch'=4] {'seq','batch'}, dimensions={0} | all-to-all | bytes 655360 | tf_op jit(solution)/shard_map/all_to_all | solution.py:384
  62.8 0.0 copy-done.7
  62.8 0.0 copy-done.9
  62.8 0.0 copy-done.1
  62.8 0.0 copy-done.3
  62.8 0.0 copy-done.5
  62.8 1.3 %backward.1 = (bf16[256,256]{1,0:T(8,128)(2,1)}, bf16[2304,128]{1,0:T(8,128)(2,1)S(1)}) custom-call(bf16[1280,128]{1,0:T(8,128)(2,1)S(1)} %bitcast.23, bf16[256,256]{1,0:T(8,128)(2,1)S(1)} %get-tuple-element.33.go, bf16[256,256]{1,0:T(8,128)(2,1)S(1)} %get-tuple-element.34.gi, bf16[256,256]{1,0:T(8,128)(2,1)S(1)} %get-tuple-element.35.v, ...), custom_call_target="tpu_custom_call" | custom-call | tf_op jit(solution)/shard_map/backward/pallas_call | solution.py:367
  64.1 18.6 %all_to_all.22 = bf16[128,9,2,128]{3,2,1,0:T(2,128)(2,1)S(1)} all-to-all(bf16[128,9,2,128]{3,2,1,0:T(2,128)(2,1)S(1)} %bitcast.24), channel_id=1, replica_groups=mesh['seq'=32,'batch'=4] {'seq','batch'}, dimensions={0} | all-to-all | bytes 1179648 | tf_op jit(solution)/shard_map/all_to_all | solution.py:384
  82.7 0.4 total.1
  83.1 18.6 %all_to_all.23 = bf16[128,9,2,128]{3,2,1,0:T(2,128)(2,1)S(1)} all-to-all(bf16[128,9,2,128]{3,2,1,0:T(2,128)(2,1)S(1)} %bitcast.20), channel_id=1, replica_groups=mesh['seq'=32,'batch'=4] {'seq','batch'}, dimensions={0} | all-to-all | bytes 1179648 | tf_op jit(solution)/shard_map/all_to_all | solution.py:384
  101.7 1.1 %unpack.1 = (f32[256,768]{1,0:T(8,128)}, f32[256,256]{1,0:T(8,128)}, f32[1,256]{1,0:T(1,128)}, f32[5,64]{1,0:T(8,128)}, f32[1,64]{1,0:T(1,128)}, /*index=5*/f32[...) custom-call(bf16[2304,128]{1,0:T(8,128)(2,1)S(1)} %bitcast.18), custom_call_target="tpu_custom_call" | custom-call | tf_op jit(solution)/shard_map/unpack/pallas_call | solution.py:367
Async XLA Ops:
  0.6 0.7 copy-start.11
  0.7 0.7 copy-start.13
  0.7 0.7 copy-start.16
  0.7 0.7 copy-start.12
  0.7 0.7 copy-start.15
  1.4 1.0 copy-start
  2.4 0.9 copy-start.2
  3.3 0.9 copy-start.4
  4.2 0.8 copy-start.6
  5.0 0.8 copy-start.8
  5.8 0.9 copy-start.10
  31.9 0.7 copy-start.14
  32.6 30.2 %copy-start.7 = (f32[64,256]{1,0:T(8,128)S(1)}, f32[64,256]{1,0:T(8,128)}, u32[]{:S(2)}) copy-start(f32[64,256]{1,0:T(8,128)} %fw.1) | copy-start | bytes 196612
  32.6 30.2 %copy-start.9 = (f32[64,64]{1,0:T(8,128)S(1)}, f32[64,64]{1,0:T(8,128)}, u32[]{:S(2)}) copy-start(f32[64,64]{1,0:T(8,128)} %hw.1) | copy-start | bytes 49156
  46.8 15.9 %copy-start.1 = (bf16[256,768]{1,0:T(8,128)(2,1)S(1)}, bf16[256,768]{1,0:T(8,128)(2,1)}, u32[]{:S(2)}) copy-start(bf16[256,768]{1,0:T(8,128)(2,1)} %wi.1) | copy-start | bytes 1179652
  46.9 15.9 %copy-start.3 = (bf16[1,256,256]{2,1,0:T(8,128)(2,1)S(1)}, bf16[1,256,256]{2,1,0:T(8,128)(2,1)}, u32[]{:S(2)}) copy-start(bf16[1,256,256]{2,1,0:T(8,128)(2,1)} %param.12) | copy-start | bytes 393220
  46.9 15.9 %copy-start.5 = (bf16[1,256,256]{2,1,0:T(8,128)(2,1)S(1)}, bf16[1,256,256]{2,1,0:T(8,128)(2,1)}, u32[]{:S(2)}) copy-start(bf16[1,256,256]{2,1,0:T(8,128)(2,1)} %param.13) | copy-start | bytes 393220

commit v3 on v2

--- a/solution.py
+++ b/solution.py
@@ -43,13 +43,13 @@
 
 
 def forward_kernel(
-    tok_h, og_h, wi_h, wo_h, ew_h, eb_h, hw_h, hb_h, fw_h, sf_h, dr_h,
-    slab, go_o, gi_o, v_o, gg_o, bias_o, emb_o, pre1_o, act1_o, pre2_o, act2_o,
-    tok, og, wi, wo, ew, eb, hw, hb, fw, sf, dr, scr, sems,
+    tok_h, og_h, wi_h, wo_h, ew_h, eb_h, hw_h, hb_h, fw_h, sf_h, dr_h, sk_h,
+    slab, go_o, gi_o, v_o, gg_o, bias_o, emb_o, pre1_o, act1_o, pre2_o, act2_o, sk_o,
+    tok, og, wi, wo, ew, eb, hw, hb, fw, sf, dr, sk, scr, sems,
 ):
     pairs = (
         (tok_h, tok), (wi_h, wi), (og_h, og), (wo_h, wo), (sf_h, sf), (ew_h, ew), (eb_h, eb),
-        (hw_h, hw), (hb_h, hb), (fw_h, fw), (dr_h, dr),
+        (hw_h, hw), (hb_h, hb), (fw_h, fw), (dr_h, dr), (sk_h, sk),
     )
     copies = [pltpu.make_async_copy(a, b, sems.at[k]) for k, (a, b) in enumerate(pairs)]
     for c in copies:
@@ -74,6 +74,7 @@
     gg_o[...] = gg
     mixed = (v.astype(F32) * gi.astype(F32)).astype(BF16).astype(F32)
     gc = (gg.astype(F32) * go.astype(F32)).astype(BF16).astype(F32)
+    sk_o[...] = sk[...]
     bias_o[...] = jnp.sum(gc * mixed, axis=0, keepdims=True)
     mixed_t = mixed.T
     gc_t = gc.T
@@ -102,9 +103,9 @@
     slab[...] = scr[...].astype(BF16)
 
 
-def row_rolls(x):
+def row_rolls(x, bits):
     row = iota(x.shape, 0)
-    for bit in range(3):
+    for bit in range(bits):
         x = jnp.where((row >> bit) & 1 == 1, pltpu.roll(x, 1 << bit, 1), x)
     return x
 
@@ -123,59 +124,105 @@
     perm = one_hot(source(row) == col)
     back = one_hot(source(col) == row)
     gather = [
-        one_hot(iota((256, 128), 1) >> 1 == 2 * (iota((256, 128), 0) >> 3) + h) for h in range(2)
+        one_hot(iota((512, 128), 1) >> 1 == 2 * (iota((512, 128), 0) >> 4) + h) for h in range(2)
     ]
     spread_g = one_hot(iota((128, 64), 0) >> 1 == iota((128, 64), 1))
     lane, sub = iota((8, 128), 1), iota((8, 128), 0)
-    ready = lane >= sub
+    lane16, sub16 = iota((16, 128), 1), iota((16, 128), 0)
 
     def line(r):
         return scr[pl.ds(r, 128, stride=10), :]
 
+    mixed_up, shifted, x_revs = [], [], []
     for ch in range(2):
         f_in = line(8 + ch).astype(BF16)
-        fscr[ch, 0:8, :] = jnp.zeros((8, 256), F32)
+        fscr[ch, 0:16, :] = jnp.zeros((16, 256), BF16)
         for h in range(2):
-            fscr[ch, 8:264, 128 * h : 128 * h + 128] = row_rolls(mm(gather[h], f_in))
+            fscr[ch, 16:528, 128 * h : 128 * h + 128] = row_rolls(mm(gather[h], f_in), 4).astype(BF16)
         ubuf[ch, 0:128, :] = jnp.zeros((128, 128), BF16)
-
-    def toeplitz_step(n, carry):
-        for ch in range(2):
-            at = pl.multiple_of(8 * n, 8)
-            before = fscr[ch, pl.ds(at, 8), 128:256]
-            now = fscr[ch, pl.ds(pl.multiple_of(at + 8, 8), 8), :]
-            for odd in range(2):
-                last = before if odd == 0 else now[:, 0:128]
-                this = now[:, 128 * odd : 128 * odd + 128]
-                fresh = jnp.where(ready, this, last)
-                tiles = [fresh]
-                for g in range(1, 16):
-                    picked = jnp.where(lane < 128 - 8 * g, fresh, last)
-                    tiles.append(pltpu.roll(picked, 8 * g, 1))
-                to = pl.multiple_of(256 * n + 128 * (odd + 1), 128)
-                ubuf[ch, pl.ds(to, 128), :] = jnp.concatenate(tiles, axis=0).astype(BF16)
-        return carry
-
-    lax.fori_loop(0, 32, toeplitz_step, 0)
-
     for ch in range(2):
         xs = [line(2 * ch + h) for h in range(2)]
         gs_in = [line(4 + 2 * ch + h) for h in range(2)]
         x2 = jnp.concatenate(xs, axis=1).astype(BF16)
         g2 = jnp.concatenate(gs_in, axis=1).astype(BF16)
         g_rev = mm(g2, rev256).astype(BF16)
-        mixed_up = mm(perm, jnp.concatenate([x2, g_rev], axis=0))
-        shifted = (
-            mixed_up.astype(BF16),
-            jnp.concatenate([jnp.zeros((8, 256), F32), mixed_up[0:248, :]], axis=0).astype(BF16),
+        up = mm(perm, jnp.concatenate([x2, g_rev], axis=0))
+        mixed_up.append(up)
+        shifted.append(
+            (
+                up.astype(BF16),
+                jnp.concatenate([jnp.zeros((8, 256), F32), up[0:248, :]], axis=0).astype(BF16),
+            )
         )
+        x_revs.append(
+            jnp.concatenate([mm(rev128, x.astype(BF16), NT).astype(BF16) for x in xs], axis=1)
+        )
+        for h in range(2):
+            at = 2 * ch + h
+            gpad[at, 0:128, :] = gs_in[h]
+            gpad[at, 128:288, :] = jnp.zeros((160, 128), F32)
+            for s in range(4):
+                gs[4 * at + s] = gpad[at, 4 * s : 4 * s + 256, :].astype(BF16)
+
+    def diagonals(c_last, c):
+        part = None
+        for g in range(16):
+            old = c_last[8 * g : 8 * g + 8, :]
+            new = jnp.zeros((8, 128), F32) if c is None else c[8 * g : 8 * g + 8, :]
+            now = pltpu.roll(jnp.where(lane + sub >= 127 - 8 * g, old, new), 8 * g + 1, 1)
+            part = now if part is None else part + now
+        return part
+
+    def step(q, carry):
+        ends = []
+        for ch in range(2):
+            for k in range(4):
+                at = pl.multiple_of(64 * q + 16 * k, 16)
+                before = fscr[ch, pl.ds(at, 16), 128:256]
+                now = fscr[ch, pl.ds(pl.multiple_of(at + 16, 16), 16), :]
+                for odd in range(2):
+                    last = before if odd == 0 else now[:, 0:128]
+                    this = now[:, 128 * odd : 128 * odd + 128]
+                    fresh = jnp.where(lane16 >= sub16, this, last)
+                    tiles = [fresh]
+                    for g in range(1, 8):
+                        picked = jnp.where(lane16 < 128 - 16 * g, fresh, last)
+                        tiles.append(pltpu.roll(picked, 16 * g, 1))
+                    to = pl.multiple_of(1024 * q + 256 * k + 128 * (odd + 1), 128)
+                    ubuf[ch, pl.ds(to, 128), :] = jnp.concatenate(tiles, axis=0)
+            c_last = carry[ch]
+            for s in range(4):
+                at = pl.multiple_of(16 * q, 16)
+                at_next = pl.multiple_of(16 * q + 16 * (s // 3), 16)
+                g0 = gs[8 * ch + s, pl.ds(at, 128), :]
+                g1 = gs[8 * ch + 4 + s, pl.ds(at, 128), :]
+                g0_next = gs[8 * ch + (s + 1) % 4, pl.ds(at_next, 128), :]
+                right = jnp.concatenate(
+                    [
+                        jnp.concatenate([g0, g1], axis=1),
+                        jnp.concatenate([g1, g0_next], axis=1),
+                    ],
+                    axis=0,
+                )
+                both = mm(x_revs[ch], right)
+                for odd in range(2):
+                    c = both[:, 128 * odd : 128 * odd + 128]
+                    to = pl.multiple_of(64 * q + 8 * (2 * s + odd), 8)
+                    gsc[ch, pl.ds(to, 8), :] = diagonals(c_last, c)
+                    c_last = c
+            ends.append(c_last)
+        return tuple(ends)
+
+    ends = lax.fori_loop(0, 8, step, (jnp.zeros((128, 128), F32),) * 2)
+
+    for ch in range(2):
         total = None
         for q in range(4):
             low = 64 * q
             left, right = [], []
             for k in range(8 * q, 8 * q + 8):
                 down = 16 * (k // 2)
-                piece = shifted[k % 2]
+                piece = shifted[ch][k % 2]
                 if down <= low:
                     left.append(piece[low - down : 256 - down, :])
                 else:
@@ -194,60 +241,15 @@
                 total = jnp.concatenate([total[0:low, :], total[low:, :] + part], axis=0)
         mine = iota((1, 256), 1) == own + 128 * ch
         skip_now = jnp.sum(jnp.where(mine, skip[...], 0.0), axis=1, keepdims=True)
-        done = (total + skip_now * mixed_up).astype(BF16)
+        done = (total + skip_now * mixed_up[ch]).astype(BF16)
         apart = mm(back, done)
         conv2 = apart[0:128, :]
         gm2 = mm(apart[128:256, :].astype(BF16), rev256)
         for h in range(2):
             osc[pl.ds(2 * ch + h, 128, stride=10), :] = conv2[:, 128 * h : 128 * h + 128]
             osc[pl.ds(4 + 2 * ch + h, 128, stride=10), :] = gm2[:, 128 * h : 128 * h + 128]
-
-        x_rev = jnp.concatenate(
-            [mm(rev128, x.astype(BF16), NT).astype(BF16) for x in xs], axis=1
-        )
-        for h in range(2):
-            gpad[0:128, :] = gs_in[h]
-            gpad[128:288, :] = jnp.zeros((160, 128), F32)
-            for s in range(4):
-                gs[4 * h + s] = gpad[4 * s : 4 * s + 256, :].astype(BF16)
-
-        def corr_step(q, c_last):
-            for s in range(4):
-                at = pl.multiple_of(16 * q, 16)
-                at_next = pl.multiple_of(16 * q + 16 * (s // 3), 16)
-                g0 = gs[s, pl.ds(at, 128), :]
-                g1 = gs[4 + s, pl.ds(at, 128), :]
-                g0_next = gs[(s + 1) % 4, pl.ds(at_next, 128), :]
-                right = jnp.concatenate(
-                    [
-                        jnp.concatenate([g0, g1], axis=1),
-                        jnp.concatenate([g1, g0_next], axis=1),
-                    ],
-                    axis=0,
-                )
-                both = mm(x_rev, right)
-                for odd in range(2):
-                    c = both[:, 128 * odd : 128 * odd + 128]
-                    part = diagonals(c_last, c)
-                    gsc[pl.ds(pl.multiple_of(64 * q + 8 * (2 * s + odd), 8), 8), :] = part
-                    c_last = c
-            return c_last
-
-        def diagonals(c_last, c):
-            part = None
-            for g in range(16):
-                old = c_last[8 * g : 8 * g + 8, :]
-                if c is None:
-                    new = jnp.zeros((8, 128), F32)
-                else:
-                    new = c[8 * g : 8 * g + 8, :]
-                now = pltpu.roll(jnp.where(lane + sub >= 127 - 8 * g, old, new), 8 * g + 1, 1)
-                part = now if part is None else part + now
-            return part
-
-        c_end = lax.fori_loop(0, 8, corr_step, jnp.zeros((128, 128), F32))
-        gsc[512:520, :] = diagonals(c_end, None)
-        gf = row_rolls(gsc[8:520, :]).reshape(64, 8, 128).sum(axis=1)
+        gsc[ch, 512:520, :] = diagonals(ends[ch], None)
+        gf = row_rolls(gsc[ch, 8:520, :], 3).reshape(64, 8, 128).sum(axis=1)
         osc[pl.ds(8 + ch, 128, stride=10), :] = mm(spread_g, gf.astype(BF16))
     out[...] = osc[...].astype(BF16)
 
@@ -399,16 +401,16 @@
     square = sds(256, 256, dtype=BF16)
     hidden = sds(64, 64)
     inputs = (tok, og, in_weight, out_weight, embed_weight, embed_bias[None, :], hidden_weight,
-              hidden_bias[None, :], filter_weight, sine_freq, decay)
-    (slab, go, gi, v, gg, bias, emb, pre1, act1, pre2, act2) = call(
+              hidden_bias[None, :], filter_weight, sine_freq, decay, skip_bias[None, :])
+    (slab, go, gi, v, gg, bias, emb, pre1, act1, pre2, act2, skip) = call(
         forward_kernel,
         "forward",
         (sds(1280, 128, dtype=BF16), square, square, square, square, sds(1, 256),
-         sds(5, 64, 64), hidden, hidden, hidden, hidden),
+         sds(5, 64, 64), hidden, hidden, hidden, hidden, sds(1, 256)),
         [pltpu.VMEM(x.shape, x.dtype) for x in inputs]
         + [pltpu.VMEM((1280, 128), F32), pltpu.SemaphoreType.DMA((len(inputs),))],
         from_hbm=True,
-    )(*inputs)
+    )(*(pltpu.with_memory_space_constraint(x, pltpu.HBM) for x in inputs))
     recv = exchange(slab, 10)
     sent = call(
         conv_kernel,
@@ -417,13 +419,13 @@
         [
             pltpu.VMEM((1280, 128), F32),
             pltpu.VMEM((1280, 128), F32),
-            pltpu.VMEM((2, 264, 256), F32),
+            pltpu.VMEM((2, 528, 256), BF16),
             pltpu.VMEM((2, 65 * 128, 128), BF16),
-            pltpu.VMEM((288, 128), F32),
-            pltpu.VMEM((8, 256, 128), BF16),
-            pltpu.VMEM((520, 128), F32),
+            pltpu.VMEM((4, 288, 128), F32),
+            pltpu.VMEM((16, 256, 128), BF16),
+            pltpu.VMEM((2, 520, 128), F32),
         ],
-    )(recv, skip_bias[None, :])
+    )(recv, skip)
     recv = exchange(sent, 10)
     gtok, slab = call(
         backward_kernel,

time: 103 us -> 92.4 us (0.90)
  local copies, waits for them, and re-layouts: 6.7 us -> 0.67 us
  Pallas kernels: 19.4 us -> 14.7 us
    unnamed x34 -> x14, local copies, waits for them, and re-layouts: 6.7 us -> 0.67 us
    pallas_call x5, Pallas kernels: 19.4 us -> 14.7 us  [run(): pl.pallas_call(kernel, out_shape=out_shape, in_specs=[pl.BlockSpec(memory...]
where the time goes in v3:
time: 92.4 us; the launch traced here: 92.1 us
  blocking collectives  76 us (82%)
  Pallas kernels  14.7 us (16%)
    all_to_all x4, blocking collectives, exchange(): y = lax.all_to_all(y, AXES, split_axis=0, concat_axis=0, tiled=True)  76 us
    pallas_call x5, Pallas kernels, run(): pl.pallas_call(kernel, out_shape=out_shape, in_specs=[pl.BlockSpec(memory...  14.7 us

profile of v3, /device:TPU:1, one launch (start us, length us, event | category | flops | bytes accessed | tf_op | source)
XLA Modules:
  0.0 92.1 jit_solution(3090461888135201215)
XLA Ops:
  0.6 2.3 %forward.1 = (bf16[1280,128]{1,0:T(8,128)(2,1)S(1)}, bf16[256,256]{1,0:T(8,128)(2,1)S(1)}, bf16[256,256]{1,0:T(8,128)(2,1)S(1)}, bf16[256,256]{1,0:T(8,128)(2,1)...) custom-call(bf16[256,256]{1,0:T(8,128)(2,1)} %bitcast.25, ...), custom_call_target="tpu_custom_call" | custom-call | tf_op jit(solution)/shard_map/forward/pallas_call | solution.py:369
  2.9 22.9 %all_to_all.20 = bf16[128,5,2,128]{3,2,1,0:T(2,128)(2,1)S(1)} all-to-all(bf16[128,5,2,128]{3,2,1,0:T(2,128)(2,1)S(1)} %bitcast.29), channel_id=1, replica_groups=mesh['seq'=32,'batch'=4] {'seq','batch'}, dimensions={0} | all-to-all | bytes 655360 | tf_op jit(solution)/shard_map/all_to_all | solution.py:386
  25.9 0.0 copy-start.3
  25.9 0.0 copy-start.4
  25.9 9.6 %conv.1 = bf16[1280,128]{1,0:T(8,128)(2,1)S(1)} custom-call(bf16[1280,128]{1,0:T(8,128)(2,1)S(1)} %bitcast.21, f32[1,256]{1,0:T(1,128)S(1)} %get-tuple-element.34.skip), custom_call_target="tpu_custom_call" | custom-call | tf_op jit(solution)/shard_map/conv/pallas_call | solution.py:369
  35.5 0.0 copy-start
  35.5 0.0 copy-start.1
  35.5 0.0 copy-start.2
  35.5 0.0 copy-start.6
  35.5 15.9 %all_to_all.21 = bf16[128,5,2,128]{3,2,1,0:T(2,128)(2,1)S(1)} all-to-all(bf16[128,5,2,128]{3,2,1,0:T(2,128)(2,1)S(1)} %bitcast.22), channel_id=1, replica_groups=mesh['seq'=32,'batch'=4] {'seq','batch'}, dimensions={0} | all-to-all | bytes 655360 | tf_op jit(solution)/shard_map/all_to_all | solution.py:386
  51.4 0.0 copy-start.5
  51.4 0.0 copy-done.3
  51.4 0.0 copy-done.4
  51.4 0.0 copy-done
  51.4 0.0 copy-done.1
  51.5 0.0 copy-done.2
  51.5 0.0 copy-done.6
  51.5 0.6 copy-done.5
  52.1 1.3 %backward.1 = (bf16[256,256]{1,0:T(8,128)(2,1)}, bf16[2304,128]{1,0:T(8,128)(2,1)S(1)}) custom-call(bf16[1280,128]{1,0:T(8,128)(2,1)S(1)} %bitcast.23, bf16[256,256]{1,0:T(8,128)(2,1)S(1)} %get-tuple-element.35.go, bf16[256,256]{1,0:T(8,128)(2,1)S(1)} %get-tuple-element.36.gi, bf16[256,256]{1,0:T(8,128)(2,1)S(1)} %get-tuple-element.37.v, ...), custom_call_target="tpu_custom_call" | custom-call | tf_op jit(solution)/shard_map/backward/pallas_call | solution.py:369
  53.4 18.6 %all_to_all.22 = bf16[128,9,2,128]{3,2,1,0:T(2,128)(2,1)S(1)} all-to-all(bf16[128,9,2,128]{3,2,1,0:T(2,128)(2,1)S(1)} %bitcast.24), channel_id=1, replica_groups=mesh['seq'=32,'batch'=4] {'seq','batch'}, dimensions={0} | all-to-all | bytes 1179648 | tf_op jit(solution)/shard_map/all_to_all | solution.py:386
  72.0 0.4 total.1
  72.4 18.6 %all_to_all.23 = bf16[128,9,2,128]{3,2,1,0:T(2,128)(2,1)S(1)} all-to-all(bf16[128,9,2,128]{3,2,1,0:T(2,128)(2,1)S(1)} %bitcast.20), channel_id=1, replica_groups=mesh['seq'=32,'batch'=4] {'seq','batch'}, dimensions={0} | all-to-all | bytes 1179648 | tf_op jit(solution)/shard_map/all_to_all | solution.py:386
  91.0 1.1 %unpack.1 = (f32[256,768]{1,0:T(8,128)}, f32[256,256]{1,0:T(8,128)}, f32[1,256]{1,0:T(1,128)}, f32[5,64]{1,0:T(8,128)}, f32[1,64]{1,0:T(1,128)}, /*index=5*/f32[...) custom-call(bf16[2304,128]{1,0:T(8,128)(2,1)S(1)} %bitcast.18), custom_call_target="tpu_custom_call" | custom-call | tf_op jit(solution)/shard_map/unpack/pallas_call | solution.py:369
Async XLA Ops:
  25.9 25.6 %copy-start.3 = (f32[64,256]{1,0:T(8,128)S(1)}, f32[64,256]{1,0:T(8,128)}, u32[]{:S(2)}) copy-start(f32[64,256]{1,0:T(8,128)} %fw.1) | copy-start | bytes 196612
  25.9 25.6 %copy-start.4 = (f32[64,64]{1,0:T(8,128)S(1)}, f32[64,64]{1,0:T(8,128)}, u32[]{:S(2)}) copy-start(f32[64,64]{1,0:T(8,128)} %hw.1) | copy-start | bytes 49156
  35.5 16.0 %copy-start = (bf16[256,768]{1,0:T(8,128)(2,1)S(1)}, bf16[256,768]{1,0:T(8,128)(2,1)}, u32[]{:S(2)}) copy-start(bf16[256,768]{1,0:T(8,128)(2,1)} %wi.1) | copy-start | bytes 1179652
  35.5 16.0 %copy-start.1 = (bf16[1,256,256]{2,1,0:T(8,128)(2,1)S(1)}, bf16[1,256,256]{2,1,0:T(8,128)(2,1)}, u32[]{:S(2)}) copy-start(bf16[1,256,256]{2,1,0:T(8,128)(2,1)} %param.12) | copy-start | bytes 393220
  35.5 15.9 %copy-start.2 = (bf16[1,256,256]{2,1,0:T(8,128)(2,1)S(1)}, bf16[1,256,256]{2,1,0:T(8,128)(2,1)}, u32[]{:S(2)}) copy-start(bf16[1,256,256]{2,1,0:T(8,128)(2,1)} %param.13) | copy-start | bytes 393220
  35.5 15.9 %copy-start.6 = (f32[256]{0:T(256)S(1)}, f32[256]{0:T(256)}, u32[]{:S(2)}) copy-start(f32[256]{0:T(256)} %param.23) | copy-start | bytes 3076
  51.4 0.7 copy-start.5

commit v4 on v3

--- a/solution.py
+++ b/solution.py
@@ -44,7 +44,8 @@
 
 def forward_kernel(
     tok_h, og_h, wi_h, wo_h, ew_h, eb_h, hw_h, hb_h, fw_h, sf_h, dr_h, sk_h,
-    slab, go_o, gi_o, v_o, gg_o, bias_o, emb_o, pre1_o, act1_o, pre2_o, act2_o, sk_o,
+    slab, go_o, gi_o, v_o, gg_o, bias_o, emb_o, pre1_o, act1_o, pre2_o, act2_o,
+    sk_o, mod_o, hw_o, fw_o, sf_o,
     tok, og, wi, wo, ew, eb, hw, hb, fw, sf, dr, sk, scr, sems,
 ):
     pairs = (
@@ -75,6 +76,9 @@
     mixed = (v.astype(F32) * gi.astype(F32)).astype(BF16).astype(F32)
     gc = (gg.astype(F32) * go.astype(F32)).astype(BF16).astype(F32)
     sk_o[...] = sk[...]
+    hw_o[...] = hw[...]
+    fw_o[...] = fw[...]
+    sf_o[...] = sf[...]
     bias_o[...] = jnp.sum(gc * mixed, axis=0, keepdims=True)
     mixed_t = mixed.T
     gc_t = gc.T
@@ -89,7 +93,9 @@
     act1_o[...] = act1
     pre2_o[...] = pre2
     act2_o[...] = act2
-    filt = mm_full(act2, fw[...]) * modulation(dr[...], first, (64, 256))
+    modul = modulation(dr[...], first, (64, 256))
+    mod_o[...] = modul
+    filt = mm_full(act2, fw[...]) * modul
     side = 64 * (lax.axis_index("batch") % 2)
     place = one_hot(iota((64, 128), 1) == iota((64, 128), 0) + side)
     filt_t = mm(filt.T.astype(BF16), place)
@@ -255,11 +261,10 @@
 
 
 def backward_kernel(
-    recv, go, gi, v, gg, tok, og, wi, emb, pre1, act1, pre2, act2, bias, hw, fw, sf, dr,
-    gtok, slab, scr, tmp, sm, ssc,
+    recv, go, gi, v, gg, tok, og, wi, emb, pre1, act1, pre2, act2, bias, modul, hw, fw, sf,
+    gtok, kept, given, scr, tmp, sm, ssc,
 ):
     own = own_index()
-    first = own * 64
     scr[...] = recv[...].astype(F32)
 
     def line(r):
@@ -298,7 +303,7 @@
 
     tmp[...] = jnp.concatenate([line(8), line(9)], axis=0).T
     gf = tmp[pl.ds(pl.multiple_of((own % 2) * 64, 64), 64), :]
-    gk = gf * modulation(dr[...], first, (64, 256))
+    gk = gf * modul[...]
     grad_fw = mm_full(act2[...].T, gk)
     ga2 = mm_full(gk, fw[...], NT)
     cos2 = jnp.cos(sf[1:2, :] * pre2[...])
@@ -324,7 +329,13 @@
     ssc[pl.ds(16, 64, stride=18), :] = grad_fw[:, 0:128]
     ssc[pl.ds(16 + 64 * 18, 64, stride=18), :] = grad_fw[:, 128:256]
     ssc[pl.ds(17, 128, stride=18), :] = sm[...]
-    slab[...] = ssc[...].astype(BF16)
+    core = own % 2
+    kept[...] = ssc[pl.ds(pl.multiple_of(core * 1152, 1152), 1152), :]
+    given[...] = ssc[pl.ds(pl.multiple_of((1 - core) * 1152, 1152), 1152), :].astype(BF16)
+
+
+def pair_kernel(kept, taken, out):
+    out[...] = (kept[...] + taken[...].astype(F32)).astype(BF16)
 
 
 def mod18(x):
@@ -332,29 +343,34 @@
 
 
 def sum_kernel(recv, out):
-    pick = one_hot(mod18(iota((32, 2304), 1)) == iota((32, 2304), 0))
+    pick = one_hot(mod18(iota((32, 1152), 1)) == iota((32, 1152), 0))
     total = mm(pick, recv[...]).astype(BF16)
     again = one_hot(mod18(iota((144, 32), 0)) == iota((144, 32), 1))
     block = mm(again, total).astype(BF16)
-    for k in range(16):
+    for k in range(8):
         out[144 * k : 144 * k + 144, :] = block
 
 
-def unpack_kernel(recv, giw, gow, gsb, gew, geb, ghw, ghb, gfw, gsf, scr):
+def unpack_kernel(own_core, other, giw, gow, gsb, gew, geb, ghw, ghb, gfw, gsf, scr, small):
     scale = 1.0 / math.sqrt(4 * LENGTH)
     fscale = scale / 4.0
-    scr[...] = recv[...].astype(F32)
-    for rb in range(2):
-        for cb in range(8):
-            tile = scr[pl.ds(8 * rb + cb, 128, stride=18), :] * scale
-            if cb < 6:
-                giw[128 * rb : 128 * rb + 128, 128 * cb : 128 * cb + 128] = tile
-            else:
-                gow[128 * rb : 128 * rb + 128, 128 * (cb - 6) : 128 * (cb - 6) + 128] = tile
-    first = scr[pl.ds(16, 128, stride=18), :] * fscale
-    gfw[:, 0:128] = first[0:64, :]
-    gfw[:, 128:256] = first[64:128, :]
-    second = scr[pl.ds(17, 128, stride=18), :]
+    core = own_index() % 2
+    for k, recv in enumerate((own_core, other)):
+        scr[k] = recv[...].astype(F32)
+        first = pl.multiple_of(64 * (core if k == 0 else 1 - core), 64)
+        for rb in range(2):
+            for cb in range(8):
+                tile = scr[k, pl.ds(8 * rb + cb, 64, stride=18), :] * scale
+                rows = pl.ds(128 * rb + first, 64)
+                if cb < 6:
+                    giw[rows, 128 * cb : 128 * cb + 128] = tile
+                else:
+                    gow[rows, 128 * (cb - 6) : 128 * (cb - 6) + 128] = tile
+        for n in range(2):
+            small[n, pl.ds(first, 64), :] = scr[k, pl.ds(16 + n, 64, stride=18), :]
+    gfw[:, 0:128] = small[0, 0:64, :] * fscale
+    gfw[:, 128:256] = small[0, 64:128, :] * fscale
+    second = small[1]
     ghw[...] = second[0:64, 0:64] * fscale
     gew[...] = second[64:69, 0:64] * fscale
     geb[...] = second[69:70, 0:64] * fscale
@@ -381,10 +397,17 @@
     return run
 
 
-def exchange(x, rows):
-    y = x.reshape(128, rows // 2, 2, 128)
-    y = lax.all_to_all(y, AXES, split_axis=0, concat_axis=0, tiled=True)
-    return y.reshape(128 * rows, 128)
+def exchange(x, rows, groups=None):
+    count = x.shape[0] // rows
+    y = x.reshape(count, rows // 2, 2, 128)
+    y = lax.all_to_all(
+        y, AXES, split_axis=0, concat_axis=0, axis_index_groups=groups, tiled=True
+    )
+    return y.reshape(count * rows, 128)
+
+
+def swap_cores(x):
+    return lax.ppermute(x, "batch", [(k, k ^ 1) for k in range(4)])
 
 
 def sds(*shape, dtype=F32):
@@ -402,11 +425,13 @@
     hidden = sds(64, 64)
     inputs = (tok, og, in_weight, out_weight, embed_weight, embed_bias[None, :], hidden_weight,
               hidden_bias[None, :], filter_weight, sine_freq, decay, skip_bias[None, :])
-    (slab, go, gi, v, gg, bias, emb, pre1, act1, pre2, act2, skip) = call(
+    (slab, go, gi, v, gg, bias, emb, pre1, act1, pre2, act2,
+     skip, modul, hw, fw, sf) = call(
         forward_kernel,
         "forward",
         (sds(1280, 128, dtype=BF16), square, square, square, square, sds(1, 256),
-         sds(5, 64, 64), hidden, hidden, hidden, hidden, sds(1, 256)),
+         sds(5, 64, 64), hidden, hidden, hidden, hidden, sds(1, 256),
+         sds(64, 256), hidden, sds(64, 256), sds(2, 64)),
         [pltpu.VMEM(x.shape, x.dtype) for x in inputs]
         + [pltpu.VMEM((1280, 128), F32), pltpu.SemaphoreType.DMA((len(inputs),))],
         from_hbm=True,
@@ -427,28 +452,30 @@
         ],
     )(recv, skip)
     recv = exchange(sent, 10)
-    gtok, slab = call(
+    gtok, kept, given = call(
         backward_kernel,
         "backward",
-        (square, sds(2304, 128, dtype=BF16)),
+        (square, sds(1152, 128), sds(1152, 128, dtype=BF16)),
         [
             pltpu.VMEM((1280, 128), F32),
             pltpu.VMEM((128, 256), F32),
             pltpu.VMEM((128, 128), F32),
             pltpu.VMEM((2304, 128), F32),
         ],
-    )(recv, go, gi, v, gg, tok, og, in_weight, emb, pre1, act1, pre2, act2, bias, hidden_weight,
-      filter_weight, sine_freq, decay)
-    recv = exchange(slab, 18)
-    total = call(sum_kernel, "total", sds(2304, 128, dtype=BF16))(recv)
-    recv = exchange(total, 18)
+    )(recv, go, gi, v, gg, tok, og, in_weight, emb, pre1, act1, pre2, act2, bias, modul, hw, fw, sf)
+    half = sds(1152, 128, dtype=BF16)
+    slab = call(pair_kernel, "pair", half)(kept, swap_cores(given))
+    by_core = [list(range(core, 128, 2)) for core in range(2)]
+    recv = exchange(slab, 18, by_core)
+    total = call(sum_kernel, "total", half)(recv)
+    recv = exchange(total, 18, by_core)
     giw, gow, gsb, gew, geb, ghw, ghb, gfw, gsf = call(
         unpack_kernel,
         "unpack",
         (sds(256, 768), sds(256, 256), sds(1, 256), sds(5, 64), sds(1, 64), sds(64, 64),
          sds(1, 64), sds(64, 256), sds(2, 64)),
-        [pltpu.VMEM((2304, 128), F32)],
-    )(recv)
+        [pltpu.VMEM((2, 1152, 128), F32), pltpu.VMEM((2, 128, 128), F32)],
+    )(recv, swap_cores(recv))
     return (gtok[None], giw, gow, gsb[0], gew, geb[0], ghw, ghb[0], gfw, gsf)
 
 

time: 92.4 us -> 89.2 us (0.965)
  blocking collectives: 76 us -> 67.2 us
  starting transfers between devices: 0 us -> 3.78 us
  waiting for transfers between devices: 0 us -> 2.42 us
    all_to_all x4, blocking collectives: 76 us -> 67.2 us  [exchange(): lax.all_to_all(y, AXES, split_axis=0, concat_axis=0, axis_index_groups=gr...]
    ppermute x0 -> x2, starting transfers between devices: none -> 3.78 us  [swap_cores(): return lax.ppermute(x, 'batch', [(k, k ^ 1) for k in range(4)])]
    ppermute x0 -> x2, waiting for transfers between devices: none -> 2.42 us  [swap_cores(): return lax.ppermute(x, 'batch', [(k, k ^ 1) for k in range(4)])]
    pallas_call x5 -> x6, Pallas kernels: 14.7 us -> 14.8 us  [run(): pl.pallas_call(kernel, out_shape=out_shape, in_specs=[pl.BlockSpec(memory...]
  transfers between devices with their start and end apart: 0 -> 2, of which waited for: 0 -> 2; matrix products, arithmetic and copies ran while one was open for 0% -> 0% of each run, Pallas kernels for 0% -> 0%
where the time goes in v4:
time: 89.2 us; the launch traced here: 88.9 us
  blocking collectives  67.2 us (75%)
  Pallas kernels  14.8 us (17%)
  starting transfers between devices  3.78 us (4%)
  waiting for transfers between devices  2.42 us (3%)
    all_to_all x4, blocking collectives, exchange(): lax.all_to_all(y, AXES, split_axis=0, concat_axis=0, axis_index_groups=gr...  67.2 us
    pallas_call x6, Pallas kernels, run(): pl.pallas_call(kernel, out_shape=out_shape, in_specs=[pl.BlockSpec(memory...  14.8 us
    ppermute x2, starting transfers between devices, swap_cores(): return lax.ppermute(x, 'batch', [(k, k ^ 1) for k in range(4)])  3.78 us
    ppermute x2, waiting for transfers between devices, swap_cores(): return lax.ppermute(x, 'batch', [(k, k ^ 1) for k in range(4)])  2.42 us
  transfers between devices with their start and end apart: 2, of which 2 were waited for; matrix products, arithmetic and copies ran while one was open for 0% of the time, Pallas kernels for 0%

profile of v4, /device:TPU:1, one launch (start us, length us, event | category | flops | bytes accessed | tf_op | source)
XLA Modules:
  0.0 88.9 jit_solution(13576101336824725170)
XLA Ops:
  0.6 2.3 %forward.1 = (bf16[1280,128]{1,0:T(8,128)(2,1)S(1)}, bf16[256,256]{1,0:T(8,128)(2,1)S(1)}, bf16[256,256]{1,0:T(8,128)(2,1)S(1)}, bf16[256,256]{1,0:T(8,128)(2,1)...) custom-call(bf16[256,256]{1,0:T(8,128)(2,1)} %bitcast.26, ...), custom_call_target="tpu_custom_call" | custom-call | tf_op jit(solution)/shard_map/forward/pallas_call | solution.py:385
  3.0 22.9 %all_to_all.20 = bf16[128,5,2,128]{3,2,1,0:T(2,128)(2,1)S(1)} all-to-all(bf16[128,5,2,128]{3,2,1,0:T(2,128)(2,1)S(1)} %bitcast.30), channel_id=1, replica_groups=mesh['seq'=32,'batch'=4] {'seq','batch'}, dimensions={0} | all-to-all | bytes 655360 | tf_op jit(solution)/shard_map/all_to_all | solution.py:403
  25.9 9.6 %conv.1 = bf16[1280,128]{1,0:T(8,128)(2,1)S(1)} custom-call(bf16[1280,128]{1,0:T(8,128)(2,1)S(1)} %bitcast.18, f32[1,256]{1,0:T(1,128)S(1)} %get-tuple-element.39.skip), custom_call_target="tpu_custom_call" | custom-call | tf_op jit(solution)/shard_map/conv/pallas_call | solution.py:385
  35.5 0.0 copy-start
  35.5 0.0 copy-start.1
  35.5 0.0 copy-start.2
  35.5 15.9 %all_to_all.21 = bf16[128,5,2,128]{3,2,1,0:T(2,128)(2,1)S(1)} all-to-all(bf16[128,5,2,128]{3,2,1,0:T(2,128)(2,1)S(1)} %bitcast.19), channel_id=1, replica_groups=mesh['seq'=32,'batch'=4] {'seq','batch'}, dimensions={0} | all-to-all | bytes 655360 | tf_op jit(solution)/shard_map/all_to_all | solution.py:403
  51.4 0.0 copy-done
  51.4 0.0 copy-done.1
  51.4 0.0 copy-done.2
  51.4 1.4 %backward.1 = (bf16[256,256]{1,0:T(8,128)(2,1)}, f32[1152,128]{1,0:T(8,128)S(1)}, bf16[1152,128]{1,0:T(8,128)(2,1)S(1)}) custom-call(bf16[1280,128]{1,0:T(8,128)(2,1)S(1)} %bitcast.20, bf16[256,256]{1,0:T(8,128)(2,1)S(1)} %get-tuple-element.40.go, bf16[256,256]{1,0:T(8,128)(2,1)S(1)} %get-tuple-element.41.gi, bf16[256,256]{1,0:T(8,128)(2,1)S(1)} %get-tuple-element.42.v, ...), custom_call_target="tpu_custom_call" | custom-call | tf_op jit(solution)/shard_map/backward/pallas_call | solution.py:385
  52.8 0.6 collective-permute-start
  53.4 1.2 %collective-permute-done.taken = bf16[1152,128]{1,0:T(8,128)(2,1)S(1)} collective-permute-done((bf16[1152,128]{1,0:T(8,128)(2,1)S(1)}, bf16[1152,128]{1,0:T(8,128)(2,1)S(1)}, u32[]{:S(2)}, u32[]{:S(2)}) %collective-permute-start) | collective-permute-done | bytes 294944 | tf_op jit(solution)/shard_map/ppermute | solution.py:410
  54.6 0.1 pair.1
  54.7 13.9 %all_to_all.22 = bf16[64,9,2,128]{3,2,1,0:T(2,128)(2,1)S(1)} all-to-all(bf16[64,9,2,128]{3,2,1,0:T(2,128)(2,1)S(1)} %bitcast.25), channel_id=1, replica_groups={{0,2,4,6,8,10,12,14,16,18,20,22,24,26,28,30,32,34,36,38,40,42,44,46,48,..., dimensions={0} | all-to-all | bytes 589824 | tf_op jit(solution)/shard_map/all_to_all | solution.py:403
  68.6 0.3 total.1
  68.9 14.5 %all_to_all.23 = bf16[64,9,2,128]{3,2,1,0:T(2,128)(2,1)S(1)} all-to-all(bf16[64,9,2,128]{3,2,1,0:T(2,128)(2,1)S(1)} %bitcast.24), channel_id=1, replica_groups={{0,2,4,6,8,10,12,14,16,18,20,22,24,26,28,30,32,34,36,38,40,42,44,46,48,..., dimensions={0} | all-to-all | bytes 589824 | tf_op jit(solution)/shard_map/all_to_all | solution.py:403
  83.4 3.2 %collective-permute-start.1 = (bf16[1152,128]{1,0:T(8,128)(2,1)S(1)}, bf16[1152,128]{1,0:T(8,128)(2,1)S(1)}, u32[]{:S(2)}, u32[]{:S(2)}) collective-permute-start(bf16[1152,128]{1,0:T(8,128)(2,1)S(1)} %bitcast.21), channel_id=1, source_target_pairs={{0,1},{1,0},{2,3},{3,2},{4,5},{5,4},{6,7},{7,6},{8,9},{9,8},{10,11... | collective-permute-start | bytes 884744 | tf_op jit(solution)/shard_map/ppermute | solution.py:410
  86.6 1.2 %collective-permute-done.1.other = bf16[1152,128]{1,0:T(8,128)(2,1)S(1)} collective-permute-done((bf16[1152,128]{1,0:T(8,128)(2,1)S(1)}, bf16[1152,128]{1,0:T(8,128)(2,1)S(1)}, u32[]{:S(2)}, u32[]{:S(2)}) %collective-permute-start.1) | collective-permute-done | bytes 294944 | tf_op jit(solution)/shard_map/ppermute | solution.py:410
  87.8 1.1 %unpack.1 = (f32[256,768]{1,0:T(8,128)}, f32[256,256]{1,0:T(8,128)}, f32[1,256]{1,0:T(1,128)}, f32[5,64]{1,0:T(8,128)}, f32[1,64]{1,0:T(1,128)}, /*index=5*/f32[...) custom-call(bf16[1152,128]{1,0:T(8,128)(2,1)S(1)} %bitcast.22, ...), custom_call_target="tpu_custom_call" | custom-call | tf_op jit(solution)/shard_map/unpack/pallas_call | solution.py:385
Async XLA Ops:
  35.5 15.9 %copy-start = (bf16[256,768]{1,0:T(8,128)(2,1)S(1)}, bf16[256,768]{1,0:T(8,128)(2,1)}, u32[]{:S(2)}) copy-start(bf16[256,768]{1,0:T(8,128)(2,1)} %wi.1) | copy-start | bytes 1179652
  35.5 15.9 %copy-start.1 = (bf16[1,256,256]{2,1,0:T(8,128)(2,1)S(1)}, bf16[1,256,256]{2,1,0:T(8,128)(2,1)}, u32[]{:S(2)}) copy-start(bf16[1,256,256]{2,1,0:T(8,128)(2,1)} %param.12) | copy-start | bytes 393220
  35.5 15.9 %copy-start.2 = (bf16[1,256,256]{2,1,0:T(8,128)(2,1)S(1)}, bf16[1,256,256]{2,1,0:T(8,128)(2,1)}, u32[]{:S(2)}) copy-start(bf16[1,256,256]{2,1,0:T(8,128)(2,1)} %param.13) | copy-start | bytes 393220
  52.8 1.8 %collective-permute-start = (bf16[1152,128]{1,0:T(8,128)(2,1)S(1)}, bf16[1152,128]{1,0:T(8,128)(2,1)S(1)}, u32[]{:S(2)}, u32[]{:S(2)}) collective-permute-start(bf16[1152,128]{1,0:T(8,128)(2,1)S(1)} %get-tuple-element.56), channel_id=1, source_target_pairs={{0,1},{1,0},{2,3},{3,2},{4,5},{5,4},{6,7},{7,6},{8,9},{9,8},{10,11... | collective-permute-start | bytes 884744 | tf_op jit(solution)/shard_map/ppermute | solution.py:410
  83.4 4.4 %collective-permute-start.1 = (bf16[1152,128]{1,0:T(8,128)(2,1)S(1)}, bf16[1152,128]{1,0:T(8,128)(2,1)S(1)}, u32[]{:S(2)}, u32[]{:S(2)}) collective-permute-start(bf16[1152,128]{1,0:T(8,128)(2,1)S(1)} %bitcast.21), channel_id=1, source_target_pairs={{0,1},{1,0},{2,3},{3,2},{4,5},{5,4},{6,7},{7,6},{8,9},{9,8},{10,11... | collective-permute-start | bytes 884744 | tf_op jit(solution)/shard_map/ppermute | solution.py:410

commit v5 on v4

--- a/solution.py
+++ b/solution.py
@@ -116,7 +116,9 @@
     return x
 
 
-def conv_kernel(recv, skip, out, scr, osc, fscr, ubuf, gpad, gs, gsc):
+def conv_kernel(
+    recv, skip, out, scr, osc, fscr, u_a, u_b, c_a, c_b, spad, spad_odd, acc, gpad, gs, gsc
+):
     scr[...] = recv[...].astype(F32)
     own = own_index()
     row, col = iota((256, 256), 0), iota((256, 256), 1)
@@ -139,13 +141,13 @@
     def line(r):
         return scr[pl.ds(r, 128, stride=10), :]
 
-    mixed_up, shifted, x_revs = [], [], []
+    mixed_up, x_revs = [], []
     for ch in range(2):
         f_in = line(8 + ch).astype(BF16)
         fscr[ch, 0:16, :] = jnp.zeros((16, 256), BF16)
+        fscr[ch, 528:592, :] = jnp.zeros((64, 256), BF16)
         for h in range(2):
             fscr[ch, 16:528, 128 * h : 128 * h + 128] = row_rolls(mm(gather[h], f_in), 4).astype(BF16)
-        ubuf[ch, 0:128, :] = jnp.zeros((128, 128), BF16)
     for ch in range(2):
         xs = [line(2 * ch + h) for h in range(2)]
         gs_in = [line(4 + 2 * ch + h) for h in range(2)]
@@ -154,12 +156,14 @@
         g_rev = mm(g2, rev256).astype(BF16)
         up = mm(perm, jnp.concatenate([x2, g_rev], axis=0))
         mixed_up.append(up)
-        shifted.append(
-            (
-                up.astype(BF16),
-                jnp.concatenate([jnp.zeros((8, 256), F32), up[0:248, :]], axis=0).astype(BF16),
-            )
-        )
+        spad[ch, 0:256, :] = jnp.zeros((256, 256), BF16)
+        spad_odd[ch, 0:256, :] = jnp.zeros((256, 256), BF16)
+        spad[ch, 256:512, :] = up.astype(BF16)
+        spad_odd[ch, 256:512, :] = jnp.concatenate(
+            [jnp.zeros((8, 256), F32), up[0:248, :]], axis=0
+        ).astype(BF16)
+        acc[ch] = jnp.zeros((256, 256), F32)
+        c_b[ch, 8] = jnp.zeros((128, 128), F32)
         x_revs.append(
             jnp.concatenate([mm(rev128, x.astype(BF16), NT).astype(BF16) for x in xs], axis=1)
         )
@@ -170,33 +174,42 @@
             for s in range(4):
                 gs[4 * at + s] = gpad[at, 4 * s : 4 * s + 256, :].astype(BF16)
 
-    def diagonals(c_last, c):
-        part = None
-        for g in range(16):
-            old = c_last[8 * g : 8 * g + 8, :]
-            new = jnp.zeros((8, 128), F32) if c is None else c[8 * g : 8 * g + 8, :]
-            now = pltpu.roll(jnp.where(lane + sub >= 127 - 8 * g, old, new), 8 * g + 1, 1)
-            part = now if part is None else part + now
-        return part
-
-    def step(q, carry):
-        ends = []
+    def build_toeplitz(q, u):
         for ch in range(2):
+            for n in range(-1, 8):
+                at = pl.multiple_of(64 * q + 16 * (n // 2 + 1), 16)
+                this = fscr[ch, pl.ds(at, 16), 128 * (n % 2) : 128 * (n % 2) + 128]
+                at = pl.multiple_of(64 * q + 16 * ((n - 1) // 2 + 1), 16)
+                last = fscr[ch, pl.ds(at, 16), 128 - 128 * (n % 2) : 256 - 128 * (n % 2)]
+                fresh = jnp.where(lane16 >= sub16, this, last)
+                tiles = [fresh]
+                for g in range(1, 8):
+                    picked = jnp.where(lane16 < 128 - 16 * g, fresh, last)
+                    tiles.append(pltpu.roll(picked, 16 * g, 1))
+                u[ch, n + 1] = jnp.concatenate(tiles, axis=0)
+
+    def convolve(q, u):
+        at = pl.multiple_of(256 - 32 * q, 16)
+        low = pl.multiple_of(240 - 32 * q, 16)
+        for ch in range(2):
+            left = jnp.concatenate(
+                [
+                    spad[ch, pl.ds(at, 256), :],
+                    spad_odd[ch, pl.ds(at, 256), :],
+                    spad[ch, pl.ds(low, 256), :],
+                    spad_odd[ch, pl.ds(low, 256), :],
+                ],
+                axis=1,
+            )
+            right = []
             for k in range(4):
-                at = pl.multiple_of(64 * q + 16 * k, 16)
-                before = fscr[ch, pl.ds(at, 16), 128:256]
-                now = fscr[ch, pl.ds(pl.multiple_of(at + 16, 16), 16), :]
-                for odd in range(2):
-                    last = before if odd == 0 else now[:, 0:128]
-                    this = now[:, 128 * odd : 128 * odd + 128]
-                    fresh = jnp.where(lane16 >= sub16, this, last)
-                    tiles = [fresh]
-                    for g in range(1, 8):
-                        picked = jnp.where(lane16 < 128 - 16 * g, fresh, last)
-                        tiles.append(pltpu.roll(picked, 16 * g, 1))
-                    to = pl.multiple_of(1024 * q + 256 * k + 128 * (odd + 1), 128)
-                    ubuf[ch, pl.ds(to, 128), :] = jnp.concatenate(tiles, axis=0)
-            c_last = carry[ch]
+                right.append(jnp.concatenate([u[ch, 2 * k + 1], u[ch, 2 * k + 2]], axis=1))
+                right.append(jnp.concatenate([u[ch, 2 * k], u[ch, 2 * k + 1]], axis=1))
+            acc[ch] += mm(left, jnp.concatenate(right, axis=0))
+
+    def correlate(q, c, c_before):
+        for ch in range(2):
+            c[ch, 0] = c_before[ch, 8]
             for s in range(4):
                 at = pl.multiple_of(16 * q, 16)
                 at_next = pl.multiple_of(16 * q + 16 * (s // 3), 16)
@@ -211,51 +224,53 @@
                     axis=0,
                 )
                 both = mm(x_revs[ch], right)
-                for odd in range(2):
-                    c = both[:, 128 * odd : 128 * odd + 128]
-                    to = pl.multiple_of(64 * q + 8 * (2 * s + odd), 8)
-                    gsc[ch, pl.ds(to, 8), :] = diagonals(c_last, c)
-                    c_last = c
-            ends.append(c_last)
-        return tuple(ends)
-
-    ends = lax.fori_loop(0, 8, step, (jnp.zeros((128, 128), F32),) * 2)
+                c[ch, 2 * s + 1] = both[:, 0:128]
+                c[ch, 2 * s + 2] = both[:, 128:256]
+
+    def diagonals(c, ch, n):
+        part = None
+        for g in range(16):
+            old = c[ch, n, 8 * g : 8 * g + 8, :]
+            new = jnp.zeros((8, 128), F32) if n == 8 else c[ch, n + 1, 8 * g : 8 * g + 8, :]
+            now = pltpu.roll(jnp.where(lane + sub >= 127 - 8 * g, old, new), 8 * g + 1, 1)
+            part = now if part is None else part + now
+        return part
+
+    def sum_diagonals(q, c):
+        for ch in range(2):
+            for n in range(8):
+                to = pl.multiple_of(64 * q + 64 + 8 * n, 8)
+                gsc[ch, pl.ds(to, 8), :] = diagonals(c, ch, n)
+
+    build_toeplitz(0, u_a)
+
+    def step(r, carry):
+        q = 2 * r
+        convolve(q, u_a)
+        correlate(q, c_a, c_b)
+        build_toeplitz(q + 1, u_b)
+        sum_diagonals(q - 1, c_b)
+        convolve(q + 1, u_b)
+        correlate(q + 1, c_b, c_a)
+        build_toeplitz(q + 2, u_a)
+        sum_diagonals(q, c_a)
+        return carry
+
+    lax.fori_loop(0, 4, step, 0)
+    sum_diagonals(7, c_b)
 
     for ch in range(2):
-        total = None
-        for q in range(4):
-            low = 64 * q
-            left, right = [], []
-            for k in range(8 * q, 8 * q + 8):
-                down = 16 * (k // 2)
-                piece = shifted[ch][k % 2]
-                if down <= low:
-                    left.append(piece[low - down : 256 - down, :])
-                else:
-                    left.append(
-                        jnp.concatenate(
-                            [jnp.zeros((down - low, 256), BF16), piece[0 : 256 - down, :]], axis=0
-                        )
-                    )
-                u = [ubuf[ch, 128 * n : 128 * n + 128, :] for n in range(2 * k, 2 * k + 3)]
-                right.append(jnp.concatenate([u[1], u[2]], axis=1))
-                right.append(jnp.concatenate([u[0], u[1]], axis=1))
-            part = mm(jnp.concatenate(left, axis=1), jnp.concatenate(right, axis=0))
-            if total is None:
-                total = part
-            else:
-                total = jnp.concatenate([total[0:low, :], total[low:, :] + part], axis=0)
         mine = iota((1, 256), 1) == own + 128 * ch
         skip_now = jnp.sum(jnp.where(mine, skip[...], 0.0), axis=1, keepdims=True)
-        done = (total + skip_now * mixed_up[ch]).astype(BF16)
+        done = (acc[ch] + skip_now * mixed_up[ch]).astype(BF16)
         apart = mm(back, done)
         conv2 = apart[0:128, :]
         gm2 = mm(apart[128:256, :].astype(BF16), rev256)
         for h in range(2):
             osc[pl.ds(2 * ch + h, 128, stride=10), :] = conv2[:, 128 * h : 128 * h + 128]
             osc[pl.ds(4 + 2 * ch + h, 128, stride=10), :] = gm2[:, 128 * h : 128 * h + 128]
-        gsc[ch, 512:520, :] = diagonals(ends[ch], None)
-        gf = row_rolls(gsc[ch, 8:520, :], 3).reshape(64, 8, 128).sum(axis=1)
+        gsc[ch, 576:584, :] = diagonals(c_b, ch, 8)
+        gf = row_rolls(gsc[ch, 72:584, :], 3).reshape(64, 8, 128).sum(axis=1)
         osc[pl.ds(8 + ch, 128, stride=10), :] = mm(spread_g, gf.astype(BF16))
     out[...] = osc[...].astype(BF16)
 
@@ -444,11 +459,17 @@
         [
             pltpu.VMEM((1280, 128), F32),
             pltpu.VMEM((1280, 128), F32),
-            pltpu.VMEM((2, 528, 256), BF16),
-            pltpu.VMEM((2, 65 * 128, 128), BF16),
+            pltpu.VMEM((2, 592, 256), BF16),
+            pltpu.VMEM((2, 9, 128, 128), BF16),
+            pltpu.VMEM((2, 9, 128, 128), BF16),
+            pltpu.VMEM((2, 9, 128, 128), F32),
+            pltpu.VMEM((2, 9, 128, 128), F32),
+            pltpu.VMEM((2, 512, 256), BF16),
+            pltpu.VMEM((2, 512, 256), BF16),
+            pltpu.VMEM((2, 256, 256), F32),
             pltpu.VMEM((4, 288, 128), F32),
             pltpu.VMEM((16, 256, 128), BF16),
-            pltpu.VMEM((2, 520, 128), F32),
+            pltpu.VMEM((2, 584, 128), F32),
         ],
     )(recv, skip)
     recv = exchange(sent, 10)

time: 89.2 us -> 86.4 us (0.969)
  Pallas kernels: 14.8 us -> 12 us
    pallas_call x6, Pallas kernels: 14.8 us -> 12 us  [run(): pl.pallas_call(kernel, out_shape=out_shape, in_specs=[pl.BlockSpec(memory...]
where the time goes in v5:
time: 86.4 us; the launch traced here: 86.2 us
  blocking collectives  67.2 us (78%)
  Pallas kernels  12 us (14%)
  starting transfers between devices  3.78 us (4%)
  waiting for transfers between devices  2.42 us (3%)
    all_to_all x4, blocking collectives, exchange(): lax.all_to_all(y, AXES, split_axis=0, concat_axis=0, axis_index_groups=gr...  67.2 us
    pallas_call x6, Pallas kernels, run(): pl.pallas_call(kernel, out_shape=out_shape, in_specs=[pl.BlockSpec(memory...  12 us
    ppermute x2, starting transfers between devices, swap_cores(): return lax.ppermute(x, 'batch', [(k, k ^ 1) for k in range(4)])  3.78 us
    ppermute x2, waiting for transfers between devices, swap_cores(): return lax.ppermute(x, 'batch', [(k, k ^ 1) for k in range(4)])  2.42 us
  transfers between devices with their start and end apart: 2, of which 2 were waited for; matrix products, arithmetic and copies ran while one was open for 0% of the time, Pallas kernels for 0%

profile of v5, /device:TPU:1, one launch (start us, length us, event | category | flops | bytes accessed | tf_op | source)
XLA Modules:
  0.0 86.2 jit_solution(2279753135611542690)
XLA Ops:
  0.6 2.3 %forward.1 = (bf16[1280,128]{1,0:T(8,128)(2,1)S(1)}, bf16[256,256]{1,0:T(8,128)(2,1)S(1)}, bf16[256,256]{1,0:T(8,128)(2,1)S(1)}, bf16[256,256]{1,0:T(8,128)(2,1)...) custom-call(bf16[256,256]{1,0:T(8,128)(2,1)} %bitcast.26, ...), custom_call_target="tpu_custom_call" | custom-call | tf_op jit(solution)/shard_map/forward/pallas_call | solution.py:400
  3.0 22.9 %all_to_all.20 = bf16[128,5,2,128]{3,2,1,0:T(2,128)(2,1)S(1)} all-to-all(bf16[128,5,2,128]{3,2,1,0:T(2,128)(2,1)S(1)} %bitcast.30), channel_id=1, replica_groups=mesh['seq'=32,'batch'=4] {'seq','batch'}, dimensions={0} | all-to-all | bytes 655360 | tf_op jit(solution)/shard_map/all_to_all | solution.py:418
  25.9 6.9 %conv.1 = bf16[1280,128]{1,0:T(8,128)(2,1)S(1)} custom-call(bf16[1280,128]{1,0:T(8,128)(2,1)S(1)} %bitcast.18, f32[1,256]{1,0:T(1,128)S(1)} %get-tuple-element.39.skip), custom_call_target="tpu_custom_call" | custom-call | tf_op jit(solution)/shard_map/conv/pallas_call | solution.py:400
  32.7 0.0 copy-start
  32.7 0.0 copy-start.1
  32.8 0.0 copy-start.2
  32.8 15.9 %all_to_all.21 = bf16[128,5,2,128]{3,2,1,0:T(2,128)(2,1)S(1)} all-to-all(bf16[128,5,2,128]{3,2,1,0:T(2,128)(2,1)S(1)} %bitcast.19), channel_id=1, replica_groups=mesh['seq'=32,'batch'=4] {'seq','batch'}, dimensions={0} | all-to-all | bytes 655360 | tf_op jit(solution)/shard_map/all_to_all | solution.py:418
  48.7 0.0 copy-done
  48.7 0.0 copy-done.1
  48.7 0.0 copy-done.2
  48.7 1.4 %backward.1 = (bf16[256,256]{1,0:T(8,128)(2,1)}, f32[1152,128]{1,0:T(8,128)S(1)}, bf16[1152,128]{1,0:T(8,128)(2,1)S(1)}) custom-call(bf16[1280,128]{1,0:T(8,128)(2,1)S(1)} %bitcast.20, bf16[256,256]{1,0:T(8,128)(2,1)S(1)} %get-tuple-element.40.go, bf16[256,256]{1,0:T(8,128)(2,1)S(1)} %get-tuple-element.41.gi, bf16[256,256]{1,0:T(8,128)(2,1)S(1)} %get-tuple-element.42.v, ...), custom_call_target="tpu_custom_call" | custom-call | tf_op jit(solution)/shard_map/backward/pallas_call | solution.py:400
  50.0 0.6 collective-permute-start
  50.6 1.2 %collective-permute-done.taken = bf16[1152,128]{1,0:T(8,128)(2,1)S(1)} collective-permute-done((bf16[1152,128]{1,0:T(8,128)(2,1)S(1)}, bf16[1152,128]{1,0:T(8,128)(2,1)S(1)}, u32[]{:S(2)}, u32[]{:S(2)}) %collective-permute-start) | collective-permute-done | bytes 294944 | tf_op jit(solution)/shard_map/ppermute | solution.py:425
  51.9 0.1 pair.1
  51.9 13.9 %all_to_all.22 = bf16[64,9,2,128]{3,2,1,0:T(2,128)(2,1)S(1)} all-to-all(bf16[64,9,2,128]{3,2,1,0:T(2,128)(2,1)S(1)} %bitcast.25), channel_id=1, replica_groups={{0,2,4,6,8,10,12,14,16,18,20,22,24,26,28,30,32,34,36,38,40,42,44,46,48,..., dimensions={0} | all-to-all | bytes 589824 | tf_op jit(solution)/shard_map/all_to_all | solution.py:418
  65.8 0.3 total.1
  66.2 14.5 %all_to_all.23 = bf16[64,9,2,128]{3,2,1,0:T(2,128)(2,1)S(1)} all-to-all(bf16[64,9,2,128]{3,2,1,0:T(2,128)(2,1)S(1)} %bitcast.24), channel_id=1, replica_groups={{0,2,4,6,8,10,12,14,16,18,20,22,24,26,28,30,32,34,36,38,40,42,44,46,48,..., dimensions={0} | all-to-all | bytes 589824 | tf_op jit(solution)/shard_map/all_to_all | solution.py:418
  80.7 3.2 %collective-permute-start.1 = (bf16[1152,128]{1,0:T(8,128)(2,1)S(1)}, bf16[1152,128]{1,0:T(8,128)(2,1)S(1)}, u32[]{:S(2)}, u32[]{:S(2)}) collective-permute-start(bf16[1152,128]{1,0:T(8,128)(2,1)S(1)} %bitcast.21), channel_id=1, source_target_pairs={{0,1},{1,0},{2,3},{3,2},{4,5},{5,4},{6,7},{7,6},{8,9},{9,8},{10,11... | collective-permute-start | bytes 884744 | tf_op jit(solution)/shard_map/ppermute | solution.py:425
  83.8 1.2 %collective-permute-done.1.other = bf16[1152,128]{1,0:T(8,128)(2,1)S(1)} collective-permute-done((bf16[1152,128]{1,0:T(8,128)(2,1)S(1)}, bf16[1152,128]{1,0:T(8,128)(2,1)S(1)}, u32[]{:S(2)}, u32[]{:S(2)}) %collective-permute-start.1) | collective-permute-done | bytes 294944 | tf_op jit(solution)/shard_map/ppermute | solution.py:425
  85.0 1.1 %unpack.1 = (f32[256,768]{1,0:T(8,128)}, f32[256,256]{1,0:T(8,128)}, f32[1,256]{1,0:T(1,128)}, f32[5,64]{1,0:T(8,128)}, f32[1,64]{1,0:T(1,128)}, /*index=5*/f32[...) custom-call(bf16[1152,128]{1,0:T(8,128)(2,1)S(1)} %bitcast.22, ...), custom_call_target="tpu_custom_call" | custom-call | tf_op jit(solution)/shard_map/unpack/pallas_call | solution.py:400
Async XLA Ops:
  32.7 15.9 %copy-start = (bf16[256,768]{1,0:T(8,128)(2,1)S(1)}, bf16[256,768]{1,0:T(8,128)(2,1)}, u32[]{:S(2)}) copy-start(bf16[256,768]{1,0:T(8,128)(2,1)} %wi.1) | copy-start | bytes 1179652
  32.7 15.9 %copy-start.1 = (bf16[1,256,256]{2,1,0:T(8,128)(2,1)S(1)}, bf16[1,256,256]{2,1,0:T(8,128)(2,1)}, u32[]{:S(2)}) copy-start(bf16[1,256,256]{2,1,0:T(8,128)(2,1)} %param.12) | copy-start | bytes 393220
  32.8 15.9 %copy-start.2 = (bf16[1,256,256]{2,1,0:T(8,128)(2,1)S(1)}, bf16[1,256,256]{2,1,0:T(8,128)(2,1)}, u32[]{:S(2)}) copy-start(bf16[1,256,256]{2,1,0:T(8,128)(2,1)} %param.13) | copy-start | bytes 393220
  50.0 1.8 %collective-permute-start = (bf16[1152,128]{1,0:T(8,128)(2,1)S(1)}, bf16[1152,128]{1,0:T(8,128)(2,1)S(1)}, u32[]{:S(2)}, u32[]{:S(2)}) collective-permute-start(bf16[1152,128]{1,0:T(8,128)(2,1)S(1)} %get-tuple-element.56), channel_id=1, source_target_pairs={{0,1},{1,0},{2,3},{3,2},{4,5},{5,4},{6,7},{7,6},{8,9},{9,8},{10,11... | collective-permute-start | bytes 884744 | tf_op jit(solution)/shard_map/ppermute | solution.py:425
  80.7 4.4 %collective-permute-start.1 = (bf16[1152,128]{1,0:T(8,128)(2,1)S(1)}, bf16[1152,128]{1,0:T(8,128)(2,1)S(1)}, u32[]{:S(2)}, u32[]{:S(2)}) collective-permute-start(bf16[1152,128]{1,0:T(8,128)(2,1)S(1)} %bitcast.21), channel_id=1, source_target_pairs={{0,1},{1,0},{2,3},{3,2},{4,5},{5,4},{6,7},{7,6},{8,9},{9,8},{10,11... | collective-permute-start | bytes 884744 | tf_op jit(solution)/shard_map/ppermute | solution.py:425

commit v6 on v5

--- a/solution.py
+++ b/solution.py
@@ -130,6 +130,7 @@
         return jnp.where(sig < 4, blk * 4 + sig, 128 + (31 - blk) * 4 + sig - 4)
 
     perm = one_hot(source(row) == col)
+    weave = one_hot(((row >> 2) & 1) * 128 + (row >> 3) * 4 + (row & 3) == col)
     back = one_hot(source(col) == row)
     gather = [
         one_hot(iota((512, 128), 1) >> 1 == 2 * (iota((512, 128), 0) >> 4) + h) for h in range(2)
@@ -164,15 +165,18 @@
         ).astype(BF16)
         acc[ch] = jnp.zeros((256, 256), F32)
         c_b[ch, 8] = jnp.zeros((128, 128), F32)
-        x_revs.append(
-            jnp.concatenate([mm(rev128, x.astype(BF16), NT).astype(BF16) for x in xs], axis=1)
+        woven = mm(
+            weave,
+            jnp.concatenate(
+                [jnp.concatenate([xs[h], gs_in[h]], axis=1) for h in range(2)], axis=0
+            ).astype(BF16),
         )
-        for h in range(2):
-            at = 2 * ch + h
-            gpad[at, 0:128, :] = gs_in[h]
-            gpad[at, 128:288, :] = jnp.zeros((160, 128), F32)
-            for s in range(4):
-                gs[4 * at + s] = gpad[at, 4 * s : 4 * s + 256, :].astype(BF16)
+        x_revs.append(mm(rev128, woven[:, 0:128].astype(BF16), NT).astype(BF16))
+        gpad[ch, 0:256, :] = woven[:, 128:256]
+        gpad[ch, 256:272, :] = jnp.zeros((16, 128), F32)
+        for s in range(4):
+            gs[4 * ch + s, 0:256, :] = gpad[ch, 4 * s : 4 * s + 256, :].astype(BF16)
+            gs[4 * ch + s, 256:384, :] = jnp.zeros((128, 128), BF16)
 
     def build_toeplitz(q, u):
         for ch in range(2):
@@ -188,16 +192,18 @@
                     tiles.append(pltpu.roll(picked, 16 * g, 1))
                 u[ch, n + 1] = jnp.concatenate(tiles, axis=0)
 
-    def convolve(q, u):
-        at = pl.multiple_of(256 - 32 * q, 16)
-        low = pl.multiple_of(240 - 32 * q, 16)
+    def convolve(q, u, late):
+        skipped = 128 if late else 0
+        at = pl.multiple_of(256 - 32 * q + skipped, 16)
+        low = pl.multiple_of(240 - 32 * q + skipped, 16)
+        count = 256 - skipped
         for ch in range(2):
             left = jnp.concatenate(
                 [
-                    spad[ch, pl.ds(at, 256), :],
-                    spad_odd[ch, pl.ds(at, 256), :],
-                    spad[ch, pl.ds(low, 256), :],
-                    spad_odd[ch, pl.ds(low, 256), :],
+                    spad[ch, pl.ds(at, count), :],
+                    spad_odd[ch, pl.ds(at, count), :],
+                    spad[ch, pl.ds(low, count), :],
+                    spad_odd[ch, pl.ds(low, count), :],
                 ],
                 axis=1,
             )
@@ -205,25 +211,19 @@
             for k in range(4):
                 right.append(jnp.concatenate([u[ch, 2 * k + 1], u[ch, 2 * k + 2]], axis=1))
                 right.append(jnp.concatenate([u[ch, 2 * k], u[ch, 2 * k + 1]], axis=1))
-            acc[ch] += mm(left, jnp.concatenate(right, axis=0))
-
-    def correlate(q, c, c_before):
+            acc[ch, skipped:256, :] += mm(left, jnp.concatenate(right, axis=0))
+
+    def correlate(q, c, c_before, late):
+        count = 128 if late else 256
         for ch in range(2):
             c[ch, 0] = c_before[ch, 8]
             for s in range(4):
-                at = pl.multiple_of(16 * q, 16)
-                at_next = pl.multiple_of(16 * q + 16 * (s // 3), 16)
-                g0 = gs[8 * ch + s, pl.ds(at, 128), :]
-                g1 = gs[8 * ch + 4 + s, pl.ds(at, 128), :]
-                g0_next = gs[8 * ch + (s + 1) % 4, pl.ds(at_next, 128), :]
+                at = pl.multiple_of(32 * q + 16 * (s // 2), 16)
                 right = jnp.concatenate(
-                    [
-                        jnp.concatenate([g0, g1], axis=1),
-                        jnp.concatenate([g1, g0_next], axis=1),
-                    ],
-                    axis=0,
+                    [gs[4 * ch + (2 * s + odd) % 4, pl.ds(at, count), :] for odd in range(2)],
+                    axis=1,
                 )
-                both = mm(x_revs[ch], right)
+                both = mm(x_revs[ch][:, 0:count], right)
                 c[ch, 2 * s + 1] = both[:, 0:128]
                 c[ch, 2 * s + 2] = both[:, 128:256]
 
@@ -244,19 +244,28 @@
 
     build_toeplitz(0, u_a)
 
-    def step(r, carry):
+    def step(r, late):
         q = 2 * r
-        convolve(q, u_a)
-        correlate(q, c_a, c_b)
+        convolve(q, u_a, late)
+        correlate(q, c_a, c_b, late)
         build_toeplitz(q + 1, u_b)
-        sum_diagonals(q - 1, c_b)
-        convolve(q + 1, u_b)
-        correlate(q + 1, c_b, c_a)
-        build_toeplitz(q + 2, u_a)
+        if r > 0:
+            sum_diagonals(q - 1, c_b)
+        convolve(q + 1, u_b, late)
+        correlate(q + 1, c_b, c_a, late)
+        if r < 3:
+            build_toeplitz(q + 2, u_a)
         sum_diagonals(q, c_a)
-        return carry
-
-    lax.fori_loop(0, 4, step, 0)
+
+    def run_step(late):
+        def run(r, carry):
+            step(r, late)
+            return carry
+
+        return run
+
+    for r in range(4):
+        step(r, r >= 2)
     sum_diagonals(7, c_b)
 
     for ch in range(2):
@@ -276,8 +285,8 @@
 
 
 def backward_kernel(
-    recv, go, gi, v, gg, tok, og, wi, emb, pre1, act1, pre2, act2, bias, modul, hw, fw, sf,
-    gtok, kept, given, scr, tmp, sm, ssc,
+    recv, go, gi, v, gg, tok, og, emb, pre1, act1, pre2, act2, bias, modul, hw, fw, sf,
+    gp_o, kept, given, scr, tmp, sm, ssc,
 ):
     own = own_index()
     scr[...] = recv[...].astype(F32)
@@ -306,7 +315,7 @@
         ],
         axis=1,
     )
-    gtok[...] = mm(gp, wi[...], NT).astype(BF16)
+    gp_o[...] = gp
     grad_iw = mm(tok[...].astype(F32).T.astype(BF16), gp)
     for rb in range(2):
         for cb in range(8):
@@ -349,6 +358,10 @@
     given[...] = ssc[pl.ds(pl.multiple_of((1 - core) * 1152, 1152), 1152), :].astype(BF16)
 
 
+def token_kernel(gp, wi, gtok):
+    gtok[...] = mm(gp[...], wi[...], NT).astype(BF16)
+
+
 def pair_kernel(kept, taken, out):
     out[...] = (kept[...] + taken[...].astype(F32)).astype(BF16)
 
@@ -401,8 +414,7 @@
             kernel,
             out_shape=out_shape,
             in_specs=[
-                pl.BlockSpec(memory_space=pltpu.HBM if from_hbm else pltpu.VMEM)
-                for _ in args
+                pl.BlockSpec(memory_space=pltpu.HBM if from_hbm else pltpu.VMEM) for _ in args
             ],
             scratch_shapes=list(scratch),
             compiler_params=pltpu.CompilerParams(vmem_limit_bytes=48 * 1024 * 1024),
@@ -410,6 +422,24 @@
         )(*args)
 
     return run
+
+
+def conv_scratch():
+    return [
+        pltpu.VMEM((1280, 128), F32),
+        pltpu.VMEM((1280, 128), F32),
+        pltpu.VMEM((2, 592, 256), BF16),
+        pltpu.VMEM((2, 9, 128, 128), BF16),
+        pltpu.VMEM((2, 9, 128, 128), BF16),
+        pltpu.VMEM((2, 9, 128, 128), F32),
+        pltpu.VMEM((2, 9, 128, 128), F32),
+        pltpu.VMEM((2, 512, 256), BF16),
+        pltpu.VMEM((2, 512, 256), BF16),
+        pltpu.VMEM((2, 256, 256), F32),
+        pltpu.VMEM((2, 272, 128), F32),
+        pltpu.VMEM((8, 384, 128), BF16),
+        pltpu.VMEM((2, 584, 128), F32),
+    ]
 
 
 def exchange(x, rows, groups=None):
@@ -456,34 +486,21 @@
         conv_kernel,
         "conv",
         sds(1280, 128, dtype=BF16),
-        [
-            pltpu.VMEM((1280, 128), F32),
-            pltpu.VMEM((1280, 128), F32),
-            pltpu.VMEM((2, 592, 256), BF16),
-            pltpu.VMEM((2, 9, 128, 128), BF16),
-            pltpu.VMEM((2, 9, 128, 128), BF16),
-            pltpu.VMEM((2, 9, 128, 128), F32),
-            pltpu.VMEM((2, 9, 128, 128), F32),
-            pltpu.VMEM((2, 512, 256), BF16),
-            pltpu.VMEM((2, 512, 256), BF16),
-            pltpu.VMEM((2, 256, 256), F32),
-            pltpu.VMEM((4, 288, 128), F32),
-            pltpu.VMEM((16, 256, 128), BF16),
-            pltpu.VMEM((2, 584, 128), F32),
-        ],
+        conv_scratch(),
     )(recv, skip)
     recv = exchange(sent, 10)
-    gtok, kept, given = call(
+    gp, kept, given = call(
         backward_kernel,
         "backward",
-        (square, sds(1152, 128), sds(1152, 128, dtype=BF16)),
+        (sds(256, 768, dtype=BF16), sds(1152, 128), sds(1152, 128, dtype=BF16)),
         [
             pltpu.VMEM((1280, 128), F32),
             pltpu.VMEM((128, 256), F32),
             pltpu.VMEM((128, 128), F32),
             pltpu.VMEM((2304, 128), F32),
         ],
-    )(recv, go, gi, v, gg, tok, og, in_weight, emb, pre1, act1, pre2, act2, bias, modul, hw, fw, sf)
+    )(recv, go, gi, v, gg, tok, og, emb, pre1, act1, pre2, act2, bias, modul, hw, fw, sf)
+    gtok = call(token_kernel, "tokens", square)(gp, in_weight)
     half = sds(1152, 128, dtype=BF16)
     slab = call(pair_kernel, "pair", half)(kept, swap_cores(given))
     by_core = [list(range(core, 128, 2)) for core in range(2)]

time: 86.4 us -> 85.2 us (0.986)
  waiting for transfers between devices: 2.42 us -> 1.46 us
    ppermute x2, waiting for transfers between devices: 2.42 us -> 1.46 us  [swap_cores(): return lax.ppermute(x, 'batch', [(k, k ^ 1) for k in range(4)])]
    pallas_call x6 -> x7, Pallas kernels: 12 us -> 11.6 us  [run(): pl.pallas_call(kernel, out_shape=out_shape, in_specs=[pl.BlockSpec(memory...]
  transfers between devices with their start and end apart: 2 -> 2, of which waited for: 2 -> 2; matrix products, arithmetic and copies ran while one was open for 0% -> 0% of each run, Pallas kernels for 0% -> 1%
where the time goes in v6:
time: 85.2 us; the launch traced here: 84.9 us
  blocking collectives  67.3 us (79%)
  Pallas kernels  11.6 us (14%)
  starting transfers between devices  3.86 us (5%)
  waiting for transfers between devices  1.46 us (2%)
    all_to_all x4, blocking collectives, exchange(): lax.all_to_all(y, AXES, split_axis=0, concat_axis=0, axis_index_groups=gr...  67.3 us
    pallas_call x7, Pallas kernels, run(): pl.pallas_call(kernel, out_shape=out_shape, in_specs=[pl.BlockSpec(memory...  11.6 us
    ppermute x2, starting transfers between devices, swap_cores(): return lax.ppermute(x, 'batch', [(k, k ^ 1) for k in range(4)])  3.86 us
  transfers between devices with their start and end apart: 2, of which 2 were waited for; matrix products, arithmetic and copies ran while one was open for 0% of the time, Pallas kernels for 1%

profile of v6, /device:TPU:1, one launch (start us, length us, event | category | flops | bytes accessed | tf_op | source)
XLA Modules:
  0.0 84.9 jit_solution(16611740078648268643)
XLA Ops:
  0.6 2.3 %forward.1 = (bf16[1280,128]{1,0:T(8,128)(2,1)S(1)}, bf16[256,256]{1,0:T(8,128)(2,1)S(1)}, bf16[256,256]{1,0:T(8,128)(2,1)S(1)}, bf16[256,256]{1,0:T(8,128)(2,1)...) custom-call(bf16[256,256]{1,0:T(8,128)(2,1)} %bitcast.26, ...), custom_call_target="tpu_custom_call" | custom-call | tf_op jit(solution)/shard_map/forward/pallas_call | solution.py:413
  3.0 22.9 %all_to_all.20 = bf16[128,5,2,128]{3,2,1,0:T(2,128)(2,1)S(1)} all-to-all(bf16[128,5,2,128]{3,2,1,0:T(2,128)(2,1)S(1)} %bitcast.30), channel_id=1, replica_groups=mesh['seq'=32,'batch'=4] {'seq','batch'}, dimensions={0} | all-to-all | bytes 655360 | tf_op jit(solution)/shard_map/all_to_all | solution.py:448
  25.9 5.8 %conv.1 = bf16[1280,128]{1,0:T(8,128)(2,1)S(1)} custom-call(bf16[1280,128]{1,0:T(8,128)(2,1)S(1)} %bitcast.18, f32[1,256]{1,0:T(1,128)S(1)} %get-tuple-element.39.skip), custom_call_target="tpu_custom_call" | custom-call | tf_op jit(solution)/shard_map/conv/pallas_call | solution.py:413
  31.7 0.0 copy-start.1
  31.7 0.0 copy-start.2
  31.7 15.9 %all_to_all.21 = bf16[128,5,2,128]{3,2,1,0:T(2,128)(2,1)S(1)} all-to-all(bf16[128,5,2,128]{3,2,1,0:T(2,128)(2,1)S(1)} %bitcast.19), channel_id=1, replica_groups=mesh['seq'=32,'batch'=4] {'seq','batch'}, dimensions={0} | all-to-all | bytes 655360 | tf_op jit(solution)/shard_map/all_to_all | solution.py:448
  47.6 0.0 copy-done.1
  47.6 0.0 copy-done.2
  47.6 1.0 %backward.1 = (bf16[256,768]{1,0:T(8,128)(2,1)S(1)}, f32[1152,128]{1,0:T(8,128)S(1)}, bf16[1152,128]{1,0:T(8,128)(2,1)S(1)}) custom-call(bf16[1280,128]{1,0:T(8,128)(2,1)S(1)} %bitcast.20, bf16[256,256]{1,0:T(8,128)(2,1)S(1)} %get-tuple-element.40.go, bf16[256,256]{1,0:T(8,128)(2,1)S(1)} %get-tuple-element.41.gi, bf16[256,256]{1,0:T(8,128)(2,1)S(1)} %get-tuple-element.42.v, ...), custom_call_target="tpu_custom_call" | custom-call | tf_op jit(solution)/shard_map/backward/pallas_call | solution.py:413
  48.6 0.7 collective-permute-start
  49.3 1.2 %collective-permute-done.taken = bf16[1152,128]{1,0:T(8,128)(2,1)S(1)} collective-permute-done((bf16[1152,128]{1,0:T(8,128)(2,1)S(1)}, bf16[1152,128]{1,0:T(8,128)(2,1)S(1)}, u32[]{:S(2)}, u32[]{:S(2)}) %collective-permute-start) | collective-permute-done | bytes 294944 | tf_op jit(solution)/shard_map/ppermute | solution.py:455
  50.5 0.1 pair.1
  50.6 13.9 %all_to_all.22 = bf16[64,9,2,128]{3,2,1,0:T(2,128)(2,1)S(1)} all-to-all(bf16[64,9,2,128]{3,2,1,0:T(2,128)(2,1)S(1)} %bitcast.25), channel_id=1, replica_groups={{0,2,4,6,8,10,12,14,16,18,20,22,24,26,28,30,32,34,36,38,40,42,44,46,48,..., dimensions={0} | all-to-all | bytes 589824 | tf_op jit(solution)/shard_map/all_to_all | solution.py:448
  64.5 0.3 total.1
  64.8 0.0 copy-start
  64.8 14.6 %all_to_all.23 = bf16[64,9,2,128]{3,2,1,0:T(2,128)(2,1)S(1)} all-to-all(bf16[64,9,2,128]{3,2,1,0:T(2,128)(2,1)S(1)} %bitcast.24), channel_id=1, replica_groups={{0,2,4,6,8,10,12,14,16,18,20,22,24,26,28,30,32,34,36,38,40,42,44,46,48,..., dimensions={0} | all-to-all | bytes 589824 | tf_op jit(solution)/shard_map/all_to_all | solution.py:448
  79.4 3.2 %collective-permute-start.1 = (bf16[1152,128]{1,0:T(8,128)(2,1)S(1)}, bf16[1152,128]{1,0:T(8,128)(2,1)S(1)}, u32[]{:S(2)}, u32[]{:S(2)}) collective-permute-start(bf16[1152,128]{1,0:T(8,128)(2,1)S(1)} %bitcast.21), channel_id=1, source_target_pairs={{0,1},{1,0},{2,3},{3,2},{4,5},{5,4},{6,7},{7,6},{8,9},{9,8},{10,11... | collective-permute-start | bytes 884744 | tf_op jit(solution)/shard_map/ppermute | solution.py:455
  82.6 0.0 copy-done
  82.6 1.0 %tokens.1 = bf16[256,256]{1,0:T(8,128)(2,1)} custom-call(bf16[256,768]{1,0:T(8,128)(2,1)S(1)} %get-tuple-element.54.gp, bf16[256,768]{1,0:T(8,128)(2,1)S(1)} %copy-done), custom_call_target="tpu_custom_call" | custom-call | tf_op jit(solution)/shard_map/tokens/pallas_call | solution.py:413
  83.6 0.2 collective-permute-done.1.other
  83.8 1.1 %unpack.1 = (f32[256,768]{1,0:T(8,128)}, f32[256,256]{1,0:T(8,128)}, f32[1,256]{1,0:T(1,128)}, f32[5,64]{1,0:T(8,128)}, f32[1,64]{1,0:T(1,128)}, /*index=5*/f32[...) custom-call(bf16[1152,128]{1,0:T(8,128)(2,1)S(1)} %bitcast.22, ...), custom_call_target="tpu_custom_call" | custom-call | tf_op jit(solution)/shard_map/unpack/pallas_call | solution.py:413
Async XLA Ops:
  31.7 15.9 %copy-start.1 = (bf16[1,256,256]{2,1,0:T(8,128)(2,1)S(1)}, bf16[1,256,256]{2,1,0:T(8,128)(2,1)}, u32[]{:S(2)}) copy-start(bf16[1,256,256]{2,1,0:T(8,128)(2,1)} %param.12) | copy-start | bytes 393220
  31.7 15.9 %copy-start.2 = (bf16[1,256,256]{2,1,0:T(8,128)(2,1)S(1)}, bf16[1,256,256]{2,1,0:T(8,128)(2,1)}, u32[]{:S(2)}) copy-start(bf16[1,256,256]{2,1,0:T(8,128)(2,1)} %param.13) | copy-start | bytes 393220
  48.6 1.9 %collective-permute-start = (bf16[1152,128]{1,0:T(8,128)(2,1)S(1)}, bf16[1152,128]{1,0:T(8,128)(2,1)S(1)}, u32[]{:S(2)}, u32[]{:S(2)}) collective-permute-start(bf16[1152,128]{1,0:T(8,128)(2,1)S(1)} %get-tuple-element.56), channel_id=1, source_target_pairs={{0,1},{1,0},{2,3},{3,2},{4,5},{5,4},{6,7},{7,6},{8,9},{9,8},{10,11... | collective-permute-start | bytes 884744 | tf_op jit(solution)/shard_map/ppermute | solution.py:455
  64.8 17.8 %copy-start = (bf16[256,768]{1,0:T(8,128)(2,1)S(1)}, bf16[256,768]{1,0:T(8,128)(2,1)}, u32[]{:S(2)}) copy-start(bf16[256,768]{1,0:T(8,128)(2,1)} %wi.1) | copy-start | bytes 1179652
  79.4 4.4 %collective-permute-start.1 = (bf16[1152,128]{1,0:T(8,128)(2,1)S(1)}, bf16[1152,128]{1,0:T(8,128)(2,1)S(1)}, u32[]{:S(2)}, u32[]{:S(2)}) collective-permute-start(bf16[1152,128]{1,0:T(8,128)(2,1)S(1)} %bitcast.21), channel_id=1, source_target_pairs={{0,1},{1,0},{2,3},{3,2},{4,5},{5,4},{6,7},{7,6},{8,9},{9,8},{10,11... | collective-permute-start | bytes 884744 | tf_op jit(solution)/shard_map/ppermute | solution.py:455

commit v7 on v6

--- a/solution.py
+++ b/solution.py
@@ -106,7 +106,7 @@
                 scr[pl.ds(at + 2 * ch + half, 128, stride=10), :] = whole[
                     128 * ch : 128 * ch + 128, 128 * half : 128 * half + 128
                 ]
-    slab[...] = scr[...].astype(BF16)
+    slab[...] = scr[0:1280, :].astype(BF16)
 
 
 def row_rolls(x, bits):
@@ -119,7 +119,7 @@
 def conv_kernel(
     recv, skip, out, scr, osc, fscr, u_a, u_b, c_a, c_b, spad, spad_odd, acc, gpad, gs, gsc
 ):
-    scr[...] = recv[...].astype(F32)
+    scr[0:1280, :] = recv[...].astype(F32)
     own = own_index()
     row, col = iota((256, 256), 0), iota((256, 256), 1)
     rev256 = one_hot(row + col == 255)
@@ -281,7 +281,7 @@
         gsc[ch, 576:584, :] = diagonals(c_b, ch, 8)
         gf = row_rolls(gsc[ch, 72:584, :], 3).reshape(64, 8, 128).sum(axis=1)
         osc[pl.ds(8 + ch, 128, stride=10), :] = mm(spread_g, gf.astype(BF16))
-    out[...] = osc[...].astype(BF16)
+    out[...] = osc[0:1280, :].astype(BF16)
 
 
 def backward_kernel(
@@ -289,7 +289,7 @@
     gp_o, kept, given, scr, tmp, sm, ssc,
 ):
     own = own_index()
-    scr[...] = recv[...].astype(F32)
+    scr[0:1280, :] = recv[...].astype(F32)
 
     def line(r):
         return scr[pl.ds(r, 128, stride=10), :]
@@ -384,7 +384,7 @@
     fscale = scale / 4.0
     core = own_index() % 2
     for k, recv in enumerate((own_core, other)):
-        scr[k] = recv[...].astype(F32)
+        scr[k, 0:1152, :] = recv[...].astype(F32)
         first = pl.multiple_of(64 * (core if k == 0 else 1 - core), 64)
         for rb in range(2):
             for cb in range(8):
@@ -426,8 +426,8 @@
 
 def conv_scratch():
     return [
-        pltpu.VMEM((1280, 128), F32),
-        pltpu.VMEM((1280, 128), F32),
+        pltpu.VMEM((1296, 128), F32),
+        pltpu.VMEM((1296, 128), F32),
         pltpu.VMEM((2, 592, 256), BF16),
         pltpu.VMEM((2, 9, 128, 128), BF16),
         pltpu.VMEM((2, 9, 128, 128), BF16),
@@ -478,7 +478,7 @@
          sds(5, 64, 64), hidden, hidden, hidden, hidden, sds(1, 256),
          sds(64, 256), hidden, sds(64, 256), sds(2, 64)),
         [pltpu.VMEM(x.shape, x.dtype) for x in inputs]
-        + [pltpu.VMEM((1280, 128), F32), pltpu.SemaphoreType.DMA((len(inputs),))],
+        + [pltpu.VMEM((1296, 128), F32), pltpu.SemaphoreType.DMA((len(inputs),))],
         from_hbm=True,
     )(*(pltpu.with_memory_space_constraint(x, pltpu.HBM) for x in inputs))
     recv = exchange(slab, 10)
@@ -494,10 +494,10 @@
         "backward",
         (sds(256, 768, dtype=BF16), sds(1152, 128), sds(1152, 128, dtype=BF16)),
         [
-            pltpu.VMEM((1280, 128), F32),
+            pltpu.VMEM((1296, 128), F32),
             pltpu.VMEM((128, 256), F32),
             pltpu.VMEM((128, 128), F32),
-            pltpu.VMEM((2304, 128), F32),
+            pltpu.VMEM((2336, 128), F32),
         ],
     )(recv, go, gi, v, gg, tok, og, emb, pre1, act1, pre2, act2, bias, modul, hw, fw, sf)
     gtok = call(token_kernel, "tokens", square)(gp, in_weight)
@@ -512,7 +512,7 @@
         "unpack",
         (sds(256, 768), sds(256, 256), sds(1, 256), sds(5, 64), sds(1, 64), sds(64, 64),
          sds(1, 64), sds(64, 256), sds(2, 64)),
-        [pltpu.VMEM((2, 1152, 128), F32), pltpu.VMEM((2, 128, 128), F32)],
+        [pltpu.VMEM((2, 1184, 128), F32), pltpu.VMEM((2, 128, 128), F32)],
     )(recv, swap_cores(recv))
     return (gtok[None], giw, gow, gsb[0], gew, geb[0], ghw, ghb[0], gfw, gsf)
 

time: 85.2 us -> 85.2 us (level)
  no operation moved by 1% of the time
where the time goes in v7:
time: 85.2 us; the launch traced here: 85 us
  blocking collectives  67.3 us (79%)
  Pallas kernels  11.6 us (14%)
  starting transfers between devices  3.87 us (5%)
  waiting for transfers between devices  1.46 us (2%)
    all_to_all x4, blocking collectives, exchange(): lax.all_to_all(y, AXES, split_axis=0, concat_axis=0, axis_index_groups=gr...  67.3 us
    pallas_call x7, Pallas kernels, run(): pl.pallas_call(kernel, out_shape=out_shape, in_specs=[pl.BlockSpec(memory...  11.6 us
    ppermute x2, starting transfers between devices, swap_cores(): return lax.ppermute(x, 'batch', [(k, k ^ 1) for k in range(4)])  3.87 us
  transfers between devices with their start and end apart: 2, of which 2 were waited for; matrix products, arithmetic and copies ran while one was open for 0% of the time, Pallas kernels for 1%

profile of v7, /device:TPU:1, one launch (start us, length us, event | category | flops | bytes accessed | tf_op | source)
XLA Modules:
  0.0 85.0 jit_solution(7883435695628356419)
XLA Ops:
  0.6 2.3 %forward.1 = (bf16[1280,128]{1,0:T(8,128)(2,1)S(1)}, bf16[256,256]{1,0:T(8,128)(2,1)S(1)}, bf16[256,256]{1,0:T(8,128)(2,1)S(1)}, bf16[256,256]{1,0:T(8,128)(2,1)...) custom-call(bf16[256,256]{1,0:T(8,128)(2,1)} %bitcast.26, ...), custom_call_target="tpu_custom_call" | custom-call | tf_op jit(solution)/shard_map/forward/pallas_call | solution.py:413
  3.0 22.9 %all_to_all.20 = bf16[128,5,2,128]{3,2,1,0:T(2,128)(2,1)S(1)} all-to-all(bf16[128,5,2,128]{3,2,1,0:T(2,128)(2,1)S(1)} %bitcast.30), channel_id=1, replica_groups=mesh['seq'=32,'batch'=4] {'seq','batch'}, dimensions={0} | all-to-all | bytes 655360 | tf_op jit(solution)/shard_map/all_to_all | solution.py:448
  25.9 5.8 %conv.1 = bf16[1280,128]{1,0:T(8,128)(2,1)S(1)} custom-call(bf16[1280,128]{1,0:T(8,128)(2,1)S(1)} %bitcast.18, f32[1,256]{1,0:T(1,128)S(1)} %get-tuple-element.39.skip), custom_call_target="tpu_custom_call" | custom-call | tf_op jit(solution)/shard_map/conv/pallas_call | solution.py:413
  31.7 0.0 copy-start.1
  31.7 0.0 copy-start.2
  31.7 15.9 %all_to_all.21 = bf16[128,5,2,128]{3,2,1,0:T(2,128)(2,1)S(1)} all-to-all(bf16[128,5,2,128]{3,2,1,0:T(2,128)(2,1)S(1)} %bitcast.19), channel_id=1, replica_groups=mesh['seq'=32,'batch'=4] {'seq','batch'}, dimensions={0} | all-to-all | bytes 655360 | tf_op jit(solution)/shard_map/all_to_all | solution.py:448
  47.6 0.0 copy-done.1
  47.6 0.0 copy-done.2
  47.6 1.0 %backward.1 = (bf16[256,768]{1,0:T(8,128)(2,1)S(1)}, f32[1152,128]{1,0:T(8,128)S(1)}, bf16[1152,128]{1,0:T(8,128)(2,1)S(1)}) custom-call(bf16[1280,128]{1,0:T(8,128)(2,1)S(1)} %bitcast.20, bf16[256,256]{1,0:T(8,128)(2,1)S(1)} %get-tuple-element.40.go, bf16[256,256]{1,0:T(8,128)(2,1)S(1)} %get-tuple-element.41.gi, bf16[256,256]{1,0:T(8,128)(2,1)S(1)} %get-tuple-element.42.v, ...), custom_call_target="tpu_custom_call" | custom-call | tf_op jit(solution)/shard_map/backward/pallas_call | solution.py:413
  48.6 0.7 collective-permute-start
  49.3 1.2 %collective-permute-done.taken = bf16[1152,128]{1,0:T(8,128)(2,1)S(1)} collective-permute-done((bf16[1152,128]{1,0:T(8,128)(2,1)S(1)}, bf16[1152,128]{1,0:T(8,128)(2,1)S(1)}, u32[]{:S(2)}, u32[]{:S(2)}) %collective-permute-start) | collective-permute-done | bytes 294944 | tf_op jit(solution)/shard_map/ppermute | solution.py:455
  50.5 0.1 pair.1
  50.6 13.9 %all_to_all.22 = bf16[64,9,2,128]{3,2,1,0:T(2,128)(2,1)S(1)} all-to-all(bf16[64,9,2,128]{3,2,1,0:T(2,128)(2,1)S(1)} %bitcast.25), channel_id=1, replica_groups={{0,2,4,6,8,10,12,14,16,18,20,22,24,26,28,30,32,34,36,38,40,42,44,46,48,..., dimensions={0} | all-to-all | bytes 589824 | tf_op jit(solution)/shard_map/all_to_all | solution.py:448
  64.5 0.3 total.1
  64.8 0.0 copy-start
  64.8 14.6 %all_to_all.23 = bf16[64,9,2,128]{3,2,1,0:T(2,128)(2,1)S(1)} all-to-all(bf16[64,9,2,128]{3,2,1,0:T(2,128)(2,1)S(1)} %bitcast.24), channel_id=1, replica_groups={{0,2,4,6,8,10,12,14,16,18,20,22,24,26,28,30,32,34,36,38,40,42,44,46,48,..., dimensions={0} | all-to-all | bytes 589824 | tf_op jit(solution)/shard_map/all_to_all | solution.py:448
  79.5 3.2 %collective-permute-start.1 = (bf16[1152,128]{1,0:T(8,128)(2,1)S(1)}, bf16[1152,128]{1,0:T(8,128)(2,1)S(1)}, u32[]{:S(2)}, u32[]{:S(2)}) collective-permute-start(bf16[1152,128]{1,0:T(8,128)(2,1)S(1)} %bitcast.21), channel_id=1, source_target_pairs={{0,1},{1,0},{2,3},{3,2},{4,5},{5,4},{6,7},{7,6},{8,9},{9,8},{10,11... | collective-permute-start | bytes 884744 | tf_op jit(solution)/shard_map/ppermute | solution.py:455
  82.6 0.0 copy-done
  82.6 1.0 %tokens.1 = bf16[256,256]{1,0:T(8,128)(2,1)} custom-call(bf16[256,768]{1,0:T(8,128)(2,1)S(1)} %get-tuple-element.54.gp, bf16[256,768]{1,0:T(8,128)(2,1)S(1)} %copy-done), custom_call_target="tpu_custom_call" | custom-call | tf_op jit(solution)/shard_map/tokens/pallas_call | solution.py:413
  83.6 0.2 collective-permute-done.1.other
  83.8 1.1 %unpack.1 = (f32[256,768]{1,0:T(8,128)}, f32[256,256]{1,0:T(8,128)}, f32[1,256]{1,0:T(1,128)}, f32[5,64]{1,0:T(8,128)}, f32[1,64]{1,0:T(1,128)}, /*index=5*/f32[...) custom-call(bf16[1152,128]{1,0:T(8,128)(2,1)S(1)} %bitcast.22, ...), custom_call_target="tpu_custom_call" | custom-call | tf_op jit(solution)/shard_map/unpack/pallas_call | solution.py:413
Async XLA Ops:
  31.7 15.9 %copy-start.1 = (bf16[1,256,256]{2,1,0:T(8,128)(2,1)S(1)}, bf16[1,256,256]{2,1,0:T(8,128)(2,1)}, u32[]{:S(2)}) copy-start(bf16[1,256,256]{2,1,0:T(8,128)(2,1)} %param.12) | copy-start | bytes 393220
  31.7 15.9 %copy-start.2 = (bf16[1,256,256]{2,1,0:T(8,128)(2,1)S(1)}, bf16[1,256,256]{2,1,0:T(8,128)(2,1)}, u32[]{:S(2)}) copy-start(bf16[1,256,256]{2,1,0:T(8,128)(2,1)} %param.13) | copy-start | bytes 393220
  48.6 1.9 %collective-permute-start = (bf16[1152,128]{1,0:T(8,128)(2,1)S(1)}, bf16[1152,128]{1,0:T(8,128)(2,1)S(1)}, u32[]{:S(2)}, u32[]{:S(2)}) collective-permute-start(bf16[1152,128]{1,0:T(8,128)(2,1)S(1)} %get-tuple-element.56), channel_id=1, source_target_pairs={{0,1},{1,0},{2,3},{3,2},{4,5},{5,4},{6,7},{7,6},{8,9},{9,8},{10,11... | collective-permute-start | bytes 884744 | tf_op jit(solution)/shard_map/ppermute | solution.py:455
  64.8 17.8 %copy-start = (bf16[256,768]{1,0:T(8,128)(2,1)S(1)}, bf16[256,768]{1,0:T(8,128)(2,1)}, u32[]{:S(2)}) copy-start(bf16[256,768]{1,0:T(8,128)(2,1)} %wi.1) | copy-start | bytes 1179652
  79.5 4.4 %collective-permute-start.1 = (bf16[1152,128]{1,0:T(8,128)(2,1)S(1)}, bf16[1152,128]{1,0:T(8,128)(2,1)S(1)}, u32[]{:S(2)}, u32[]{:S(2)}) collective-permute-start(bf16[1152,128]{1,0:T(8,128)(2,1)S(1)} %bitcast.21), channel_id=1, source_target_pairs={{0,1},{1,0},{2,3},{3,2},{4,5},{5,4},{6,7},{7,6},{8,9},{9,8},{10,11... | collective-permute-start | bytes 884744 | tf_op jit(solution)/shard_map/ppermute | solution.py:455

commit v8 on v7

--- a/solution.py
+++ b/solution.py
@@ -49,8 +49,8 @@
     tok, og, wi, wo, ew, eb, hw, hb, fw, sf, dr, sk, scr, sems,
 ):
     pairs = (
-        (tok_h, tok), (wi_h, wi), (og_h, og), (wo_h, wo), (sf_h, sf), (ew_h, ew), (eb_h, eb),
-        (hw_h, hw), (hb_h, hb), (fw_h, fw), (dr_h, dr), (sk_h, sk),
+        (ew_h, ew), (eb_h, eb), (sf_h, sf), (hw_h, hw), (hb_h, hb), (wi_h, wi), (tok_h, tok),
+        (og_h, og), (wo_h, wo), (fw_h, fw), (dr_h, dr), (sk_h, sk),
     )
     copies = [pltpu.make_async_copy(a, b, sems.at[k]) for k, (a, b) in enumerate(pairs)]
     for c in copies:
@@ -62,7 +62,15 @@
         angle = 2.0 * math.pi * band * scaled
         rows.append(jnp.cos(angle))
         rows.append(jnp.sin(angle))
-    for c in copies:
+    for c in copies[0:5]:
+        c.wait()
+    pre1 = eb[...]
+    for k in range(5):
+        pre1 = pre1 + rows[k] * ew[k : k + 1, :]
+        emb_o[k] = rows[k]
+    act1 = jnp.sin(sf[0:1, :] * pre1)
+    pre2 = mm_full(act1, hw[...]) + hb[...]
+    for c in copies[5:]:
         c.wait()
     proj = mm(tok[...], wi[...])
     go = proj[:, :256].astype(BF16)
@@ -82,12 +90,6 @@
     bias_o[...] = jnp.sum(gc * mixed, axis=0, keepdims=True)
     mixed_t = mixed.T
     gc_t = gc.T
-    pre1 = eb[...]
-    for k in range(5):
-        pre1 = pre1 + rows[k] * ew[k : k + 1, :]
-        emb_o[k] = rows[k]
-    act1 = jnp.sin(sf[0:1, :] * pre1)
-    pre2 = mm_full(act1, hw[...]) + hb[...]
     act2 = jnp.sin(sf[1:2, :] * pre2)
     pre1_o[...] = pre1
     act1_o[...] = act1

time: 85.2 us -> 85 us (level)
  no operation moved by 1% of the time
where the time goes in v8:
time: 85 us; the launch traced here: 84.7 us
  blocking collectives  67.3 us (79%)
  Pallas kernels  11.3 us (13%)
  starting transfers between devices  3.86 us (5%)
  waiting for transfers between devices  1.46 us (2%)
    all_to_all x4, blocking collectives, exchange(): lax.all_to_all(y, AXES, split_axis=0, concat_axis=0, axis_index_groups=gr...  67.3 us
    pallas_call x7, Pallas kernels, run(): pl.pallas_call(kernel, out_shape=out_shape, in_specs=[pl.BlockSpec(memory...  11.3 us
    ppermute x2, starting transfers between devices, swap_cores(): return lax.ppermute(x, 'batch', [(k, k ^ 1) for k in range(4)])  3.86 us
  transfers between devices with their start and end apart: 2, of which 2 were waited for; matrix products, arithmetic and copies ran while one was open for 0% of the time, Pallas kernels for 1%

profile of v8, /device:TPU:1, one launch (start us, length us, event | category | flops | bytes accessed | tf_op | source)
XLA Modules:
  0.0 84.7 jit_solution(17990828708522398554)
XLA Ops:
  0.6 2.0 %forward.1 = (bf16[1280,128]{1,0:T(8,128)(2,1)S(1)}, bf16[256,256]{1,0:T(8,128)(2,1)S(1)}, bf16[256,256]{1,0:T(8,128)(2,1)S(1)}, bf16[256,256]{1,0:T(8,128)(2,1)...) custom-call(bf16[256,256]{1,0:T(8,128)(2,1)} %bitcast.26, ...), custom_call_target="tpu_custom_call" | custom-call | tf_op jit(solution)/shard_map/forward/pallas_call | solution.py:415
  2.7 22.9 %all_to_all.20 = bf16[128,5,2,128]{3,2,1,0:T(2,128)(2,1)S(1)} all-to-all(bf16[128,5,2,128]{3,2,1,0:T(2,128)(2,1)S(1)} %bitcast.30), channel_id=1, replica_groups=mesh['seq'=32,'batch'=4] {'seq','batch'}, dimensions={0} | all-to-all | bytes 655360 | tf_op jit(solution)/shard_map/all_to_all | solution.py:450
  25.6 5.8 %conv.1 = bf16[1280,128]{1,0:T(8,128)(2,1)S(1)} custom-call(bf16[1280,128]{1,0:T(8,128)(2,1)S(1)} %bitcast.18, f32[1,256]{1,0:T(1,128)S(1)} %get-tuple-element.39.skip), custom_call_target="tpu_custom_call" | custom-call | tf_op jit(solution)/shard_map/conv/pallas_call | solution.py:415
  31.4 0.0 copy-start.1
  31.4 0.0 copy-start.2
  31.4 15.9 %all_to_all.21 = bf16[128,5,2,128]{3,2,1,0:T(2,128)(2,1)S(1)} all-to-all(bf16[128,5,2,128]{3,2,1,0:T(2,128)(2,1)S(1)} %bitcast.19), channel_id=1, replica_groups=mesh['seq'=32,'batch'=4] {'seq','batch'}, dimensions={0} | all-to-all | bytes 655360 | tf_op jit(solution)/shard_map/all_to_all | solution.py:450
  47.3 0.0 copy-done.1
  47.4 0.0 copy-done.2
  47.4 1.0 %backward.1 = (bf16[256,768]{1,0:T(8,128)(2,1)S(1)}, f32[1152,128]{1,0:T(8,128)S(1)}, bf16[1152,128]{1,0:T(8,128)(2,1)S(1)}) custom-call(bf16[1280,128]{1,0:T(8,128)(2,1)S(1)} %bitcast.20, bf16[256,256]{1,0:T(8,128)(2,1)S(1)} %get-tuple-element.40.go, bf16[256,256]{1,0:T(8,128)(2,1)S(1)} %get-tuple-element.41.gi, bf16[256,256]{1,0:T(8,128)(2,1)S(1)} %get-tuple-element.42.v, ...), custom_call_target="tpu_custom_call" | custom-call | tf_op jit(solution)/shard_map/backward/pallas_call | solution.py:415
  48.3 0.7 collective-permute-start
  49.0 1.2 %collective-permute-done.taken = bf16[1152,128]{1,0:T(8,128)(2,1)S(1)} collective-permute-done((bf16[1152,128]{1,0:T(8,128)(2,1)S(1)}, bf16[1152,128]{1,0:T(8,128)(2,1)S(1)}, u32[]{:S(2)}, u32[]{:S(2)}) %collective-permute-start) | collective-permute-done | bytes 294944 | tf_op jit(solution)/shard_map/ppermute | solution.py:457
  50.3 0.1 pair.1
  50.3 13.9 %all_to_all.22 = bf16[64,9,2,128]{3,2,1,0:T(2,128)(2,1)S(1)} all-to-all(bf16[64,9,2,128]{3,2,1,0:T(2,128)(2,1)S(1)} %bitcast.25), channel_id=1, replica_groups={{0,2,4,6,8,10,12,14,16,18,20,22,24,26,28,30,32,34,36,38,40,42,44,46,48,..., dimensions={0} | all-to-all | bytes 589824 | tf_op jit(solution)/shard_map/all_to_all | solution.py:450
  64.2 0.3 total.1
  64.6 0.0 copy-start
  64.6 14.6 %all_to_all.23 = bf16[64,9,2,128]{3,2,1,0:T(2,128)(2,1)S(1)} all-to-all(bf16[64,9,2,128]{3,2,1,0:T(2,128)(2,1)S(1)} %bitcast.24), channel_id=1, replica_groups={{0,2,4,6,8,10,12,14,16,18,20,22,24,26,28,30,32,34,36,38,40,42,44,46,48,..., dimensions={0} | all-to-all | bytes 589824 | tf_op jit(solution)/shard_map/all_to_all | solution.py:450
  79.2 3.2 %collective-permute-start.1 = (bf16[1152,128]{1,0:T(8,128)(2,1)S(1)}, bf16[1152,128]{1,0:T(8,128)(2,1)S(1)}, u32[]{:S(2)}, u32[]{:S(2)}) collective-permute-start(bf16[1152,128]{1,0:T(8,128)(2,1)S(1)} %bitcast.21), channel_id=1, source_target_pairs={{0,1},{1,0},{2,3},{3,2},{4,5},{5,4},{6,7},{7,6},{8,9},{9,8},{10,11... | collective-permute-start | bytes 884744 | tf_op jit(solution)/shard_map/ppermute | solution.py:457
  82.4 0.0 copy-done
  82.4 1.0 %tokens.1 = bf16[256,256]{1,0:T(8,128)(2,1)} custom-call(bf16[256,768]{1,0:T(8,128)(2,1)S(1)} %get-tuple-element.54.gp, bf16[256,768]{1,0:T(8,128)(2,1)S(1)} %copy-done), custom_call_target="tpu_custom_call" | custom-call | tf_op jit(solution)/shard_map/tokens/pallas_call | solution.py:415
  83.3 0.2 collective-permute-done.1.other
  83.6 1.1 %unpack.1 = (f32[256,768]{1,0:T(8,128)}, f32[256,256]{1,0:T(8,128)}, f32[1,256]{1,0:T(1,128)}, f32[5,64]{1,0:T(8,128)}, f32[1,64]{1,0:T(1,128)}, /*index=5*/f32[...) custom-call(bf16[1152,128]{1,0:T(8,128)(2,1)S(1)} %bitcast.22, ...), custom_call_target="tpu_custom_call" | custom-call | tf_op jit(solution)/shard_map/unpack/pallas_call | solution.py:415
Async XLA Ops:
  31.4 15.9 %copy-start.1 = (bf16[1,256,256]{2,1,0:T(8,128)(2,1)S(1)}, bf16[1,256,256]{2,1,0:T(8,128)(2,1)}, u32[]{:S(2)}) copy-start(bf16[1,256,256]{2,1,0:T(8,128)(2,1)} %param.12) | copy-start | bytes 393220
  31.4 15.9 %copy-start.2 = (bf16[1,256,256]{2,1,0:T(8,128)(2,1)S(1)}, bf16[1,256,256]{2,1,0:T(8,128)(2,1)}, u32[]{:S(2)}) copy-start(bf16[1,256,256]{2,1,0:T(8,128)(2,1)} %param.13) | copy-start | bytes 393220
  48.3 1.9 %collective-permute-start = (bf16[1152,128]{1,0:T(8,128)(2,1)S(1)}, bf16[1152,128]{1,0:T(8,128)(2,1)S(1)}, u32[]{:S(2)}, u32[]{:S(2)}) collective-permute-start(bf16[1152,128]{1,0:T(8,128)(2,1)S(1)} %get-tuple-element.56), channel_id=1, source_target_pairs={{0,1},{1,0},{2,3},{3,2},{4,5},{5,4},{6,7},{7,6},{8,9},{9,8},{10,11... | collective-permute-start | bytes 884744 | tf_op jit(solution)/shard_map/ppermute | solution.py:457
  64.6 17.8 %copy-start = (bf16[256,768]{1,0:T(8,128)(2,1)S(1)}, bf16[256,768]{1,0:T(8,128)(2,1)}, u32[]{:S(2)}) copy-start(bf16[256,768]{1,0:T(8,128)(2,1)} %wi.1) | copy-start | bytes 1179652
  79.2 4.4 %collective-permute-start.1 = (bf16[1152,128]{1,0:T(8,128)(2,1)S(1)}, bf16[1152,128]{1,0:T(8,128)(2,1)S(1)}, u32[]{:S(2)}, u32[]{:S(2)}) collective-permute-start(bf16[1152,128]{1,0:T(8,128)(2,1)S(1)} %bitcast.21), channel_id=1, source_target_pairs={{0,1},{1,0},{2,3},{3,2},{4,5},{5,4},{6,7},{7,6},{8,9},{9,8},{10,11... | collective-permute-start | bytes 884744 | tf_op jit(solution)/shard_map/ppermute | solution.py:457
